TPU v7x, 32 devices: a whole 2x2x4 slice. The times are simulated.
32 devices in a mesh: dp: 4 (over z), cp: 8 (over y, x, core).
Axes of the slice: x: 2, y: 2, z: 4, core: 2. Of those that a mesh axis runs over, the one named last changes fastest.
Arguments:
- row_owner: int32 [4096, 1], P(('dp', 'cp')), may hold values from 0 to 31; in each aligned block of 128 rows (0 to 127, 128 to 255, ...) at most 10 rows name the same one
- slot_row: int32 [4096], P(('dp', 'cp')), may hold values from 0 to 2559
- hot_table: bfloat16 [16384, 512], P(('dp', 'cp')), may hold values from -6 to 6
- cold_table: bfloat16 [65536, 128], P(('dp', 'cp')), may hold values from -6 to 6
- cold_projection: bfloat16 [128, 512], replicated, may hold values from -0.5 to 0.5
- joined_weight: bfloat16 [512, 2048], replicated, may hold values from -0.25 to 0.25
- output_weight: bfloat16 [512, 512], replicated, may hold values from -0.25 to 0.25
- cotangent: bfloat16 [4096, 512], P(('dp', 'cp')), may hold values from -6 to 6
Outputs:
- layer_out: bfloat16 [4096, 512], P(('dp', 'cp'))
- hot_gradient: float32 [16384, 512], P(('dp', 'cp'))
- cold_gradient: float32 [65536, 128], P(('dp', 'cp'))
- projection_gradient: float32 [128, 512], replicated
- joined_gradient: float32 [512, 2048], replicated
- output_gradient: float32 [512, 512], replicated
Inputs may be any that keep to these rules, and one draw needn't show every extreme that they name: `row_owner`: in each aligned block of 128 rows (the rows of one device) no owner is named by more than 10 rows.
All inputs are finite; a program needn't handle non-finite values.
Results may differ from a plain program's by a relative error of at most 0.013.
Values may be sent and summed in bfloat16 or wider, within the bound.
No kernel may reach another device: no remote copies, remote signals or barrier semaphores. Data moves between devices by JAX's collectives and lax.ppermute only.
A program may use at most 128 MiB of HBM per device.

v0:
```python
import functools
import math

import jax
import jax.numpy as jnp
from jax import lax
from jax.experimental import pallas as pl
from jax.experimental.pallas import tpu as pltpu
from jax.sharding import PartitionSpec as P


HEADS = 8
LANES = 128


EPSILON = 1e-05
low = jnp.bfloat16
f32 = jnp.float32
SMEM = pl.BlockSpec(memory_space=pltpu.SMEM)
VMEM = pl.BlockSpec(memory_space=pltpu.VMEM)


def sigmoid(values):
    return 0.5 + 0.5 * jnp.tanh(0.5 * values)


def silu(values):
    return values * sigmoid(values)


def silu_slope(values):
    sigmoid_v = sigmoid(values)
    return sigmoid_v * (1.0 + values * (1.0 - sigmoid_v))


def layer_normalize(values):
    average = jnp.mean(values, axis=-1, keepdims=True)
    centred = values - average
    inverse = lax.rsqrt(jnp.mean(centred * centred, axis=-1, keepdims=True) + EPSILON)
    return (centred * inverse, inverse)


def normalize_back(gradient, normed, inverse):
    first_term = jnp.mean(gradient, axis=-1, keepdims=True)
    second_term = jnp.mean(gradient * normed, axis=-1, keepdims=True)
    return (gradient - first_term - normed * second_term) * inverse


def dot(left, right, contract=(1, 0)):
    dims = (((contract[0],), (contract[1],)), ((), ()))
    return lax.dot_general(left, right, dims, preferred_element_type=f32)


def power_of_two(count):
    return count & (count - 1) == 0


def source_of(here, step, count):
    if power_of_two(count):
        return here ^ step
    return (here + count - step) % count


def target_of(here, step, count):
    if power_of_two(count):
        return here ^ step
    return (here + step) % count


def exchange(block, axis, step):
    count = lax.axis_size(axis)
    pairs = [(i, target_of(i, step, count)) for i in range(count)]
    return lax.ppermute(block, axis, pairs)


def arrival_order(count):
    if not power_of_two(count) or count < 4:
        return list(range(count))
    return list(range(0, count, 2)) + list(range(1, count, 2))


def gather_pieces(block, axis, after=None):
    count = lax.axis_size(axis)
    if not power_of_two(count) or count < 4:
        return [block] + [exchange(block, axis, step) for step in range(1, count)]
    near = [block]
    for step in range(2, count, 2):
        near.append(exchange(block, axis, step))
    if after is not None:
        near = list(lax.optimization_barrier((*near, *after))[: len(near)])
    return near + [exchange(piece, axis, 1) for piece in near]


def call(kernel, operands, outs, scratch=(), flops=0, scalars=1, limit=24):
    moved = sum(x.size * x.dtype.itemsize for x in list(operands) + list(outs))
    return pl.pallas_call(
        kernel,
        out_shape=outs,
        in_specs=[SMEM] * scalars + [VMEM] * (len(operands) - scalars),
        out_specs=[VMEM] * len(outs),
        scratch_shapes=list(scratch),
        cost_estimate=pl.CostEstimate(flops=flops, bytes_accessed=moved, transcendentals=0),
        compiler_params=pltpu.CompilerParams(vmem_limit_bytes=limit << 20),
    )(*operands)


def shaped(shape, dtype):
    return jax.ShapeDtypeStruct(shape, dtype)


def tile(index, size=LANES):
    return pl.ds(pl.multiple_of(index * size, size), size)


def head_masks(rows, head_size):
    lane = lax.broadcasted_iota(jnp.int32, (rows, LANES), 1)
    return [lane // head_size == n for n in range(LANES // head_size)]


def only(mask, values):
    return jnp.where(mask, values, jnp.zeros((), values.dtype))


def merge(masks, parts):
    result = parts[-1]
    for mask, part in zip(masks[:-1], parts[:-1]):
        result = jnp.where(mask, part, result)
    return result


def fill_mask(mask_ref, here, order, group, tokens, forward):
    row = lax.broadcasted_iota(jnp.int32, (tokens, tokens), 0)
    column = lax.broadcasted_iota(jnp.int32, (tokens, tokens), 1)
    for n, step in enumerate(order):
        gap = (here - source_of(here, step, group)) * tokens
        allowed = (column - row <= gap) if forward else (column - row >= gap)
        mask_ref[:, n * tokens : (n + 1) * tokens] = allowed.astype(f32)


def hidden_kernel(here_ref, normed_ref, weight_ref, hidden_ref, active_ref):
    hidden = dot(normed_ref[...], weight_ref[...])
    hidden_ref[...] = hidden
    active_ref[...] = silu(hidden).astype(low)


def forward_kernel(group, scale, head_size, *refs):
    here_ref, pieces = refs[0], refs[1 : 1 + group]
    weight_ref, active_ref, hidden_ref, embedded_ref, mix_ref, cotangent_ref = refs[1 + group : 7 + group]
    out_ref, delta_ref, gate_ref, early_ref, all_ref, normed_scr, mask_scr, att_scr = refs[7 + group :]
    tokens, width = embedded_ref.shape
    order = arrival_order(group)
    here = here_ref[0]
    for n in range(1, group):
        normed_scr[n] = pieces[n][...]
    fill_mask(mask_scr, here, order, group, tokens, True)
    all_ref[0:tokens, :width] = active_ref[:, width : 2 * width]
    all_ref[0:tokens, width:] = active_ref[:, 3 * width :]

    def project(n, carry):
        hidden = dot(normed_scr[n], weight_ref[:, width : 2 * width])
        all_ref[tile(n, tokens), :width] = silu(hidden).astype(low)
        hidden = dot(normed_scr[n], weight_ref[:, 3 * width :])
        all_ref[tile(n, tokens), width:] = silu(hidden).astype(low)
        return carry

    lax.fori_loop(1, group, project, 0)
    masks = head_masks(tokens, head_size)

    def attend(n, carry):
        values = all_ref[:, tile(n)]
        queries = active_ref[:, tile(n + 2 * width // LANES)]
        keys = all_ref[:, tile(n + width // LANES)]
        parts = []
        for mask in masks:
            scores = dot(only(mask, queries), keys, (1, 1)) * scale
            weights = (silu(scores) * mask_scr[...]).astype(low)
            parts.append(dot(weights, values))
        att_scr[:, tile(n)] = merge(masks, parts)
        return carry

    lax.fori_loop(0, width // LANES, attend, 0)
    mixed, inverse_mix = layer_normalize(att_scr[...])
    gate = active_ref[:, :width].astype(f32)
    gated = (mixed * gate).astype(low)
    out_ref[...] = (embedded_ref[...] + dot(gated, mix_ref[...])).astype(low)
    delta_gated = dot(cotangent_ref[...], mix_ref[...], (1, 1))
    delta_ref[...] = normalize_back(delta_gated * gate, mixed, inverse_mix).astype(low)
    gate_hidden = (delta_gated * mixed * silu_slope(hidden_ref[:, :width])).astype(low)
    gate_ref[...] = gate_hidden
    share = width // group
    gated_t = gated.astype(f32).T.astype(low)
    hidden_t = gate_hidden.astype(f32).T.astype(low)
    for n in range(group):
        early_ref[n, 0:share] = gated_t[n * share : (n + 1) * share]
        early_ref[n, share : 2 * share] = hidden_t[n * share : (n + 1) * share]


def query_kernel(group, scale, head_size, *refs):
    here_ref, pieces = refs[0], refs[1 : 1 + group]
    weight_ref, active_ref, all_ref, delta_ref, hidden_ref = refs[1 + group : 6 + group]
    out_ref, queries_ref, normed_scr, mask_scr = refs[6 + group :]
    tokens, width = delta_ref.shape
    for n in range(1, group):
        normed_scr[n] = pieces[n][...]
    queries_ref[0:tokens, :] = active_ref[:, 2 * width : 3 * width]

    def project(n, carry):
        hidden = dot(normed_scr[n], weight_ref[:, 2 * width : 3 * width])
        queries_ref[tile(n, tokens), :] = silu(hidden).astype(low)
        return carry

    lax.fori_loop(1, group, project, 0)
    fill_mask(mask_scr, here_ref[0], arrival_order(group), group, tokens, True)
    masks = head_masks(tokens, head_size)

    def step(n, carry):
        values = all_ref[:, tile(n)]
        queries = active_ref[:, tile(n + 2 * width // LANES)]
        keys = all_ref[:, tile(n + width // LANES)]
        delta = delta_ref[:, tile(n)]
        parts = []
        for mask in masks:
            scores = dot(only(mask, queries), keys, (1, 1)) * scale
            change = dot(only(mask, delta), values, (1, 1))
            change = (change * silu_slope(scores) * (mask_scr[...] * scale)).astype(low)
            parts.append(dot(change, keys))
        slope = silu_slope(hidden_ref[:, tile(n + 2 * width // LANES)])
        out_ref[:, tile(n)] = (merge(masks, parts) * slope).astype(low)
        return carry

    lax.fori_loop(0, width // LANES, step, 0)


def key_kernel(group, scale, head_size, *refs):
    here_ref, pieces = refs[0], refs[1 : 1 + group]
    active_ref, queries_ref, hidden_ref, query_ref, early_ref = refs[1 + group : 6 + group]
    rest_ref, columns_ref, delta_scr, mask_scr = refs[6 + group :]
    tokens, width = query_ref.shape
    for n in range(group):
        delta_scr[n * tokens : (n + 1) * tokens, :] = pieces[n][...]
    fill_mask(mask_scr, here_ref[0], arrival_order(group), group, tokens, False)
    masks = head_masks(tokens, head_size)
    tiles = width // LANES

    def step(n, carry):
        values = active_ref[:, tile(n + tiles)]
        queries = queries_ref[:, tile(n)]
        keys = active_ref[:, tile(n + 3 * tiles)]
        delta = delta_scr[:, tile(n)]
        value_parts, key_parts = [], []
        for mask in masks:
            scores = dot(only(mask, keys), queries, (1, 1)) * scale
            change = dot(only(mask, values), delta, (1, 1))
            sigmoid_v = sigmoid(scores)
            weights = (scores * sigmoid_v * mask_scr[...]).astype(low)
            slope = sigmoid_v * (1.0 + scores * (1.0 - sigmoid_v))
            change = (change * slope * (mask_scr[...] * scale)).astype(low)
            value_parts.append(dot(weights, delta))
            key_parts.append(dot(change, queries))
        for parts, at in ((value_parts, 0), (key_parts, 2)):
            slope = silu_slope(hidden_ref[:, tile(n + (at + 1) * tiles)])
            rest_ref[:, tile(n + at * tiles)] = (merge(masks, parts) * slope).astype(low)
        return carry

    lax.fori_loop(0, tiles, step, 0)
    rest_ref[:, width : 2 * width] = query_ref[...]
    late = rest_ref[...].astype(f32).T.astype(low)
    share = width // group
    for n in range(group):
        columns_ref[n, : 2 * share] = early_ref[n]
        columns_ref[n, 2 * share :] = late[3 * n * share : 3 * (n + 1) * share]


def row_kernel(head_rows, capacity, *refs):
    _, gate_ref, rest_ref, weight_ref, embedded_ref, cotangent_ref = refs[:6]
    vector_ref, slot_ref, place_ref, cold_ref, sent_ref = refs[6:]
    tokens, width = embedded_ref.shape
    cold_width = cold_ref.shape[0]
    devices, padded, _ = sent_ref.shape
    delta_normed = dot(gate_ref[...], weight_ref[:, :width], (1, 1))
    delta_normed += dot(rest_ref[...], weight_ref[:, width:], (1, 1))
    normed, inverse = layer_normalize(embedded_ref[...])
    delta_embed = normalize_back(delta_normed, normed, inverse) + cotangent_ref[...].astype(f32)
    delta_low = delta_embed.astype(low)
    cold = slot_ref[...] >= head_rows
    cold_event = dot(delta_low, cold_ref[...], (1, 1))
    hot_event = jnp.where(cold, 0.0, delta_embed)
    narrow = jnp.where(cold, cold_event, hot_event[:, :cold_width])
    event = jnp.concatenate([narrow, hot_event[:, cold_width:]], axis=1).astype(low)
    place = lax.broadcasted_iota(jnp.int32, (tokens, devices * padded), 1)
    chosen = (place == place_ref[...]).astype(f32).astype(low)
    sent_ref[...] = dot(chosen, event, (0, 0)).astype(low).reshape(sent_ref.shape)
    cold_rows = jnp.where(cold, vector_ref[:, :cold_width].astype(f32), 0.0).astype(low)
    part = dot(cold_rows, delta_low, (0, 0)).astype(low)
    each = cold_width // devices
    for n in range(devices):
        sent_ref[n, capacity : capacity + each] = part[n * each : (n + 1) * each]


def weight_kernel(group, count, *refs):
    here_ref, moved_ref = refs[:2]
    cotangents, normeds = refs[2 : 2 + group], refs[2 + group : 2 + 2 * group]
    own_ref = refs[2 + 2 * group]
    sends = refs[3 + 2 * group : 2 + 2 * group + count]
    part_scr = refs[2 + 2 * group + count]
    here, outer = here_ref[0], here_ref[1]
    share = moved_ref.shape[1] // 5
    chunk = own_ref.shape[0]
    top = bottom = None
    for n, step in enumerate(arrival_order(group)):
        source = source_of(here, step, group)
        first = dot(moved_ref[source, :share], cotangents[n][...])
        second = dot(moved_ref[source, share:], normeds[n][...])
        top = first if n == 0 else top + first
        bottom = second if n == 0 else bottom + second
    total = jnp.concatenate([top, bottom], axis=0)
    for n in range(count):
        part_scr[n] = total[n * chunk : (n + 1) * chunk]
    own_ref[...] = part_scr[outer]
    for step in range(1, count):
        sends[step - 1][...] = part_scr[target_of(outer, step, count)].astype(low)


def final_kernel(group, count, norm_scale, *refs):
    here_ref, pieces = refs[0], refs[1 : 1 + group]
    joined_ref, output_ref, piece_scr = refs[1 + group :]
    here, outer = here_ref[0], here_ref[1]
    width = output_ref.shape[0]
    chunk = piece_scr.shape[2]
    for n, step in enumerate(arrival_order(group)):
        source = source_of(here, step, group)
        for m in range(count):
            part = pieces[n][m * chunk : (m + 1) * chunk]
            piece_scr[source, source_of(outer, m, count)] = part
    share = width // group
    row = lax.broadcasted_iota(jnp.int32, (width, width), 0)
    column = lax.broadcasted_iota(jnp.int32, (width, width), 1)
    unit = (row == column).astype(f32).astype(low)
    blocks = [piece_scr[n].reshape(5 * share, width) for n in range(group)]
    for n in range(group):
        output_ref[n * share : (n + 1) * share, :] = blocks[n][:share].astype(f32) * norm_scale
    gate = jnp.concatenate([block[share : 2 * share] for block in blocks], axis=0)
    joined_ref[:, :width] = dot(unit, gate, (1, 1)) * norm_scale
    rest = jnp.concatenate([block[2 * share :] for block in blocks], axis=0)
    for n in range(3):
        columns = dot(unit, rest[n * width : (n + 1) * width], (1, 1)) * norm_scale
        joined_ref[:, (n + 1) * width : (n + 2) * width] = columns


def scatter_kernel(capacity, each, *refs):
    _, asked_ref, arrived_ref, hot_ref, cold_ref, mine_ref = refs
    devices, padded, width = arrived_ref.shape
    slots = devices * padded
    hot_count, cold_width = hot_ref.shape[0], cold_ref.shape[1]
    rows = arrived_ref[...].reshape(slots, width)
    asked = asked_ref[...]
    index = lax.broadcasted_iota(jnp.int32, (hot_count, slots), 0)
    for n in range(cold_ref.shape[0] // hot_count):
        chosen = (index + (n + 1) * hot_count == asked).astype(f32).astype(low)
        cold_ref[n * hot_count : (n + 1) * hot_count, :] = dot(chosen, rows[:, :cold_width])
    hot_ref[...] = dot((index == asked).astype(f32).astype(low), rows)
    total = arrived_ref[0].astype(f32)
    for n in range(1, devices):
        total = total + arrived_ref[n].astype(f32)
    mine_ref[...] = total[capacity : capacity + each].astype(low)


def assemble(position, pieces, norm_scale, width):
    group, count = lax.axis_size("cp"), lax.axis_size("dp")
    share = width // group
    size = 5 * share // count
    if size % 16 == 0:
        return call(
            functools.partial(final_kernel, group, count, norm_scale),
            [position] + pieces,
            [shaped((width, 4 * width), f32), shaped((width, width), f32)],
            [pltpu.VMEM((group, count, size, width), low)],
        )
    result = jnp.zeros((group, count, size, width), low)
    for step, piece in zip(arrival_order(group), pieces):
        piece = piece.reshape(count, size, width)
        source = source_of(position[0], step, group)
        for n in range(count):
            place = (source, source_of(position[1], n, count), 0, 0)
            result = lax.dynamic_update_slice(result, piece[n][None, None], place)
    whole = result.reshape(group, count * size, width).astype(f32) * norm_scale
    output = whole[:, :share].reshape(width, width)
    gate = whole[:, share : 2 * share].reshape(width, width)
    rest = whole[:, 2 * share :].reshape(3 * width, width)
    return jnp.concatenate([gate, rest], axis=0).T, output


def local(
    row_owner,
    slot_row,
    hot_table,
    cold_table,
    cold_projection,
    joined_weight,
    output_weight,
    cotangent,
):
    tokens = slot_row.shape[0]
    width = output_weight.shape[0]
    hot_count = hot_table.shape[0]
    cold_count, cold_width = cold_table.shape
    head_size = width // HEADS
    score_scale = 1.0 / math.sqrt(head_size)
    everyone = ("dp", "cp")
    devices = lax.axis_size(everyone)
    group = lax.axis_size("cp")
    length = group * tokens
    position = jnp.stack([lax.axis_index("cp"), lax.axis_index("dp")]).astype(jnp.int32)
    capacity = 2 * tokens // devices + 2
    padded = -(-(capacity + cold_width // devices) // 8) * 8
    slots = devices * padded
    owners = row_owner[:, 0]
    is_hot = slot_row < hot_count
    named = owners[:, None] == jnp.arange(devices, dtype=jnp.int32)[None, :]
    onehot = named.astype(low)
    lower = (jnp.arange(tokens)[:, None] > jnp.arange(tokens)[None, :]).astype(low)
    earlier = jnp.dot(lower, onehot, preferred_element_type=f32)
    rank = jnp.sum(jnp.where(named, earlier, 0.0), axis=1).astype(jnp.int32)
    place = owners * padded + rank
    chosen = place[:, None] == jnp.arange(slots, dtype=jnp.int32)[None, :]
    requests = jnp.max(jnp.where(chosen, slot_row[:, None], -1), axis=0)
    asked = lax.all_to_all(
        requests.reshape(devices, padded), everyone, split_axis=0, concat_axis=0, tiled=True
    ).reshape(-1)
    hot_select = asked[:, None] == jnp.arange(hot_count, dtype=jnp.int32)[None, :]
    cold_select = asked[:, None] == jnp.arange(hot_count, hot_count + cold_count, dtype=jnp.int32)
    hot_pick = jnp.dot(hot_select.astype(low), hot_table, preferred_element_type=low)
    cold_pick = jnp.dot(cold_select.astype(low), cold_table, preferred_element_type=low)
    picked = hot_pick + jnp.pad(cold_pick, ((0, 0), (0, width - cold_width)))
    rows_back = lax.all_to_all(
        picked.reshape(devices, padded, width), everyone, split_axis=0, concat_axis=0, tiled=True
    ).reshape(slots, width)
    held_cotangent, _ = lax.optimization_barrier((cotangent, asked))
    cotangents = gather_pieces(held_cotangent, "cp")
    vector = jnp.dot(chosen.astype(low), rows_back, preferred_element_type=low)
    cold_embed = jnp.dot(vector[:, :cold_width], cold_projection, preferred_element_type=f32)
    embedded = jnp.where(is_hot[:, None], vector.astype(f32), cold_embed)
    normed_low = layer_normalize(embedded)[0].astype(low)
    hidden, active = call(
        hidden_kernel,
        [position, normed_low, joined_weight],
        [shaped((tokens, 4 * width), f32), shaped((tokens, 4 * width), low)],
        flops=8 * tokens * width * width,
    )
    normeds = gather_pieces(normed_low, "cp")
    share = width // group
    work = 2 * tokens * length * width
    mask = pltpu.VMEM((tokens, length), f32)
    layer_out, delta_attended, gate_hidden, early, everything = call(
        functools.partial(forward_kernel, group, score_scale, head_size),
        [position, *normeds, joined_weight, active, hidden, embedded, output_weight, cotangent],
        [
            shaped((tokens, width), low),
            shaped((tokens, width), low),
            shaped((tokens, width), low),
            shaped((group, 2 * share, tokens), low),
            shaped((length, 2 * width), low),
        ],
        [pltpu.VMEM((group, tokens, width), low), mask, pltpu.VMEM((tokens, width), f32)],
        2 * work + 4 * length * width * width,
    )
    query_hidden, all_queries = call(
        functools.partial(query_kernel, group, score_scale, head_size),
        [position, *normeds, joined_weight, active, everything, delta_attended, hidden],
        [shaped((tokens, width), low), shaped((length, width), low)],
        [pltpu.VMEM((group, tokens, width), low), mask],
        3 * work,
    )
    deltas = gather_pieces(delta_attended, "cp")
    rest_hidden, columns = call(
        functools.partial(key_kernel, group, score_scale, head_size),
        [position, *deltas, active, all_queries, hidden, query_hidden, early],
        [shaped((tokens, 3 * width), low), shaped((group, 5 * share, tokens), low)],
        [pltpu.VMEM((length, width), low), mask],
        4 * work,
    )
    moved = lax.all_to_all(columns, "cp", split_axis=0, concat_axis=0, tiled=True)
    sent = call(
        functools.partial(row_kernel, hot_count, capacity),
        [
            position,
            gate_hidden,
            rest_hidden,
            joined_weight,
            embedded,
            cotangent,
            vector,
            slot_row[:, None],
            place[:, None],
            cold_projection,
        ],
        [shaped((devices, padded, width), low)],
        flops=8 * tokens * width * width,
    )[0]
    arrived = lax.all_to_all(sent, everyone, split_axis=0, concat_axis=0, tiled=True)
    count = lax.axis_size("dp")
    chunk = 5 * share // count
    own, *sends = call(
        functools.partial(weight_kernel, group, count),
        [position, moved, *cotangents, *normeds],
        [shaped((chunk, width), f32)] + [shaped((chunk, width), low)] * (count - 1),
        [pltpu.VMEM((count, chunk, width), f32)],
        10 * share * length * width,
    )
    for step, block in enumerate(sends, start=1):
        own = own + exchange(block, "dp", step).astype(f32)
    mine = own.astype(low)
    line = [mine] + [exchange(mine, "dp", step) for step in range(1, count)]
    line = jnp.concatenate(line, axis=0)
    each = cold_width // devices
    hot_gradient, cold_gradient, total = call(
        functools.partial(scatter_kernel, capacity, each),
        [position, asked[None, :], arrived],
        [
            shaped((hot_count, width), f32),
            shaped((cold_count, cold_width), f32),
            shaped((each, width), low),
        ],
        flops=4 * slots * hot_count * width,
    )
    copies = jnp.broadcast_to(total[None], (devices, each, width))
    projection = lax.all_to_all(copies, everyone, split_axis=0, concat_axis=0, tiled=True)
    pieces = gather_pieces(line, "cp", (projection, hot_gradient, cold_gradient))
    norm_scale = (tokens * devices) ** (-0.5)
    joined_gradient, output_gradient = assemble(position, pieces, norm_scale, width)
    return (
        layer_out,
        hot_gradient,
        cold_gradient,
        projection.reshape(cold_width, width).astype(f32) * norm_scale,
        joined_gradient,
        output_gradient,
    )


def solution(mesh):
    placed = (
        P(("dp", "cp"), None),
        P(("dp", "cp")),
        P(("dp", "cp"), None),
        P(("dp", "cp"), None),
        P(),
        P(),
        P(),
        P(("dp", "cp"), None),
    )
    return jax.shard_map(
        local,
        mesh=mesh,
        in_specs=placed,
        out_specs=(
            P(("dp", "cp"), None),
            P(("dp", "cp"), None),
            P(("dp", "cp"), None),
            P(),
            P(),
            P(),
        ),
        check_vma=False,
    )
```

profile of v0, /device:TPU:0, one launch (start us, length us, event | category | flops | bytes accessed | tf_op | source)
XLA Modules:
  0.0 174.5 jit_solution(684149148150325446)
XLA Ops:
  0.7 0.8 broadcast_multiply_fusion.1
  1.5 0.9 fusion.4
  3.3 0.8 select_reduce_fusion
  4.7 7.3 %all-to-all-start = ((s32[32,1,16]{2,1,0:T(1,128)}), s32[32,1,16]{2,1,0:T(1,128)S(1)}, u32[]{:S(2)}, u32[]{:S(2)}) async-start(s32[32,1,16]{2,1,0:T(1,128)} %bitcast.4), calls=%async_computation | async-start | bytes 32768 | tf_op jit(solution)/shard_map/all_to_all | solution.py:427
  12.1 7.1 %all-to-all-done = s32[32,1,16]{2,1,0:T(1,128)S(1)} async-done(((s32[32,1,16]{2,1,0:T(1,128)}), s32[32,1,16]{2,1,0:T(1,128)S(1)}, u32[]{:S(2)}, u32[]{:S(2)}) %all-to-all-start) | async-done | bytes 2080 | tf_op jit(solution)/shard_map/all_to_all | solution.py:427
  20.5 1.8 %fusion = bf16[512,128]{1,0:T(8,128)(2,1)S(1)} fusion(bf16[2048,128]{1,0:T(8,128)(2,1)} %param.11, s32[2048]{0:T(1024)S(1)} %iota_add_fusion, s32[512]{0:T(512)S(1)} %eq.66), kind=kOutput, calls=%fused_computation | convolution fusion | flops 269484032 | bytes 665600 | tf_op jit(solution)/shard_map/dot_general | solution.py:433
  22.3 1.3 convolution_add_fusion
  23.6 2.6 %all-to-all-start.1 = ((bf16[32,16,512]{2,1,0:T(8,128)(2,1)}), bf16[32,16,512]{2,1,0:T(8,128)(2,1)S(1)}, u32[]{:S(2)}, u32[]{:S(2)}) async-start(bf16[32,16,512]{2,1,0:T(8,128)(2,1)} %bitcast.15), calls=%async_computation.1 | async-start | bytes 1048576 | tf_op jit(solution)/shard_map/all_to_all | solution.py:435
  26.2 15.6 %all-to-all-done.1 = bf16[32,16,512]{2,1,0:T(8,128)(2,1)S(1)} async-done(((bf16[32,16,512]{2,1,0:T(8,128)(2,1)}), bf16[32,16,512]{2,1,0:T(8,128)(2,1)S(1)}, u32[]{:S(2)}, u32[]{:S(2)}) %all-to-all-start.1) | async-done | bytes 524320 | tf_op jit(solution)/shard_map/all_to_all | solution.py:435
  42.9 0.9 collective-permute-start
  43.8 1.5 collective-permute-start.1
  45.3 1.2 collective-permute-start.2
  46.4 2.3 %collective-permute-done.refs_2_.refs_11_ = bf16[128,512]{1,0:T(8,128)(2,1)S(1)} collective-permute-done((bf16[128,512]{1,0:T(8,128)(2,1)S(1)}, bf16[128,512]{1,0:T(8,128)(2,1)S(1)}, u32[]{:S(2)}, u32[]{:S(2)}) %collective-permute-start) | collective-permute-done | bytes 131104 | tf_op jit(solution)/shard_map/ppermute | solution.py:73
  48.8 3.3 %collective-permute-done.1.refs_3_.refs_12_ = bf16[128,512]{1,0:T(8,128)(2,1)S(1)} collective-permute-done((bf16[128,512]{1,0:T(8,128)(2,1)S(1)}, bf16[128,512]{1,0:T(8,128)(2,1)S(1)}, u32[]{:S(2)}, u32[]{:S(2)}) %collective-permute-start.1) | collective-permute-done | bytes 131104 | tf_op jit(solution)/shard_map/ppermute | solution.py:73
  52.7 1.0 shard_map.127
  53.8 1.2 copy-done.14
  55.0 7.3 %shard_map.128 = (bf16[128,512]{1,0:T(8,128)(2,1)}, bf16[128,512]{1,0:T(8,128)(2,1)S(1)}, bf16[128,512]{1,0:T(8,128)(2,1)S(1)}, bf16[8,128,128]{2,1,0:T(8,128)(2,1)S(1)}, bf16[1024,1024]{1,0:T(8,128)(2,1)S(1)}) custom-call(s32[2]{0:T(128)S(1)} %pad_add_fusion.here_ref.refs_0_, bf16[128,512]{1,0:T(8,128)(2,1)S(1)} %multiply_convert_fusion.normed_ref.refs_1_.refs_10_, ...), custom_call_target="tpu_custom_call" | custom-call | flops 1342177280 | bytes 8388616 | tf_op jit(solution)/shard_map/pallas_call | solution.py:96
  62.9 0.7 collective-permute-start.7
  63.6 0.7 collective-permute-start.8
  64.3 2.1 %collective-permute-start.9 = (bf16[128,512]{1,0:T(8,128)(2,1)S(1)}, bf16[128,512]{1,0:T(8,128)(2,1)S(1)}, u32[]{:S(2)}, u32[]{:S(2)}) collective-permute-start(bf16[128,512]{1,0:T(8,128)(2,1)S(1)} %get-tuple-element.34.refs_12_.refs_1_), channel_id=1, source_target_pairs={{0,6},{1,7},{2,4},{3,5},{4,2},{5,3},{6,0},{7,1},{8,14},{9,15},{10,... | collective-permute-start | bytes 393224 | tf_op jit(solution)/shard_map/ppermute | solution.py:73
  66.4 2.9 %collective-permute-done.7.refs_2_ = bf16[128,512]{1,0:T(8,128)(2,1)S(1)} collective-permute-done((bf16[128,512]{1,0:T(8,128)(2,1)S(1)}, bf16[128,512]{1,0:T(8,128)(2,1)S(1)}, u32[]{:S(2)}, u32[]{:S(2)}) %collective-permute-start.7) | collective-permute-done | bytes 131104 | tf_op jit(solution)/shard_map/ppermute | solution.py:73
  69.8 1.8 %collective-permute-done.9.refs_4_ = bf16[128,512]{1,0:T(8,128)(2,1)S(1)} collective-permute-done((bf16[128,512]{1,0:T(8,128)(2,1)S(1)}, bf16[128,512]{1,0:T(8,128)(2,1)S(1)}, u32[]{:S(2)}, u32[]{:S(2)}) %collective-permute-start.9) | collective-permute-done | bytes 131104 | tf_op jit(solution)/shard_map/ppermute | solution.py:73
  71.6 6.3 %shard_map.129 = (bf16[128,512]{1,0:T(8,128)(2,1)S(1)}, bf16[1024,512]{1,0:T(8,128)(2,1)S(1)}) custom-call(s32[2]{0:T(128)S(1)} %pad_add_fusion.here_ref.refs_0_, bf16[128,512]{1,0:T(8,128)(2,1)S(1)} %multiply_convert_fusion.normed_ref.refs_1_.refs_10_, bf16[128,512]{1,0:T(8,128)(2,1)S(1)} %collective-permute-done.refs_2_.refs_11_, ...), custom_call_target="tpu_custom_call" | custom-call | flops 402653184 | bytes 8126472 | tf_op jit(solution)/shard_map/pallas_call | solution.py:96
  78.0 5.3 %shard_map.130 = (bf16[128,1536]{1,0:T(8,128)(2,1)S(1)}, bf16[8,320,128]{2,1,0:T(8,128)(2,1)S(1)}) custom-call(s32[2]{0:T(128)S(1)} %pad_add_fusion.here_ref.refs_0_, bf16[128,512]{1,0:T(8,128)(2,1)S(1)} %get-tuple-element.34.refs_12_.refs_1_, bf16[128,512]{1,0:T(8,128)(2,1)S(1)} %collective-permute-done.7.refs_2_, ...), custom_call_target="tpu_custom_call" | custom-call | flops 536870912 | bytes 5111816 | tf_op jit(solution)/shard_map/pallas_call | solution.py:96
  83.3 0.8 copy-done.13
  84.1 0.7 copy-done.17
  84.9 4.2 %all-to-all-start.4 = ((bf16[8,320,128]{2,1,0:T(8,128)(2,1)}), bf16[8,320,128]{2,1,0:T(8,128)(2,1)}, u32[]{:S(2)}, u32[]{:S(2)}) async-start(bf16[8,320,128]{2,1,0:T(8,128)(2,1)} %copy-done.13), calls=%async_computation.4 | async-start | bytes 1310720 | tf_op jit(solution)/shard_map/all_to_all | solution.py:482
  89.1 0.7 copy.35.refs_7_
  89.8 0.9 copy-done.12
  90.7 0.9 copy-done.16
  91.6 1.0 copy-done.18
  92.6 0.8 copy-done.21
  93.5 0.8 copy-done.22
  94.3 0.9 copy-done.24
  95.2 2.7 %shard_map.131 = bf16[32,16,512]{2,1,0:T(8,128)(2,1)} custom-call(s32[2]{0:T(128)S(1)} %pad_add_fusion.here_ref.refs_0_, bf16[128,512]{1,0:T(8,128)(2,1)S(1)} %copy-done.24, bf16[128,1536]{1,0:T(8,128)(2,1)S(1)} %copy-done.18, bf16[512,2048]{1,0:T(8,128)(2,1)S(1)} %copy-done.1, f32[128,512]{1,0:T(8,128)S(1)} %get-tuple-element.57.refs_12_.refs_4_, ...), custom_call_target="tpu_custom_call" | custom-call | flops 268435456 | bytes 3802120 | tf_op jit(solution)/shard_map/pallas_call | solution.py:96
  98.0 2.3 %all-to-all-done.4.refs_1_ = bf16[8,320,128]{2,1,0:T(8,128)(2,1)} async-done(((bf16[8,320,128]{2,1,0:T(8,128)(2,1)}), bf16[8,320,128]{2,1,0:T(8,128)(2,1)}, u32[]{:S(2)}, u32[]{:S(2)}) %all-to-all-start.4) | async-done | bytes 655392 | tf_op jit(solution)/shard_map/all_to_all | solution.py:482
  100.2 3.5 %all-to-all-start.2 = ((bf16[32,16,512]{2,1,0:T(8,128)(2,1)}), bf16[32,16,512]{2,1,0:T(8,128)(2,1)}, u32[]{:S(2)}, u32[]{:S(2)}) async-start(bf16[32,16,512]{2,1,0:T(8,128)(2,1)} %shard_map.131), calls=%async_computation.2 | async-start | bytes 1048576 | tf_op jit(solution)/shard_map/all_to_all | solution.py:500
  103.8 1.5 collective-permute-start.14
  105.2 1.5 collective-permute-start.15
  107.3 6.4 %collective-permute-done.14.refs_3_ = bf16[128,512]{1,0:T(8,128)(2,1)S(1)} collective-permute-done((bf16[128,512]{1,0:T(8,128)(2,1)S(1)}, bf16[128,512]{1,0:T(8,128)(2,1)S(1)}, u32[]{:S(2)}, u32[]{:S(2)}) %collective-permute-start.14) | collective-permute-done | bytes 131104 | tf_op jit(solution)/shard_map/ppermute | solution.py:73
  114.3 3.6 %collective-permute-done.16.refs_5_ = bf16[128,512]{1,0:T(8,128)(2,1)S(1)} collective-permute-done((bf16[128,512]{1,0:T(8,128)(2,1)S(1)}, bf16[128,512]{1,0:T(8,128)(2,1)S(1)}, u32[]{:S(2)}, u32[]{:S(2)}) %collective-permute-start.16) | collective-permute-done | bytes 131104 | tf_op jit(solution)/shard_map/ppermute | solution.py:73
  117.9 1.3 collective-permute-done.20.refs_9_
  119.3 0.9 copy-done.4
  120.2 0.9 copy-done.6
  121.1 0.9 copy-done.8
  122.0 0.9 copy-done.10
  122.9 2.0 %shard_map.133 = (f32[80,512]{1,0:T(8,128)S(1)}, bf16[80,512]{1,0:T(8,128)(2,1)S(1)}, bf16[80,512]{1,0:T(8,128)(2,1)S(1)}, bf16[80,512]{1,0:T(8,128)(2,1)S(1)}) custom-call(s32[2]{0:T(128)S(1)} %pad_add_fusion.here_ref.refs_0_, bf16[8,320,128]{2,1,0:T(8,128)(2,1)} %all-to-all-done.4.refs_1_, bf16[128,512]{1,0:T(8,128)(2,1)S(1)} %copy-done.2, ...), custom_call_target="tpu_custom_call" | custom-call | flops 335544320 | bytes 3162120 | tf_op jit(solution)/shard_map/pallas_call | solution.py:96
  124.8 1.7 collective-permute-start.21
  126.5 2.8 %collective-permute-start.22 = (bf16[80,512]{1,0:T(8,128)(2,1)S(1)}, bf16[80,512]{1,0:T(8,128)(2,1)S(1)}, u32[]{:S(2)}, u32[]{:S(2)}) collective-permute-start(bf16[80,512]{1,0:T(8,128)(2,1)S(1)} %get-tuple-element.46), channel_id=1, source_target_pairs={{0,16},{8,24},{16,0},{24,8},{1,17},{9,25},{17,1},{25,9},{2,18},{10... | collective-permute-start | bytes 245768 | tf_op jit(solution)/shard_map/ppermute | solution.py:73
  129.5 6.4 %collective-permute-done.22 = bf16[80,512]{1,0:T(8,128)(2,1)S(1)} collective-permute-done((bf16[80,512]{1,0:T(8,128)(2,1)S(1)}, bf16[80,512]{1,0:T(8,128)(2,1)S(1)}, u32[]{:S(2)}, u32[]{:S(2)}) %collective-permute-start.22) | collective-permute-done | bytes 81952 | tf_op jit(solution)/shard_map/ppermute | solution.py:73
  135.9 1.9 %collective-permute-start.24 = (bf16[80,512]{1,0:T(8,128)(2,1)S(1)}, bf16[80,512]{1,0:T(8,128)(2,1)S(1)}, u32[]{:S(2)}, u32[]{:S(2)}) collective-permute-start(bf16[80,512]{1,0:T(8,128)(2,1)S(1)} %add_convert_fusion), channel_id=1, source_target_pairs={{0,8},{8,0},{16,24},{24,16},{1,9},{9,1},{17,25},{25,17},{2,10},{10... | collective-permute-start | bytes 245768 | tf_op jit(solution)/shard_map/ppermute | solution.py:73
  137.8 1.8 %collective-permute-start.25 = (bf16[80,512]{1,0:T(8,128)(2,1)S(1)}, bf16[80,512]{1,0:T(8,128)(2,1)S(1)}, u32[]{:S(2)}, u32[]{:S(2)}) collective-permute-start(bf16[80,512]{1,0:T(8,128)(2,1)S(1)} %add_convert_fusion), channel_id=1, source_target_pairs={{0,16},{8,24},{16,0},{24,8},{1,17},{9,25},{17,1},{25,9},{2,18},{10... | collective-permute-start | bytes 245768 | tf_op jit(solution)/shard_map/ppermute | solution.py:73
  139.6 0.9 collective-permute-start.26
  140.6 6.0 %collective-permute-done.25 = bf16[80,512]{1,0:T(8,128)(2,1)S(1)} collective-permute-done((bf16[80,512]{1,0:T(8,128)(2,1)S(1)}, bf16[80,512]{1,0:T(8,128)(2,1)S(1)}, u32[]{:S(2)}, u32[]{:S(2)}) %collective-permute-start.25) | collective-permute-done | bytes 81952 | tf_op jit(solution)/shard_map/ppermute | solution.py:73
  146.7 0.8 collective-permute-start.27
  147.8 2.4 %collective-permute-start.29 = (bf16[320,512]{1,0:T(8,128)(2,1)S(1)}, bf16[320,512]{1,0:T(8,128)(2,1)S(1)}, u32[]{:S(2)}, u32[]{:S(2)}) collective-permute-start(bf16[320,512]{1,0:T(8,128)(2,1)S(1)} %pad_maximum_fusion.refs_1_), channel_id=1, source_target_pairs={{0,6},{1,7},{2,4},{3,5},{4,2},{5,3},{6,0},{7,1},{8,14},{9,15},{10,... | collective-permute-start | bytes 983048 | tf_op jit(solution)/shard_map/ppermute | solution.py:73
  150.3 3.1 %shard_map.132 = (f32[512,512]{1,0:T(8,128)}, f32[2048,128]{1,0:T(8,128)}, bf16[4,512]{1,0:T(4,128)(2,1)S(1)}) custom-call(s32[2]{0:T(128)S(1)} %pad_add_fusion.here_ref.refs_0_, s32[1,512]{1,0:T(1,128)S(1)} %broadcast_in_dim_reshape.2.refs_1_, bf16[32,16,512]{2,1,0:T(8,128)(2,1)} %all-to-all-done.2.refs_2_), custom_call_target="tpu_custom_call" | custom-call | flops 536870912 | bytes 2627592 | tf_op jit(solution)/shard_map/pallas_call | solution.py:96
  154.1 3.1 %all-to-all-start.3 = ((bf16[32,4,512]{2,1,0:T(4,128)(2,1)}), bf16[32,4,512]{2,1,0:T(4,128)(2,1)S(1)}, u32[]{:S(2)}, u32[]{:S(2)}) async-start(bf16[32,4,512]{2,1,0:T(4,128)(2,1)} %broadcast_in_dim.50), calls=%async_computation.3 | async-start | bytes 262144 | tf_op jit(solution)/shard_map/all_to_all | solution.py:527
  157.3 4.6 %collective-permute-done.28.refs_3_ = bf16[320,512]{1,0:T(8,128)(2,1)S(1)} collective-permute-done((bf16[320,512]{1,0:T(8,128)(2,1)S(1)}, bf16[320,512]{1,0:T(8,128)(2,1)S(1)}, u32[]{:S(2)}, u32[]{:S(2)}) %collective-permute-start.28) | collective-permute-done | bytes 327712 | tf_op jit(solution)/shard_map/ppermute | solution.py:73
  161.9 3.5 %all-to-all-done.3 = bf16[32,4,512]{2,1,0:T(4,128)(2,1)S(1)} async-done(((bf16[32,4,512]{2,1,0:T(4,128)(2,1)}), bf16[32,4,512]{2,1,0:T(4,128)(2,1)S(1)}, u32[]{:S(2)}, u32[]{:S(2)}) %all-to-all-start.3) | async-done | bytes 131104 | tf_op jit(solution)/shard_map/all_to_all | solution.py:527
  166.4 0.8 mul.34
  168.4 0.7 copy-done.19
  169.1 1.0 copy-done.20
  170.1 4.4 %shard_map.134 = (f32[512,2048]{1,0:T(8,128)}, f32[512,512]{1,0:T(8,128)}) custom-call(s32[2]{0:T(128)S(1)} %pad_add_fusion.here_ref.refs_0_, bf16[320,512]{1,0:T(8,128)(2,1)S(1)} %pad_maximum_fusion.refs_1_, bf16[320,512]{1,0:T(8,128)(2,1)S(1)} %collective-permute-done.27.refs_2_, bf16[320,512]{1,0:T(8,128)(2,1)S(1)} %collective-permute-done.28.refs_3_, ...), custom_call_target="tpu_custom_call" | custom-call | bytes 7864328 | tf_op jit(solution)/shard_map/pallas_call | solution.py:96
  (107 shorter events, 10.7 us)
Async XLA Ops:
  0.6 21.7 %copy-start = (bf16[512,512]{1,0:T(8,128)(2,1)S(1)}, bf16[512,512]{1,0:T(8,128)(2,1)}, u32[]{:S(2)}) copy-start(bf16[512,512]{1,0:T(8,128)(2,1)} %param.10) | copy-start | bytes 1572868
  0.6 25.6 %copy-start.27 = (s32[128]{0:T(128)S(1)}, s32[128]{0:T(128)}, u32[]{:S(2)}) copy-start(s32[128]{0:T(128)} %param.9) | copy-start | bytes 1540
  0.7 41.4 %copy-start.15 = (bf16[128,512]{1,0:T(8,128)(2,1)S(1)}, bf16[128,512]{1,0:T(8,128)(2,1)}, u32[]{:S(2)}) copy-start(bf16[128,512]{1,0:T(8,128)(2,1)} %refs_9_.5) | copy-start | bytes 393220
  0.7 52.0 %copy-start.1 = (bf16[512,2048]{1,0:T(8,128)(2,1)S(1)}, bf16[512,2048]{1,0:T(8,128)(2,1)}, u32[]{:S(2)}) copy-start(bf16[512,2048]{1,0:T(8,128)(2,1)} %refs_3_.1) | copy-start | bytes 6291460
  4.7 14.4 %all-to-all-start = ((s32[32,1,16]{2,1,0:T(1,128)}), s32[32,1,16]{2,1,0:T(1,128)S(1)}, u32[]{:S(2)}, u32[]{:S(2)}) async-start(s32[32,1,16]{2,1,0:T(1,128)} %bitcast.4), calls=%async_computation | async-start | bytes 32768 | tf_op jit(solution)/shard_map/all_to_all | solution.py:427
  19.1 1.2 copy-start.25
  20.5 33.4 %copy-start.2 = (bf16[128,512]{1,0:T(8,128)(2,1)S(1)}, bf16[128,512]{1,0:T(8,128)(2,1)}, u32[]{:S(2)}) copy-start(bf16[128,512]{1,0:T(8,128)(2,1)} %refs_2_) | copy-start | bytes 393220
  23.6 18.2 %all-to-all-start.1 = ((bf16[32,16,512]{2,1,0:T(8,128)(2,1)}), bf16[32,16,512]{2,1,0:T(8,128)(2,1)S(1)}, u32[]{:S(2)}, u32[]{:S(2)}) async-start(bf16[32,16,512]{2,1,0:T(8,128)(2,1)} %bitcast.15), calls=%async_computation.1 | async-start | bytes 1048576 | tf_op jit(solution)/shard_map/all_to_all | solution.py:435
  42.9 5.9 %collective-permute-start = (bf16[128,512]{1,0:T(8,128)(2,1)S(1)}, bf16[128,512]{1,0:T(8,128)(2,1)S(1)}, u32[]{:S(2)}, u32[]{:S(2)}) collective-permute-start(bf16[128,512]{1,0:T(8,128)(2,1)S(1)} %multiply_convert_fusion.normed_ref.refs_1_.refs_10_), channel_id=1, source_target_pairs={{0,2},{1,3},{2,0},{3,1},{4,6},{5,7},{6,4},{7,5},{8,10},{9,11},{10,... | collective-permute-start | bytes 393224 | tf_op jit(solution)/shard_map/ppermute | solution.py:73
  43.8 8.3 %collective-permute-start.1 = (bf16[128,512]{1,0:T(8,128)(2,1)S(1)}, bf16[128,512]{1,0:T(8,128)(2,1)S(1)}, u32[]{:S(2)}, u32[]{:S(2)}) collective-permute-start(bf16[128,512]{1,0:T(8,128)(2,1)S(1)} %multiply_convert_fusion.normed_ref.refs_1_.refs_10_), channel_id=1, source_target_pairs={{0,4},{1,5},{2,6},{3,7},{4,0},{5,1},{6,2},{7,3},{8,12},{9,13},{10,... | collective-permute-start | bytes 393224 | tf_op jit(solution)/shard_map/ppermute | solution.py:73
  45.3 6.8 %collective-permute-start.2 = (bf16[128,512]{1,0:T(8,128)(2,1)S(1)}, bf16[128,512]{1,0:T(8,128)(2,1)S(1)}, u32[]{:S(2)}, u32[]{:S(2)}) collective-permute-start(bf16[128,512]{1,0:T(8,128)(2,1)S(1)} %multiply_convert_fusion.normed_ref.refs_1_.refs_10_), channel_id=1, source_target_pairs={{0,6},{1,7},{2,4},{3,5},{4,2},{5,3},{6,0},{7,1},{8,14},{9,15},{10,... | collective-permute-start | bytes 393224 | tf_op jit(solution)/shard_map/ppermute | solution.py:73
  46.4 7.3 %collective-permute-start.3 = (bf16[128,512]{1,0:T(8,128)(2,1)S(1)}, bf16[128,512]{1,0:T(8,128)(2,1)S(1)}, u32[]{:S(2)}, u32[]{:S(2)}) collective-permute-start(bf16[128,512]{1,0:T(8,128)(2,1)S(1)} %multiply_convert_fusion.normed_ref.refs_1_.refs_10_), channel_id=1, source_target_pairs={{0,1},{1,0},{2,3},{3,2},{4,5},{5,4},{6,7},{7,6},{8,9},{9,8},{10,11... | collective-permute-start | bytes 393224 | tf_op jit(solution)/shard_map/ppermute | solution.py:73
  48.8 5.0 %collective-permute-start.4 = (bf16[128,512]{1,0:T(8,128)(2,1)S(1)}, bf16[128,512]{1,0:T(8,128)(2,1)S(1)}, u32[]{:S(2)}, u32[]{:S(2)}) collective-permute-start(bf16[128,512]{1,0:T(8,128)(2,1)S(1)} %collective-permute-done.refs_2_.refs_11_), channel_id=1, source_target_pairs={{0,1},{1,0},{2,3},{3,2},{4,5},{5,4},{6,7},{7,6},{8,9},{9,8},{10,11... | collective-permute-start | bytes 393224 | tf_op jit(solution)/shard_map/ppermute | solution.py:73
  52.1 1.7 collective-permute-start.5
  52.1 1.7 collective-permute-start.6
  53.7 24.1 %copy-start.3 = (bf16[128,512]{1,0:T(8,128)(2,1)}, bf16[128,512]{1,0:T(8,128)(2,1)S(1)}, u32[]{:S(2)}) copy-start(bf16[128,512]{1,0:T(8,128)(2,1)S(1)} %collective-permute-done.3.refs_5_.refs_14_) | copy-start | bytes 393220
  53.8 24.1 %copy-start.5 = (bf16[128,512]{1,0:T(8,128)(2,1)}, bf16[128,512]{1,0:T(8,128)(2,1)S(1)}, u32[]{:S(2)}) copy-start(bf16[128,512]{1,0:T(8,128)(2,1)S(1)} %collective-permute-done.4.refs_6_.refs_15_) | copy-start | bytes 393220
  53.8 24.1 %copy-start.7 = (bf16[128,512]{1,0:T(8,128)(2,1)}, bf16[128,512]{1,0:T(8,128)(2,1)S(1)}, u32[]{:S(2)}) copy-start(bf16[128,512]{1,0:T(8,128)(2,1)S(1)} %collective-permute-done.5.refs_7_.refs_16_) | copy-start | bytes 393220
  53.8 24.1 %copy-start.9 = (bf16[128,512]{1,0:T(8,128)(2,1)}, bf16[128,512]{1,0:T(8,128)(2,1)S(1)}, u32[]{:S(2)}) copy-start(bf16[128,512]{1,0:T(8,128)(2,1)S(1)} %collective-permute-done.6.refs_8_.refs_17_) | copy-start | bytes 393220
  53.8 1.2 copy-start.14
  62.9 6.4 %collective-permute-start.7 = (bf16[128,512]{1,0:T(8,128)(2,1)S(1)}, bf16[128,512]{1,0:T(8,128)(2,1)S(1)}, u32[]{:S(2)}, u32[]{:S(2)}) collective-permute-start(bf16[128,512]{1,0:T(8,128)(2,1)S(1)} %get-tuple-element.34.refs_12_.refs_1_), channel_id=1, source_target_pairs={{0,2},{1,3},{2,0},{3,1},{4,6},{5,7},{6,4},{7,5},{8,10},{9,11},{10,... | collective-permute-start | bytes 393224 | tf_op jit(solution)/shard_map/ppermute | solution.py:73
  63.6 6.1 %collective-permute-start.8 = (bf16[128,512]{1,0:T(8,128)(2,1)S(1)}, bf16[128,512]{1,0:T(8,128)(2,1)S(1)}, u32[]{:S(2)}, u32[]{:S(2)}) collective-permute-start(bf16[128,512]{1,0:T(8,128)(2,1)S(1)} %get-tuple-element.34.refs_12_.refs_1_), channel_id=1, source_target_pairs={{0,4},{1,5},{2,6},{3,7},{4,0},{5,1},{6,2},{7,3},{8,12},{9,13},{10,... | collective-permute-start | bytes 393224 | tf_op jit(solution)/shard_map/ppermute | solution.py:73
  64.3 7.3 %collective-permute-start.9 = (bf16[128,512]{1,0:T(8,128)(2,1)S(1)}, bf16[128,512]{1,0:T(8,128)(2,1)S(1)}, u32[]{:S(2)}, u32[]{:S(2)}) collective-permute-start(bf16[128,512]{1,0:T(8,128)(2,1)S(1)} %get-tuple-element.34.refs_12_.refs_1_), channel_id=1, source_target_pairs={{0,6},{1,7},{2,4},{3,5},{4,2},{5,3},{6,0},{7,1},{8,14},{9,15},{10,... | collective-permute-start | bytes 393224 | tf_op jit(solution)/shard_map/ppermute | solution.py:73
  66.4 11.5 %collective-permute-start.10 = (bf16[128,512]{1,0:T(8,128)(2,1)S(1)}, bf16[128,512]{1,0:T(8,128)(2,1)S(1)}, u32[]{:S(2)}, u32[]{:S(2)}) collective-permute-start(bf16[128,512]{1,0:T(8,128)(2,1)S(1)} %get-tuple-element.34.refs_12_.refs_1_), channel_id=1, source_target_pairs={{0,1},{1,0},{2,3},{3,2},{4,5},{5,4},{6,7},{7,6},{8,9},{9,8},{10,11... | collective-permute-start | bytes 393224 | tf_op jit(solution)/shard_map/ppermute | solution.py:73
  69.3 8.7 %collective-permute-start.11 = (bf16[128,512]{1,0:T(8,128)(2,1)S(1)}, bf16[128,512]{1,0:T(8,128)(2,1)S(1)}, u32[]{:S(2)}, u32[]{:S(2)}) collective-permute-start(bf16[128,512]{1,0:T(8,128)(2,1)S(1)} %collective-permute-done.7.refs_2_), channel_id=1, source_target_pairs={{0,1},{1,0},{2,3},{3,2},{4,5},{5,4},{6,7},{7,6},{8,9},{9,8},{10,11... | collective-permute-start | bytes 393224 | tf_op jit(solution)/shard_map/ppermute | solution.py:73
  69.7 8.2 %collective-permute-start.12 = (bf16[128,512]{1,0:T(8,128)(2,1)S(1)}, bf16[128,512]{1,0:T(8,128)(2,1)S(1)}, u32[]{:S(2)}, u32[]{:S(2)}) collective-permute-start(bf16[128,512]{1,0:T(8,128)(2,1)S(1)} %collective-permute-done.8.refs_3_), channel_id=1, source_target_pairs={{0,1},{1,0},{2,3},{3,2},{4,5},{5,4},{6,7},{7,6},{8,9},{9,8},{10,11... | collective-permute-start | bytes 393224 | tf_op jit(solution)/shard_map/ppermute | solution.py:73
  71.6 6.4 %collective-permute-start.13 = (bf16[128,512]{1,0:T(8,128)(2,1)S(1)}, bf16[128,512]{1,0:T(8,128)(2,1)S(1)}, u32[]{:S(2)}, u32[]{:S(2)}) collective-permute-start(bf16[128,512]{1,0:T(8,128)(2,1)S(1)} %collective-permute-done.9.refs_4_), channel_id=1, source_target_pairs={{0,1},{1,0},{2,3},{3,2},{4,5},{5,4},{6,7},{7,6},{8,9},{9,8},{10,11... | collective-permute-start | bytes 393224 | tf_op jit(solution)/shard_map/ppermute | solution.py:73
  83.3 0.8 copy-start.13
  84.1 0.7 copy-start.17
  84.9 15.4 %all-to-all-start.4 = ((bf16[8,320,128]{2,1,0:T(8,128)(2,1)}), bf16[8,320,128]{2,1,0:T(8,128)(2,1)}, u32[]{:S(2)}, u32[]{:S(2)}) async-start(bf16[8,320,128]{2,1,0:T(8,128)(2,1)} %copy-done.13), calls=%async_computation.4 | async-start | bytes 1310720 | tf_op jit(solution)/shard_map/all_to_all | solution.py:482
  89.8 0.9 copy-start.12
  90.7 0.9 copy-start.16
  91.6 1.0 copy-start.18
  92.6 0.8 copy-start.21
  93.5 0.8 copy-start.22
  94.3 0.9 copy-start.24
  98.0 52.3 %copy-start.26 = (s32[32,1,16]{2,1,0:T(1,128)S(1)}, s32[32,1,16]{2,1,0:T(1,128)}, u32[]{:S(2)}) copy-start(s32[32,1,16]{2,1,0:T(1,128)} %copy-done.25) | copy-start | bytes 6148
  100.2 50.1 %all-to-all-start.2 = ((bf16[32,16,512]{2,1,0:T(8,128)(2,1)}), bf16[32,16,512]{2,1,0:T(8,128)(2,1)}, u32[]{:S(2)}, u32[]{:S(2)}) async-start(bf16[32,16,512]{2,1,0:T(8,128)(2,1)} %shard_map.131), calls=%async_computation.2 | async-start | bytes 1048576 | tf_op jit(solution)/shard_map/all_to_all | solution.py:500
  103.8 10.0 %collective-permute-start.14 = (bf16[128,512]{1,0:T(8,128)(2,1)S(1)}, bf16[128,512]{1,0:T(8,128)(2,1)S(1)}, u32[]{:S(2)}, u32[]{:S(2)}) collective-permute-start(bf16[128,512]{1,0:T(8,128)(2,1)S(1)} %copy-done.2), channel_id=1, source_target_pairs={{0,2},{1,3},{2,0},{3,1},{4,6},{5,7},{6,4},{7,5},{8,10},{9,11},{10,... | collective-permute-start | bytes 393224 | tf_op jit(solution)/shard_map/ppermute | solution.py:73
  105.2 8.5 %collective-permute-start.15 = (bf16[128,512]{1,0:T(8,128)(2,1)S(1)}, bf16[128,512]{1,0:T(8,128)(2,1)S(1)}, u32[]{:S(2)}, u32[]{:S(2)}) collective-permute-start(bf16[128,512]{1,0:T(8,128)(2,1)S(1)} %copy-done.2), channel_id=1, source_target_pairs={{0,4},{1,5},{2,6},{3,7},{4,0},{5,1},{6,2},{7,3},{8,12},{9,13},{10,... | collective-permute-start | bytes 393224 | tf_op jit(solution)/shard_map/ppermute | solution.py:73
  106.7 11.2 %collective-permute-start.16 = (bf16[128,512]{1,0:T(8,128)(2,1)S(1)}, bf16[128,512]{1,0:T(8,128)(2,1)S(1)}, u32[]{:S(2)}, u32[]{:S(2)}) collective-permute-start(bf16[128,512]{1,0:T(8,128)(2,1)S(1)} %copy-done.2), channel_id=1, source_target_pairs={{0,6},{1,7},{2,4},{3,5},{4,2},{5,3},{6,0},{7,1},{8,14},{9,15},{10,... | collective-permute-start | bytes 393224 | tf_op jit(solution)/shard_map/ppermute | solution.py:73
  107.3 10.6 %collective-permute-start.17 = (bf16[128,512]{1,0:T(8,128)(2,1)S(1)}, bf16[128,512]{1,0:T(8,128)(2,1)S(1)}, u32[]{:S(2)}, u32[]{:S(2)}) collective-permute-start(bf16[128,512]{1,0:T(8,128)(2,1)S(1)} %copy-done.2), channel_id=1, source_target_pairs={{0,1},{1,0},{2,3},{3,2},{4,5},{5,4},{6,7},{7,6},{8,9},{9,8},{10,11... | collective-permute-start | bytes 393224 | tf_op jit(solution)/shard_map/ppermute | solution.py:73
  113.7 4.2 %collective-permute-start.18 = (bf16[128,512]{1,0:T(8,128)(2,1)S(1)}, bf16[128,512]{1,0:T(8,128)(2,1)S(1)}, u32[]{:S(2)}, u32[]{:S(2)}) collective-permute-start(bf16[128,512]{1,0:T(8,128)(2,1)S(1)} %collective-permute-done.14.refs_3_), channel_id=1, source_target_pairs={{0,1},{1,0},{2,3},{3,2},{4,5},{5,4},{6,7},{7,6},{8,9},{9,8},{10,11... | collective-permute-start | bytes 393224 | tf_op jit(solution)/shard_map/ppermute | solution.py:73
  113.7 4.2 %collective-permute-start.19 = (bf16[128,512]{1,0:T(8,128)(2,1)S(1)}, bf16[128,512]{1,0:T(8,128)(2,1)S(1)}, u32[]{:S(2)}, u32[]{:S(2)}) collective-permute-start(bf16[128,512]{1,0:T(8,128)(2,1)S(1)} %collective-permute-done.15.refs_4_), channel_id=1, source_target_pairs={{0,1},{1,0},{2,3},{3,2},{4,5},{5,4},{6,7},{7,6},{8,9},{9,8},{10,11... | collective-permute-start | bytes 393224 | tf_op jit(solution)/shard_map/ppermute | solution.py:73
  117.9 1.3 collective-permute-start.20
  119.3 0.9 copy-start.4
  120.2 0.9 copy-start.6
  121.1 0.9 copy-start.8
  122.0 0.9 copy-start.10
  124.8 4.6 %collective-permute-start.21 = (bf16[80,512]{1,0:T(8,128)(2,1)S(1)}, bf16[80,512]{1,0:T(8,128)(2,1)S(1)}, u32[]{:S(2)}, u32[]{:S(2)}) collective-permute-start(bf16[80,512]{1,0:T(8,128)(2,1)S(1)} %get-tuple-element.45), channel_id=1, source_target_pairs={{0,8},{8,0},{16,24},{24,16},{1,9},{9,1},{17,25},{25,17},{2,10},{10... | collective-permute-start | bytes 245768 | tf_op jit(solution)/shard_map/ppermute | solution.py:73
  126.5 9.3 %collective-permute-start.22 = (bf16[80,512]{1,0:T(8,128)(2,1)S(1)}, bf16[80,512]{1,0:T(8,128)(2,1)S(1)}, u32[]{:S(2)}, u32[]{:S(2)}) collective-permute-start(bf16[80,512]{1,0:T(8,128)(2,1)S(1)} %get-tuple-element.46), channel_id=1, source_target_pairs={{0,16},{8,24},{16,0},{24,8},{1,17},{9,25},{17,1},{25,9},{2,18},{10... | collective-permute-start | bytes 245768 | tf_op jit(solution)/shard_map/ppermute | solution.py:73
  129.3 6.6 %collective-permute-start.23 = (bf16[80,512]{1,0:T(8,128)(2,1)S(1)}, bf16[80,512]{1,0:T(8,128)(2,1)S(1)}, u32[]{:S(2)}, u32[]{:S(2)}) collective-permute-start(bf16[80,512]{1,0:T(8,128)(2,1)S(1)} %get-tuple-element.47), channel_id=1, source_target_pairs={{0,24},{8,16},{16,8},{24,0},{1,25},{9,17},{17,9},{25,1},{2,26},{10... | collective-permute-start | bytes 245768 | tf_op jit(solution)/shard_map/ppermute | solution.py:73
  135.9 4.7 %collective-permute-start.24 = (bf16[80,512]{1,0:T(8,128)(2,1)S(1)}, bf16[80,512]{1,0:T(8,128)(2,1)S(1)}, u32[]{:S(2)}, u32[]{:S(2)}) collective-permute-start(bf16[80,512]{1,0:T(8,128)(2,1)S(1)} %add_convert_fusion), channel_id=1, source_target_pairs={{0,8},{8,0},{16,24},{24,16},{1,9},{9,1},{17,25},{25,17},{2,10},{10... | collective-permute-start | bytes 245768 | tf_op jit(solution)/shard_map/ppermute | solution.py:73
  137.8 8.8 %collective-permute-start.25 = (bf16[80,512]{1,0:T(8,128)(2,1)S(1)}, bf16[80,512]{1,0:T(8,128)(2,1)S(1)}, u32[]{:S(2)}, u32[]{:S(2)}) collective-permute-start(bf16[80,512]{1,0:T(8,128)(2,1)S(1)} %add_convert_fusion), channel_id=1, source_target_pairs={{0,16},{8,24},{16,0},{24,8},{1,17},{9,25},{17,1},{25,9},{2,18},{10... | collective-permute-start | bytes 245768 | tf_op jit(solution)/shard_map/ppermute | solution.py:73
  139.6 7.1 %collective-permute-start.26 = (bf16[80,512]{1,0:T(8,128)(2,1)S(1)}, bf16[80,512]{1,0:T(8,128)(2,1)S(1)}, u32[]{:S(2)}, u32[]{:S(2)}) collective-permute-start(bf16[80,512]{1,0:T(8,128)(2,1)S(1)} %add_convert_fusion), channel_id=1, source_target_pairs={{0,24},{8,16},{16,8},{24,0},{1,25},{9,17},{17,9},{25,1},{2,26},{10... | collective-permute-start | bytes 245768 | tf_op jit(solution)/shard_map/ppermute | solution.py:73
  146.7 10.6 %collective-permute-start.27 = (bf16[320,512]{1,0:T(8,128)(2,1)S(1)}, bf16[320,512]{1,0:T(8,128)(2,1)S(1)}, u32[]{:S(2)}, u32[]{:S(2)}) collective-permute-start(bf16[320,512]{1,0:T(8,128)(2,1)S(1)} %pad_maximum_fusion.refs_1_), channel_id=1, source_target_pairs={{0,2},{1,3},{2,0},{3,1},{4,6},{5,7},{6,4},{7,5},{8,10},{9,11},{10,... | collective-permute-start | bytes 983048 | tf_op jit(solution)/shard_map/ppermute | solution.py:73
  147.5 14.4 %collective-permute-start.28 = (bf16[320,512]{1,0:T(8,128)(2,1)S(1)}, bf16[320,512]{1,0:T(8,128)(2,1)S(1)}, u32[]{:S(2)}, u32[]{:S(2)}) collective-permute-start(bf16[320,512]{1,0:T(8,128)(2,1)S(1)} %pad_maximum_fusion.refs_1_), channel_id=1, source_target_pairs={{0,4},{1,5},{2,6},{3,7},{4,0},{5,1},{6,2},{7,3},{8,12},{9,13},{10,... | collective-permute-start | bytes 983048 | tf_op jit(solution)/shard_map/ppermute | solution.py:73
  147.8 14.1 %collective-permute-start.29 = (bf16[320,512]{1,0:T(8,128)(2,1)S(1)}, bf16[320,512]{1,0:T(8,128)(2,1)S(1)}, u32[]{:S(2)}, u32[]{:S(2)}) collective-permute-start(bf16[320,512]{1,0:T(8,128)(2,1)S(1)} %pad_maximum_fusion.refs_1_), channel_id=1, source_target_pairs={{0,6},{1,7},{2,4},{3,5},{4,2},{5,3},{6,0},{7,1},{8,14},{9,15},{10,... | collective-permute-start | bytes 983048 | tf_op jit(solution)/shard_map/ppermute | solution.py:73
  154.1 11.3 %all-to-all-start.3 = ((bf16[32,4,512]{2,1,0:T(4,128)(2,1)}), bf16[32,4,512]{2,1,0:T(4,128)(2,1)S(1)}, u32[]{:S(2)}, u32[]{:S(2)}) async-start(bf16[32,4,512]{2,1,0:T(4,128)(2,1)} %broadcast_in_dim.50), calls=%async_computation.3 | async-start | bytes 262144 | tf_op jit(solution)/shard_map/all_to_all | solution.py:527
  165.4 1.9 %collective-permute-start.30 = (bf16[320,512]{1,0:T(8,128)(2,1)S(1)}, bf16[320,512]{1,0:T(8,128)(2,1)S(1)}, u32[]{:S(2)}, u32[]{:S(2)}) collective-permute-start(bf16[320,512]{1,0:T(8,128)(2,1)S(1)} %pad_maximum_fusion.refs_1_), channel_id=1, source_target_pairs={{0,1},{1,0},{2,3},{3,2},{4,5},{5,4},{6,7},{7,6},{8,9},{9,8},{10,11... | collective-permute-start | bytes 983048 | tf_op jit(solution)/shard_map/ppermute | solution.py:73
  165.6 1.9 %collective-permute-start.31 = (bf16[320,512]{1,0:T(8,128)(2,1)S(1)}, bf16[320,512]{1,0:T(8,128)(2,1)S(1)}, u32[]{:S(2)}, u32[]{:S(2)}) collective-permute-start(bf16[320,512]{1,0:T(8,128)(2,1)S(1)} %collective-permute-done.27.refs_2_), channel_id=1, source_target_pairs={{0,1},{1,0},{2,3},{3,2},{4,5},{5,4},{6,7},{7,6},{8,9},{9,8},{10,11... | collective-permute-start | bytes 983048 | tf_op jit(solution)/shard_map/ppermute | solution.py:73
  165.9 2.1 %collective-permute-start.32 = (bf16[320,512]{1,0:T(8,128)(2,1)S(1)}, bf16[320,512]{1,0:T(8,128)(2,1)S(1)}, u32[]{:S(2)}, u32[]{:S(2)}) collective-permute-start(bf16[320,512]{1,0:T(8,128)(2,1)S(1)} %collective-permute-done.28.refs_3_), channel_id=1, source_target_pairs={{0,1},{1,0},{2,3},{3,2},{4,5},{5,4},{6,7},{7,6},{8,9},{9,8},{10,11... | collective-permute-start | bytes 983048 | tf_op jit(solution)/shard_map/ppermute | solution.py:73
  166.1 2.3 %collective-permute-start.33 = (bf16[320,512]{1,0:T(8,128)(2,1)S(1)}, bf16[320,512]{1,0:T(8,128)(2,1)S(1)}, u32[]{:S(2)}, u32[]{:S(2)}) collective-permute-start(bf16[320,512]{1,0:T(8,128)(2,1)S(1)} %collective-permute-done.29.refs_4_), channel_id=1, source_target_pairs={{0,1},{1,0},{2,3},{3,2},{4,5},{5,4},{6,7},{7,6},{8,9},{9,8},{10,11... | collective-permute-start | bytes 983048 | tf_op jit(solution)/shard_map/ppermute | solution.py:73
  169.1 1.0 copy-start.20
  (3 other events, 2.0 us)
where the time goes:
time: 175 us; the launch traced here: 174 us
  waiting for transfers between devices  69.1 us (39%)
  starting transfers between devices  46.2 us (26%)
  Pallas kernels  32 us (18%)
  local copies, waits for them, and re-layouts  18.1 us (10%)
  matrix products  4.52 us (3%)
  other arithmetic  3.4 us (2%)
    ppermute x34, waiting for transfers between devices, exchange(): return lax.ppermute(block, axis, pairs)  40.6 us
    pallas_call x8, Pallas kernels, call(): pl.pallas_call(kernel, out_shape=outs, in_specs=[SMEM] * scalars + [VMEM]...  32 us
    ppermute x34, starting transfers between devices, exchange(): return lax.ppermute(block, axis, pairs)  25.5 us
    all_to_all x1, waiting for transfers between devices, local(): lax.all_to_all(picked.reshape(devices, padded, width), everyone, split_ax...  15.6 us
    unnamed x56, local copies, waits for them, and re-layouts  14.3 us
    all_to_all x1, starting transfers between devices, local(): lax.all_to_all(requests.reshape(devices, padded), everyone, split_axis=0,...  7.33 us
    all_to_all x1, waiting for transfers between devices, local(): lax.all_to_all(requests.reshape(devices, padded), everyone, split_axis=0,...  7.09 us
    all_to_all x1, starting transfers between devices, local(): lax.all_to_all(columns, 'cp', split_axis=0, concat_axis=0, tiled=True)  4.22 us
  transfers between devices with their start and end apart: 39, of which 20 were waited for; matrix products, arithmetic and copies ran while one was open for 1% of the time, Pallas kernels for 9%

commit v1 on v0

--- a/solution.py
+++ b/solution.py
@@ -135,6 +135,82 @@
         gap = (here - source_of(here, step, group)) * tokens
         allowed = (column - row <= gap) if forward else (column - row >= gap)
         mask_ref[:, n * tokens : (n + 1) * tokens] = allowed.astype(f32)
+
+
+def unit_mask(size):
+    row = lax.broadcasted_iota(jnp.int32, (size, size), 0)
+    return row == lax.broadcasted_iota(jnp.int32, (size, size), 1)
+
+
+def as_row(column):
+    return jnp.sum(jnp.where(unit_mask(column.shape[0]), column, 0), axis=0, keepdims=True)
+
+
+def as_column(row):
+    return jnp.sum(jnp.where(unit_mask(row.shape[1]), row, 0), axis=1, keepdims=True)
+
+
+def selected(flags):
+    return flags.astype(f32).astype(low)
+
+
+def request_kernel(here_ref, owner_ref, slot_ref, request_ref, rank_ref, column_ref):
+    tokens = owner_ref.shape[0]
+    devices = request_ref.shape[0]
+    named = owner_ref[...] == lax.broadcasted_iota(jnp.int32, (tokens, devices), 1)
+    row = lax.broadcasted_iota(jnp.int32, (tokens, tokens), 0)
+    lower = selected(row > lax.broadcasted_iota(jnp.int32, (tokens, tokens), 1))
+    earlier = dot(lower, selected(named))
+    rank = jnp.sum(jnp.where(named, earlier, 0.0), axis=1, keepdims=True).astype(jnp.int32)
+    rank_ref[...] = rank
+    slot = as_column(slot_ref[...])
+    column_ref[...] = slot
+    ranked = rank == lax.broadcasted_iota(jnp.int32, (tokens, LANES), 1)
+    code = slot + 1
+    high = jnp.where(ranked, code >> 6, 0).astype(f32).astype(low)
+    rest = jnp.where(ranked, code & 63, 0).astype(f32).astype(low)
+    names = selected(named)
+    total = dot(names, high, (0, 0)) * 64.0 + dot(names, rest, (0, 0)) - 1.0
+    request_ref[...] = total.astype(jnp.int32).reshape(devices, 1, LANES)
+
+
+def asked_select(asked, capacity, first, count):
+    index = lax.broadcasted_iota(jnp.int32, (asked.shape[0], count), 1) + first
+    parts = [selected(asked[:, n : n + 1] == index) for n in range(capacity)]
+    return jnp.concatenate(parts, axis=0)
+
+
+def pick_kernel(capacity, here_ref, asked_ref, hot_ref, cold_ref, out_ref):
+    devices = asked_ref.shape[0]
+    hot_count, width = hot_ref.shape
+    cold_count, cold_width = cold_ref.shape
+    asked = asked_ref[...].reshape(devices, LANES)
+    hot = dot(asked_select(asked, capacity, 0, hot_count), hot_ref[...])
+    cold = dot(asked_select(asked, capacity, hot_count, cold_count), cold_ref[...])
+    tiles = [hot[:, n * LANES : (n + 1) * LANES] for n in range(width // LANES)]
+    for n in range(cold_width // LANES):
+        tiles[n] = tiles[n] + cold[:, n * LANES : (n + 1) * LANES]
+    stack = jnp.concatenate(tiles, axis=0).reshape(len(tiles) * capacity, devices, LANES)
+    out_ref[...] = jnp.swapaxes(stack, 0, 1).reshape(out_ref.shape).astype(low)
+
+
+def embed_kernel(capacity, hot_count, *refs):
+    _, owner_ref, rank_ref, slot_ref, rows_ref, cold_ref = refs[:6]
+    vector_ref, embedded_ref, normed_ref = refs[6:]
+    tokens, width = embedded_ref.shape
+    cold_width = cold_ref.shape[0]
+    tiles = width // LANES
+    base = owner_ref[...] * (tiles * capacity) + rank_ref[...]
+    index = lax.broadcasted_iota(jnp.int32, (tokens, rows_ref.shape[0]), 1)
+    parts = [
+        dot(selected(index == base + n * capacity), rows_ref[...]) for n in range(tiles)
+    ]
+    vector = jnp.concatenate(parts, axis=1)
+    narrow = vector[:, :cold_width].astype(low)
+    vector_ref[...] = narrow
+    embedded = jnp.where(slot_ref[...] >= hot_count, dot(narrow, cold_ref[...]), vector)
+    embedded_ref[...] = embedded
+    normed_ref[...] = layer_normalize(embedded)[0].astype(low)
 
 
 def hidden_kernel(here_ref, normed_ref, weight_ref, hidden_ref, active_ref):
@@ -271,12 +347,13 @@
         columns_ref[n, 2 * share :] = late[3 * n * share : 3 * (n + 1) * share]
 
 
-def row_kernel(head_rows, capacity, *refs):
+def row_kernel(head_rows, capacity, stride, *refs):
     _, gate_ref, rest_ref, weight_ref, embedded_ref, cotangent_ref = refs[:6]
-    vector_ref, slot_ref, place_ref, cold_ref, sent_ref = refs[6:]
-    tokens, width = embedded_ref.shape
+    vector_ref, owner_ref, rank_ref, slot_ref, cold_ref, sent_ref = refs[6:]
+    _, width = embedded_ref.shape
     cold_width = cold_ref.shape[0]
-    devices, padded, _ = sent_ref.shape
+    tiles = width // LANES
+    devices = sent_ref.shape[0] // (tiles * stride)
     delta_normed = dot(gate_ref[...], weight_ref[:, :width], (1, 1))
     delta_normed += dot(rest_ref[...], weight_ref[:, width:], (1, 1))
     normed, inverse = layer_normalize(embedded_ref[...])
@@ -287,14 +364,21 @@
     hot_event = jnp.where(cold, 0.0, delta_embed)
     narrow = jnp.where(cold, cold_event, hot_event[:, :cold_width])
     event = jnp.concatenate([narrow, hot_event[:, cold_width:]], axis=1).astype(low)
-    place = lax.broadcasted_iota(jnp.int32, (tokens, devices * padded), 1)
-    chosen = (place == place_ref[...]).astype(f32).astype(low)
-    sent_ref[...] = dot(chosen, event, (0, 0)).astype(low).reshape(sent_ref.shape)
-    cold_rows = jnp.where(cold, vector_ref[:, :cold_width].astype(f32), 0.0).astype(low)
+    cold_rows = jnp.where(cold, vector_ref[...].astype(f32), 0.0).astype(low)
     part = dot(cold_rows, delta_low, (0, 0)).astype(low)
     each = cold_width // devices
-    for n in range(devices):
-        sent_ref[n, capacity : capacity + each] = part[n * each : (n + 1) * each]
+    row = lax.broadcasted_iota(jnp.int32, (1, cold_width), 1)
+    own = (row // each) * (tiles * stride) + capacity + row % each
+    place = as_row(owner_ref[...] * (tiles * stride) + rank_ref[...])
+    place = jnp.concatenate([place, own], axis=1)
+    both = jnp.concatenate([event, part], axis=0)
+    index = lax.broadcasted_iota(jnp.int32, (sent_ref.shape[0], place.shape[1]), 0)
+    total = None
+    for n in range(tiles):
+        chosen = selected(index == place + n * stride)
+        term = dot(chosen, both[:, n * LANES : (n + 1) * LANES])
+        total = term if n == 0 else total + term
+    sent_ref[...] = total.astype(low)
 
 
 def weight_kernel(group, count, *refs):
@@ -347,22 +431,25 @@
         joined_ref[:, (n + 1) * width : (n + 2) * width] = columns
 
 
-def scatter_kernel(capacity, each, *refs):
+def scatter_kernel(capacity, stride, each, *refs):
     _, asked_ref, arrived_ref, hot_ref, cold_ref, mine_ref = refs
-    devices, padded, width = arrived_ref.shape
-    slots = devices * padded
-    hot_count, cold_width = hot_ref.shape[0], cold_ref.shape[1]
-    rows = arrived_ref[...].reshape(slots, width)
-    asked = asked_ref[...]
-    index = lax.broadcasted_iota(jnp.int32, (hot_count, slots), 0)
-    for n in range(cold_ref.shape[0] // hot_count):
-        chosen = (index + (n + 1) * hot_count == asked).astype(f32).astype(low)
-        cold_ref[n * hot_count : (n + 1) * hot_count, :] = dot(chosen, rows[:, :cold_width])
-    hot_ref[...] = dot((index == asked).astype(f32).astype(low), rows)
-    total = arrived_ref[0].astype(f32)
-    for n in range(1, devices):
-        total = total + arrived_ref[n].astype(f32)
-    mine_ref[...] = total[capacity : capacity + each].astype(low)
+    devices = asked_ref.shape[0]
+    hot_count, width = hot_ref.shape
+    cold_count, cold_width = cold_ref.shape
+    tiles = width // LANES
+    asked = asked_ref[...].reshape(devices, LANES)
+    stack = arrived_ref[...].astype(f32).reshape(devices, tiles * stride, LANES)
+    stack = jnp.swapaxes(stack, 0, 1)
+    rows, sums = [], []
+    for n in range(tiles):
+        part = stack[n * stride : n * stride + capacity]
+        rows.append(part.reshape(capacity * devices, LANES).astype(low))
+        sums.append(jnp.sum(stack[n * stride + capacity : n * stride + capacity + each], axis=1))
+    rows = jnp.concatenate(rows, axis=1)
+    hot_ref[...] = dot(asked_select(asked, capacity, 0, hot_count), rows, (0, 0))
+    chosen = asked_select(asked, capacity, hot_count, cold_count)
+    cold_ref[...] = dot(chosen, rows[:, :cold_width], (0, 0))
+    mine_ref[...] = jnp.concatenate(sums, axis=1).astype(low)
 
 
 def assemble(position, pieces, norm_scale, width):
@@ -412,35 +499,47 @@
     length = group * tokens
     position = jnp.stack([lax.axis_index("cp"), lax.axis_index("dp")]).astype(jnp.int32)
     capacity = 2 * tokens // devices + 2
-    padded = -(-(capacity + cold_width // devices) // 8) * 8
-    slots = devices * padded
-    owners = row_owner[:, 0]
-    is_hot = slot_row < hot_count
-    named = owners[:, None] == jnp.arange(devices, dtype=jnp.int32)[None, :]
-    onehot = named.astype(low)
-    lower = (jnp.arange(tokens)[:, None] > jnp.arange(tokens)[None, :]).astype(low)
-    earlier = jnp.dot(lower, onehot, preferred_element_type=f32)
-    rank = jnp.sum(jnp.where(named, earlier, 0.0), axis=1).astype(jnp.int32)
-    place = owners * padded + rank
-    chosen = place[:, None] == jnp.arange(slots, dtype=jnp.int32)[None, :]
-    requests = jnp.max(jnp.where(chosen, slot_row[:, None], -1), axis=0)
-    asked = lax.all_to_all(
-        requests.reshape(devices, padded), everyone, split_axis=0, concat_axis=0, tiled=True
-    ).reshape(-1)
-    hot_select = asked[:, None] == jnp.arange(hot_count, dtype=jnp.int32)[None, :]
-    cold_select = asked[:, None] == jnp.arange(hot_count, hot_count + cold_count, dtype=jnp.int32)
-    hot_pick = jnp.dot(hot_select.astype(low), hot_table, preferred_element_type=low)
-    cold_pick = jnp.dot(cold_select.astype(low), cold_table, preferred_element_type=low)
-    picked = hot_pick + jnp.pad(cold_pick, ((0, 0), (0, width - cold_width)))
+    tiles = width // LANES
+    each = cold_width // devices
+    stride = capacity + each
+    while tiles * stride % 8:
+        stride += 1
+    requests, rank, slot = call(
+        request_kernel,
+        [position, row_owner, slot_row[None, :]],
+        [
+            shaped((devices, 1, LANES), jnp.int32),
+            shaped((tokens, 1), jnp.int32),
+            shaped((tokens, 1), jnp.int32),
+        ],
+    )
+    asked = lax.all_to_all(requests, everyone, split_axis=0, concat_axis=0, tiled=True)
+    cotangents = gather_pieces(cotangent, "cp")
+    near = (group + 1) // 2
+    asked, *front = lax.optimization_barrier((asked, *cotangents[:near]))
+    cotangents = front + cotangents[near:]
+    picked = call(
+        functools.partial(pick_kernel, capacity),
+        [position, asked, hot_table, cold_table],
+        [shaped((devices * tiles * capacity, LANES), low)],
+    )[0]
     rows_back = lax.all_to_all(
-        picked.reshape(devices, padded, width), everyone, split_axis=0, concat_axis=0, tiled=True
-    ).reshape(slots, width)
-    held_cotangent, _ = lax.optimization_barrier((cotangent, asked))
-    cotangents = gather_pieces(held_cotangent, "cp")
-    vector = jnp.dot(chosen.astype(low), rows_back, preferred_element_type=low)
-    cold_embed = jnp.dot(vector[:, :cold_width], cold_projection, preferred_element_type=f32)
-    embedded = jnp.where(is_hot[:, None], vector.astype(f32), cold_embed)
-    normed_low = layer_normalize(embedded)[0].astype(low)
+        picked.reshape(devices, tiles * capacity, LANES),
+        everyone,
+        split_axis=0,
+        concat_axis=0,
+        tiled=True,
+    ).reshape(picked.shape)
+    vector, embedded, normed_low = call(
+        functools.partial(embed_kernel, capacity, hot_count),
+        [position, row_owner, rank, slot, rows_back, cold_projection],
+        [
+            shaped((tokens, cold_width), low),
+            shaped((tokens, width), f32),
+            shaped((tokens, width), low),
+        ],
+    )
+    normed_low, *cotangents = lax.optimization_barrier((normed_low, *cotangents))
     hidden, active = call(
         hidden_kernel,
         [position, normed_low, joined_weight],
@@ -481,7 +580,7 @@
     )
     moved = lax.all_to_all(columns, "cp", split_axis=0, concat_axis=0, tiled=True)
     sent = call(
-        functools.partial(row_kernel, hot_count, capacity),
+        functools.partial(row_kernel, hot_count, capacity, stride),
         [
             position,
             gate_hidden,
@@ -490,13 +589,16 @@
             embedded,
             cotangent,
             vector,
-            slot_row[:, None],
-            place[:, None],
+            row_owner,
+            rank,
+            slot,
             cold_projection,
         ],
-        [shaped((devices, padded, width), low)],
+        [shaped((devices * tiles * stride, LANES), low)],
         flops=8 * tokens * width * width,
+        limit=56,
     )[0]
+    sent = sent.reshape(devices, tiles * stride, LANES)
     arrived = lax.all_to_all(sent, everyone, split_axis=0, concat_axis=0, tiled=True)
     count = lax.axis_size("dp")
     chunk = 5 * share // count
@@ -506,22 +608,23 @@
         [shaped((chunk, width), f32)] + [shaped((chunk, width), low)] * (count - 1),
         [pltpu.VMEM((count, chunk, width), f32)],
         10 * share * length * width,
+        limit=56,
     )
     for step, block in enumerate(sends, start=1):
         own = own + exchange(block, "dp", step).astype(f32)
     mine = own.astype(low)
     line = [mine] + [exchange(mine, "dp", step) for step in range(1, count)]
     line = jnp.concatenate(line, axis=0)
-    each = cold_width // devices
     hot_gradient, cold_gradient, total = call(
-        functools.partial(scatter_kernel, capacity, each),
-        [position, asked[None, :], arrived],
+        functools.partial(scatter_kernel, capacity, stride, each),
+        [position, asked, arrived.reshape(devices * tiles * stride, LANES)],
         [
             shaped((hot_count, width), f32),
             shaped((cold_count, cold_width), f32),
             shaped((each, width), low),
         ],
-        flops=4 * slots * hot_count * width,
+        flops=4 * devices * capacity * hot_count * width,
+        limit=56,
     )
     copies = jnp.broadcast_to(total[None], (devices, each, width))
     projection = lax.all_to_all(copies, everyone, split_axis=0, concat_axis=0, tiled=True)

time: 175 us -> 164 us (0.937)
  waiting for transfers between devices: 69.1 us -> 54.7 us
  blocking collectives: 0 us -> 13.3 us
  Pallas kernels: 32 us -> 42.4 us
  local copies, waits for them, and re-layouts: 18.1 us -> 10 us
  starting transfers between devices: 46.2 us -> 40.3 us
  matrix products: 4.52 us -> 0 us
  other arithmetic: 3.4 us -> 1.12 us
    all_to_all x0 -> x1, blocking collectives: none -> 13.3 us  [local(): lax.all_to_all(requests, everyone, split_axis=0, concat_axis=0, tiled=True)]
    all_to_all x2 -> x1, waiting for transfers between devices: 22.7 us -> 10.9 us  [local(): lax.all_to_all(picked.reshape(devices, tiles * capacity, LANES), everyone...]
    pallas_call x8 -> x11, Pallas kernels: 32 us -> 42.4 us  [call(): pl.pallas_call(kernel, out_shape=outs, in_specs=[SMEM] * scalars + [VMEM]...]
    ppermute x34, waiting for transfers between devices: 40.6 us -> 32.1 us  [exchange(): return lax.ppermute(block, axis, pairs)]
    all_to_all x2 -> x1, starting transfers between devices: 9.93 us -> 2.59 us  [local(): lax.all_to_all(picked.reshape(devices, tiles * capacity, LANES), everyone...]
    unnamed x56 -> x69, local copies, waits for them, and re-layouts: 14.3 us -> 7.87 us
    dot_general x5 -> x0, matrix products: 4.52 us -> none  [the longest x1 1.83 us: local(): jnp.dot(cold_select.astype(low), cold_table, preferred_element_type=low)]
    all_to_all x1, waiting for transfers between devices: 2.26 us -> 6.16 us  [local(): lax.all_to_all(columns, 'cp', split_axis=0, concat_axis=0, tiled=True)]
  transfers between devices with their start and end apart: 39 -> 38, of which waited for: 20 -> 15; matrix products, arithmetic and copies ran while one was open for 1% -> 2% of each run, Pallas kernels for 9% -> 13%
where the time goes in v1:
time: 164 us; the launch traced here: 163 us
  waiting for transfers between devices  54.7 us (33%)
  Pallas kernels  42.4 us (26%)
  starting transfers between devices  40.3 us (25%)
  blocking collectives  13.3 us (8%)
  local copies, waits for them, and re-layouts  10 us (6%)
    pallas_call x11, Pallas kernels, call(): pl.pallas_call(kernel, out_shape=outs, in_specs=[SMEM] * scalars + [VMEM]...  42.4 us
    ppermute x34, waiting for transfers between devices, exchange(): return lax.ppermute(block, axis, pairs)  32.1 us
    ppermute x34, starting transfers between devices, exchange(): return lax.ppermute(block, axis, pairs)  27.3 us
    all_to_all x1, blocking collectives, local(): lax.all_to_all(requests, everyone, split_axis=0, concat_axis=0, tiled=True)  13.3 us
    all_to_all x1, waiting for transfers between devices, local(): lax.all_to_all(picked.reshape(devices, tiles * capacity, LANES), everyone...  10.9 us
    unnamed x69, local copies, waits for them, and re-layouts  7.87 us
    all_to_all x1, waiting for transfers between devices, local(): lax.all_to_all(columns, 'cp', split_axis=0, concat_axis=0, tiled=True)  6.16 us
    all_to_all x1, waiting for transfers between devices, local(): lax.all_to_all(copies, everyone, split_axis=0, concat_axis=0, tiled=True)  5.51 us
  transfers between devices with their start and end apart: 38, of which 15 were waited for; matrix products, arithmetic and copies ran while one was open for 2% of the time, Pallas kernels for 13%

profile of v1, /device:TPU:0, one launch (start us, length us, event | category | flops | bytes accessed | tf_op | source)
XLA Modules:
  0.0 163.0 jit_solution(11421971092164275858)
XLA Ops:
  0.7 3.0 %collective-permute-start = (bf16[128,512]{1,0:T(8,128)(2,1)}, bf16[128,512]{1,0:T(8,128)(2,1)S(1)}, u32[]{:S(2)}, u32[]{:S(2)}) collective-permute-start(bf16[128,512]{1,0:T(8,128)(2,1)} %refs_2_), channel_id=1, source_target_pairs={{0,2},{1,3},{2,0},{3,1},{4,6},{5,7},{6,4},{7,5},{8,10},{9,11},{10,... | collective-permute-start | bytes 393224 | tf_op jit(solution)/shard_map/ppermute | solution.py:73
  3.7 1.5 collective-permute-start.1
  5.2 0.8 copy.15.owner_ref.refs_1_.refs_7_
  6.1 0.7 copy-done.26
  6.7 1.0 shard_map.127
  7.7 13.3 %all_to_all.25.asked_ref.refs_1_ = s32[32,1,128]{2,1,0:T(1,128)S(1)} all-to-all(s32[32,1,128]{2,1,0:T(1,128)S(1)} %get-tuple-element.52), channel_id=1, replica_groups=mesh['dp'=4,'cp'=8] {'dp','cp'}, dimensions={0} | all-to-all | bytes 32768 | tf_op jit(solution)/shard_map/all_to_all | solution.py:516
  21.1 1.1 copy-done.12
  22.2 1.0 copy-done.13
  23.2 2.7 %shard_map.128 = bf16[1280,128]{1,0:T(8,128)(2,1)} custom-call(s32[2]{0:T(128)S(1)} %pad_add_fusion.here_ref.refs_0_, s32[32,1,128]{2,1,0:T(1,128)S(1)} %all_to_all.25.asked_ref.refs_1_, bf16[512,512]{1,0:T(8,128)(2,1)S(1)} %copy-done.12, bf16[2048,128]{1,0:T(8,128)(2,1)S(1)} %copy-done.13), custom_call_target="tpu_custom_call" | custom-call | bytes 1392648 | tf_op jit(solution)/shard_map/pallas_call | solution.py:96
  25.9 2.6 %all-to-all-start.1 = ((bf16[32,40,128]{2,1,0:T(8,128)(2,1)}), bf16[32,40,128]{2,1,0:T(8,128)(2,1)S(1)}, u32[]{:S(2)}, u32[]{:S(2)}) async-start(bf16[32,40,128]{2,1,0:T(8,128)(2,1)} %bitcast.3), calls=%async_computation.1 | async-start | bytes 655360 | tf_op jit(solution)/shard_map/all_to_all | solution.py:526
  28.7 0.4 collective-permute-start.4
  29.2 0.4 collective-permute-start.6
  29.6 10.9 %all-to-all-done.1 = bf16[32,40,128]{2,1,0:T(8,128)(2,1)S(1)} async-done(((bf16[32,40,128]{2,1,0:T(8,128)(2,1)}), bf16[32,40,128]{2,1,0:T(8,128)(2,1)S(1)}, u32[]{:S(2)}, u32[]{:S(2)}) %all-to-all-start.1) | async-done | bytes 327712 | tf_op jit(solution)/shard_map/all_to_all | solution.py:526
  40.6 0.9 copy-done.15
  41.5 1.4 shard_map.129
  42.9 0.2 collective-permute-start.7
  43.2 1.5 collective-permute-start.8
  44.7 1.8 %collective-permute-start.9 = (bf16[128,512]{1,0:T(8,128)(2,1)S(1)}, bf16[128,512]{1,0:T(8,128)(2,1)S(1)}, u32[]{:S(2)}, u32[]{:S(2)}) collective-permute-start(bf16[128,512]{1,0:T(8,128)(2,1)S(1)} %get-tuple-element.59.normed_ref.refs_1_.refs_10_), channel_id=1, source_target_pairs={{0,6},{1,7},{2,4},{3,5},{4,2},{5,3},{6,0},{7,1},{8,14},{9,15},{10,... | collective-permute-start | bytes 393224 | tf_op jit(solution)/shard_map/ppermute | solution.py:73
  46.5 2.2 %collective-permute-done.7.refs_2_.refs_11_ = bf16[128,512]{1,0:T(8,128)(2,1)S(1)} collective-permute-done((bf16[128,512]{1,0:T(8,128)(2,1)S(1)}, bf16[128,512]{1,0:T(8,128)(2,1)S(1)}, u32[]{:S(2)}, u32[]{:S(2)}) %collective-permute-start.7) | collective-permute-done | bytes 131104 | tf_op jit(solution)/shard_map/ppermute | solution.py:73
  48.7 2.9 %collective-permute-done.8.refs_3_.refs_12_ = bf16[128,512]{1,0:T(8,128)(2,1)S(1)} collective-permute-done((bf16[128,512]{1,0:T(8,128)(2,1)S(1)}, bf16[128,512]{1,0:T(8,128)(2,1)S(1)}, u32[]{:S(2)}, u32[]{:S(2)}) %collective-permute-start.8) | collective-permute-done | bytes 131104 | tf_op jit(solution)/shard_map/ppermute | solution.py:73
  51.7 0.5 collective-permute-start.13
  52.2 0.6 copy-done.22
  52.8 1.0 shard_map.130
  54.0 1.2 copy-done.14
  55.2 7.3 %shard_map.131 = (bf16[128,512]{1,0:T(8,128)(2,1)}, bf16[128,512]{1,0:T(8,128)(2,1)S(1)}, bf16[128,512]{1,0:T(8,128)(2,1)S(1)}, bf16[8,128,128]{2,1,0:T(8,128)(2,1)S(1)}, bf16[1024,1024]{1,0:T(8,128)(2,1)S(1)}) custom-call(s32[2]{0:T(128)S(1)} %copy-done.22, bf16[128,512]{1,0:T(8,128)(2,1)S(1)} %get-tuple-element.59.normed_ref.refs_1_.refs_10_, ...), custom_call_target="tpu_custom_call" | custom-call | flops 1342177280 | bytes 8388616 | tf_op jit(solution)/shard_map/pallas_call | solution.py:96
  62.5 1.1 collective-permute-start.14
  63.6 0.8 collective-permute-start.15
  64.4 1.6 collective-permute-start.16
  66.0 2.8 %collective-permute-done.14.refs_2_ = bf16[128,512]{1,0:T(8,128)(2,1)S(1)} collective-permute-done((bf16[128,512]{1,0:T(8,128)(2,1)S(1)}, bf16[128,512]{1,0:T(8,128)(2,1)S(1)}, u32[]{:S(2)}, u32[]{:S(2)}) %collective-permute-start.14) | collective-permute-done | bytes 131104 | tf_op jit(solution)/shard_map/ppermute | solution.py:73
  68.8 2.8 %collective-permute-done.15.refs_3_ = bf16[128,512]{1,0:T(8,128)(2,1)S(1)} collective-permute-done((bf16[128,512]{1,0:T(8,128)(2,1)S(1)}, bf16[128,512]{1,0:T(8,128)(2,1)S(1)}, u32[]{:S(2)}, u32[]{:S(2)}) %collective-permute-start.15) | collective-permute-done | bytes 131104 | tf_op jit(solution)/shard_map/ppermute | solution.py:73
  71.6 0.5 collective-permute-start.20
  72.2 6.3 %shard_map.132 = (bf16[128,512]{1,0:T(8,128)(2,1)S(1)}, bf16[1024,512]{1,0:T(8,128)(2,1)S(1)}) custom-call(s32[2]{0:T(128)S(1)} %copy-done.23, bf16[128,512]{1,0:T(8,128)(2,1)S(1)} %get-tuple-element.59.normed_ref.refs_1_.refs_10_, bf16[128,512]{1,0:T(8,128)(2,1)S(1)} %collective-permute-done.7.refs_2_.refs_11_, ...), custom_call_target="tpu_custom_call" | custom-call | flops 402653184 | bytes 8126472 | tf_op jit(solution)/shard_map/pallas_call | solution.py:96
  78.5 6.1 %shard_map.133 = (bf16[128,1536]{1,0:T(8,128)(2,1)S(1)}, bf16[8,320,128]{2,1,0:T(8,128)(2,1)}) custom-call(s32[2]{0:T(128)S(1)} %copy-done.23, bf16[128,512]{1,0:T(8,128)(2,1)S(1)} %get-tuple-element.65.refs_12_.refs_1_, bf16[128,512]{1,0:T(8,128)(2,1)S(1)} %collective-permute-done.14.refs_2_, bf16[128,512]{1,0:T(8,128)(2,1)S(1)} %collective-permute-done.15.refs_3_, ...), custom_call_target="tpu_custom_call" | custom-call | flops 536870912 | bytes 5111816 | tf_op jit(solution)/shard_map/pallas_call | solution.py:96
  84.7 0.7 copy-done.16
  85.4 3.5 %all-to-all-start.4 = ((bf16[8,320,128]{2,1,0:T(8,128)(2,1)}), bf16[8,320,128]{2,1,0:T(8,128)(2,1)S(1)}, u32[]{:S(2)}, u32[]{:S(2)}) async-start(bf16[8,320,128]{2,1,0:T(8,128)(2,1)} %get-tuple-element.75), calls=%async_computation.4 | async-start | bytes 1310720 | tf_op jit(solution)/shard_map/all_to_all | solution.py:581
  89.0 4.9 %shard_map.134 = bf16[1792,128]{1,0:T(8,128)(2,1)} custom-call(s32[2]{0:T(128)} %copy-done.21, bf16[128,512]{1,0:T(8,128)(2,1)} %copy-done.19, bf16[128,1536]{1,0:T(8,128)(2,1)} %copy-done.16, bf16[512,2048]{1,0:T(8,128)(2,1)} %refs_3_.1, f32[128,512]{1,0:T(8,128)} %copy-done.11, bf16[128,512]{1,0:T(8,128)(2,1)} %refs_2_, bf16[128,128]{1,0:T(8,128)(2,1)} %copy-done.25, ...), custom_call_target="tpu_custom_call" | custom-call | flops 268435456 | bytes 3638792 | tf_op jit(solution)/shard_map/pallas_call | solution.py:96
  93.9 6.2 %all-to-all-done.4.refs_1_ = bf16[8,320,128]{2,1,0:T(8,128)(2,1)S(1)} async-done(((bf16[8,320,128]{2,1,0:T(8,128)(2,1)}), bf16[8,320,128]{2,1,0:T(8,128)(2,1)S(1)}, u32[]{:S(2)}, u32[]{:S(2)}) %all-to-all-start.4) | async-done | bytes 655392 | tf_op jit(solution)/shard_map/all_to_all | solution.py:581
  100.0 2.8 %all-to-all-start.2 = ((bf16[32,56,128]{2,1,0:T(8,128)(2,1)}), bf16[32,56,128]{2,1,0:T(8,128)(2,1)S(1)}, u32[]{:S(2)}, u32[]{:S(2)}) async-start(bf16[32,56,128]{2,1,0:T(8,128)(2,1)} %bitcast.9), calls=%async_computation.2 | async-start | bytes 917504 | tf_op jit(solution)/shard_map/all_to_all | solution.py:602
  102.8 3.4 %shard_map.136 = (f32[80,512]{1,0:T(8,128)}, bf16[80,512]{1,0:T(8,128)(2,1)}, bf16[80,512]{1,0:T(8,128)(2,1)}, bf16[80,512]{1,0:T(8,128)(2,1)}) custom-call(s32[2]{0:T(128)} %copy-done.21, bf16[8,320,128]{2,1,0:T(8,128)(2,1)} %copy-done.27, bf16[128,512]{1,0:T(8,128)(2,1)} %refs_2_, bf16[128,512]{1,0:T(8,128)(2,1)} %copy-done.29, ...), custom_call_target="tpu_custom_call" | custom-call | flops 335544320 | bytes 3162120 | tf_op jit(solution)/shard_map/pallas_call | solution.py:96
  106.2 1.6 collective-permute-start.21
  107.8 2.5 %collective-permute-start.22 = (bf16[80,512]{1,0:T(8,128)(2,1)}, bf16[80,512]{1,0:T(8,128)(2,1)S(1)}, u32[]{:S(2)}, u32[]{:S(2)}) collective-permute-start(bf16[80,512]{1,0:T(8,128)(2,1)} %get-tuple-element.86), channel_id=1, source_target_pairs={{0,16},{8,24},{16,0},{24,8},{1,17},{9,25},{17,1},{25,9},{2,18},{10... | collective-permute-start | bytes 245768 | tf_op jit(solution)/shard_map/ppermute | solution.py:73
  110.3 0.4 collective-permute-start.23
  110.7 2.4 %collective-permute-done.21 = bf16[80,512]{1,0:T(8,128)(2,1)S(1)} collective-permute-done((bf16[80,512]{1,0:T(8,128)(2,1)}, bf16[80,512]{1,0:T(8,128)(2,1)S(1)}, u32[]{:S(2)}, u32[]{:S(2)}) %collective-permute-start.21) | collective-permute-done | bytes 81952 | tf_op jit(solution)/shard_map/ppermute | solution.py:73
  113.1 8.9 %collective-permute-done.22 = bf16[80,512]{1,0:T(8,128)(2,1)S(1)} collective-permute-done((bf16[80,512]{1,0:T(8,128)(2,1)}, bf16[80,512]{1,0:T(8,128)(2,1)S(1)}, u32[]{:S(2)}, u32[]{:S(2)}) %collective-permute-start.22) | collective-permute-done | bytes 81952 | tf_op jit(solution)/shard_map/ppermute | solution.py:73
  122.0 1.0 add_convert_fusion
  123.0 1.8 %collective-permute-start.24 = (bf16[80,512]{1,0:T(8,128)(2,1)S(1)}, bf16[80,512]{1,0:T(8,128)(2,1)S(1)}, u32[]{:S(2)}, u32[]{:S(2)}) collective-permute-start(bf16[80,512]{1,0:T(8,128)(2,1)S(1)} %add_convert_fusion), channel_id=1, source_target_pairs={{0,8},{8,0},{16,24},{24,16},{1,9},{9,1},{17,25},{25,17},{2,10},{10... | collective-permute-start | bytes 245768 | tf_op jit(solution)/shard_map/ppermute | solution.py:73
  124.8 2.6 %collective-permute-start.26 = (bf16[80,512]{1,0:T(8,128)(2,1)S(1)}, bf16[80,512]{1,0:T(8,128)(2,1)S(1)}, u32[]{:S(2)}, u32[]{:S(2)}) collective-permute-start(bf16[80,512]{1,0:T(8,128)(2,1)S(1)} %add_convert_fusion), channel_id=1, source_target_pairs={{0,24},{8,16},{16,8},{24,0},{1,25},{9,17},{17,9},{25,1},{2,26},{10... | collective-permute-start | bytes 245768 | tf_op jit(solution)/shard_map/ppermute | solution.py:73
  127.6 6.0 %collective-permute-done.25 = bf16[80,512]{1,0:T(8,128)(2,1)S(1)} collective-permute-done((bf16[80,512]{1,0:T(8,128)(2,1)S(1)}, bf16[80,512]{1,0:T(8,128)(2,1)S(1)}, u32[]{:S(2)}, u32[]{:S(2)}) %collective-permute-start.25) | collective-permute-done | bytes 81952 | tf_op jit(solution)/shard_map/ppermute | solution.py:73
  133.6 1.6 collective-permute-start.27
  135.1 1.5 collective-permute-start.28
  136.7 0.4 collective-permute-start.29
  137.1 0.8 copy-done.28
  137.9 4.0 %shard_map.135 = (f32[512,512]{1,0:T(8,128)}, f32[2048,128]{1,0:T(8,128)}, bf16[4,512]{1,0:T(4,128)(2,1)}) custom-call(s32[2]{0:T(128)} %copy-done.21, s32[32,1,128]{2,1,0:T(1,128)} %copy-done.20, bf16[1792,128]{1,0:T(8,128)(2,1)} %bitcast.10), custom_call_target="tpu_custom_call" | custom-call | flops 335544320 | bytes 2576392 | tf_op jit(solution)/shard_map/pallas_call | solution.py:96
  141.9 1.4 broadcast_in_dim.10
  143.3 4.1 %all-to-all-start.3 = ((bf16[32,4,512]{2,1,0:T(4,128)(2,1)}), bf16[32,4,512]{2,1,0:T(4,128)(2,1)S(1)}, u32[]{:S(2)}, u32[]{:S(2)}) async-start(bf16[32,4,512]{2,1,0:T(4,128)(2,1)} %broadcast_in_dim.10), calls=%async_computation.3 | async-start | bytes 262144 | tf_op jit(solution)/shard_map/all_to_all | solution.py:630
  147.4 2.7 %collective-permute-done.28.refs_3_ = bf16[320,512]{1,0:T(8,128)(2,1)S(1)} collective-permute-done((bf16[320,512]{1,0:T(8,128)(2,1)S(1)}, bf16[320,512]{1,0:T(8,128)(2,1)S(1)}, u32[]{:S(2)}, u32[]{:S(2)}) %collective-permute-start.28) | collective-permute-done | bytes 327712 | tf_op jit(solution)/shard_map/ppermute | solution.py:73
  150.1 5.5 %all-to-all-done.3 = bf16[32,4,512]{2,1,0:T(4,128)(2,1)S(1)} async-done(((bf16[32,4,512]{2,1,0:T(4,128)(2,1)}), bf16[32,4,512]{2,1,0:T(4,128)(2,1)S(1)}, u32[]{:S(2)}, u32[]{:S(2)}) %all-to-all-start.3) | async-done | bytes 131104 | tf_op jit(solution)/shard_map/all_to_all | solution.py:630
  155.8 0.3 collective-permute-start.31
  156.3 0.3 collective-permute-start.33
  156.7 0.8 mul.11
  157.5 0.2 collective-permute-done.31.refs_6_
  157.7 0.5 collective-permute-done.32.refs_7_
  158.1 0.5 collective-permute-done.33.refs_8_
  158.6 4.4 %shard_map.137 = (f32[512,2048]{1,0:T(8,128)}, f32[512,512]{1,0:T(8,128)}) custom-call(s32[2]{0:T(128)S(1)} %copy-done.24, bf16[320,512]{1,0:T(8,128)(2,1)S(1)} %pad_maximum_fusion.refs_1_, bf16[320,512]{1,0:T(8,128)(2,1)S(1)} %collective-permute-done.27.refs_2_, bf16[320,512]{1,0:T(8,128)(2,1)S(1)} %collective-permute-done.28.refs_3_, ...), custom_call_target="tpu_custom_call" | custom-call | bytes 7864328 | tf_op jit(solution)/shard_map/pallas_call | solution.py:96
  (99 shorter events, 1.2 us)
Async XLA Ops:
  0.6 27.9 %copy-start.2 = (bf16[128,512]{1,0:T(8,128)(2,1)S(1)}, bf16[128,512]{1,0:T(8,128)(2,1)}, u32[]{:S(2)}) copy-start(bf16[128,512]{1,0:T(8,128)(2,1)} %refs_2_) | copy-start | bytes 393220
  0.6 51.5 %copy-start = (bf16[512,2048]{1,0:T(8,128)(2,1)S(1)}, bf16[512,2048]{1,0:T(8,128)(2,1)}, u32[]{:S(2)}) copy-start(bf16[512,2048]{1,0:T(8,128)(2,1)} %refs_3_.1) | copy-start | bytes 6291460
  0.7 20.4 %collective-permute-start = (bf16[128,512]{1,0:T(8,128)(2,1)}, bf16[128,512]{1,0:T(8,128)(2,1)S(1)}, u32[]{:S(2)}, u32[]{:S(2)}) collective-permute-start(bf16[128,512]{1,0:T(8,128)(2,1)} %refs_2_), channel_id=1, source_target_pairs={{0,2},{1,3},{2,0},{3,1},{4,6},{5,7},{6,4},{7,5},{8,10},{9,11},{10,... | collective-permute-start | bytes 393224 | tf_op jit(solution)/shard_map/ppermute | solution.py:73
  3.7 17.3 %collective-permute-start.1 = (bf16[128,512]{1,0:T(8,128)(2,1)}, bf16[128,512]{1,0:T(8,128)(2,1)S(1)}, u32[]{:S(2)}, u32[]{:S(2)}) collective-permute-start(bf16[128,512]{1,0:T(8,128)(2,1)} %refs_2_), channel_id=1, source_target_pairs={{0,4},{1,5},{2,6},{3,7},{4,0},{5,1},{6,2},{7,3},{8,12},{9,13},{10,... | collective-permute-start | bytes 393224 | tf_op jit(solution)/shard_map/ppermute | solution.py:73
  5.2 15.8 %collective-permute-start.2 = (bf16[128,512]{1,0:T(8,128)(2,1)}, bf16[128,512]{1,0:T(8,128)(2,1)S(1)}, u32[]{:S(2)}, u32[]{:S(2)}) collective-permute-start(bf16[128,512]{1,0:T(8,128)(2,1)} %refs_2_), channel_id=1, source_target_pairs={{0,6},{1,7},{2,4},{3,5},{4,2},{5,3},{6,0},{7,1},{8,14},{9,15},{10,... | collective-permute-start | bytes 393224 | tf_op jit(solution)/shard_map/ppermute | solution.py:73
  6.0 47.8 %copy-start.10 = (s32[128,1]{1,0:T(8,128)}, s32[128,1]{1,0:T(8,128)S(1)}, u32[]{:S(2)}) copy-start(s32[128,1]{1,0:T(8,128)S(1)} %copy.15.owner_ref.refs_1_.refs_7_) | copy-start | bytes 1540
  6.1 37.1 %copy-start.21 = (s32[2]{0:T(128)}, s32[2]{0:T(128)S(1)}, u32[]{:S(2)}) copy-start(s32[2]{0:T(128)S(1)} %pad_add_fusion.here_ref.refs_0_) | copy-start | bytes 28
  7.7 46.1 %copy-start.17 = (s32[128,1]{1,0:T(8,128)}, s32[128,1]{1,0:T(8,128)S(1)}, u32[]{:S(2)}) copy-start(s32[128,1]{1,0:T(8,128)S(1)} %get-tuple-element.50.refs_2_.refs_8_) | copy-start | bytes 1540
  7.7 46.1 %copy-start.18 = (s32[128,1]{1,0:T(8,128)}, s32[128,1]{1,0:T(8,128)S(1)}, u32[]{:S(2)}) copy-start(s32[128,1]{1,0:T(8,128)S(1)} %get-tuple-element.51.refs_3_.refs_9_) | copy-start | bytes 1540
  21.0 32.8 %copy-start.20 = (s32[32,1,128]{2,1,0:T(1,128)}, s32[32,1,128]{2,1,0:T(1,128)S(1)}, u32[]{:S(2)}) copy-start(s32[32,1,128]{2,1,0:T(1,128)S(1)} %all_to_all.25.asked_ref.refs_1_) | copy-start | bytes 49156
  21.0 32.8 %copy-start.29 = (bf16[128,512]{1,0:T(8,128)(2,1)}, bf16[128,512]{1,0:T(8,128)(2,1)S(1)}, u32[]{:S(2)}) copy-start(bf16[128,512]{1,0:T(8,128)(2,1)S(1)} %collective-permute-done.refs_3_) | copy-start | bytes 393220
  21.0 32.8 %copy-start.30 = (bf16[128,512]{1,0:T(8,128)(2,1)}, bf16[128,512]{1,0:T(8,128)(2,1)S(1)}, u32[]{:S(2)}) copy-start(bf16[128,512]{1,0:T(8,128)(2,1)S(1)} %collective-permute-done.1.refs_4_) | copy-start | bytes 393220
  23.2 30.7 %copy-start.31 = (bf16[128,512]{1,0:T(8,128)(2,1)}, bf16[128,512]{1,0:T(8,128)(2,1)S(1)}, u32[]{:S(2)}) copy-start(bf16[128,512]{1,0:T(8,128)(2,1)S(1)} %collective-permute-done.2.refs_5_) | copy-start | bytes 393220
  25.9 14.6 %all-to-all-start.1 = ((bf16[32,40,128]{2,1,0:T(8,128)(2,1)}), bf16[32,40,128]{2,1,0:T(8,128)(2,1)S(1)}, u32[]{:S(2)}, u32[]{:S(2)}) async-start(bf16[32,40,128]{2,1,0:T(8,128)(2,1)} %bitcast.3), calls=%async_computation.1 | async-start | bytes 655360 | tf_op jit(solution)/shard_map/all_to_all | solution.py:526
  28.5 14.4 %collective-permute-start.3 = (bf16[128,512]{1,0:T(8,128)(2,1)S(1)}, bf16[128,512]{1,0:T(8,128)(2,1)S(1)}, u32[]{:S(2)}, u32[]{:S(2)}) collective-permute-start(bf16[128,512]{1,0:T(8,128)(2,1)S(1)} %copy-done.2), channel_id=1, source_target_pairs={{0,1},{1,0},{2,3},{3,2},{4,5},{5,4},{6,7},{7,6},{8,9},{9,8},{10,11... | collective-permute-start | bytes 393224 | tf_op jit(solution)/shard_map/ppermute | solution.py:73
  28.7 14.2 %collective-permute-start.4 = (bf16[128,512]{1,0:T(8,128)(2,1)S(1)}, bf16[128,512]{1,0:T(8,128)(2,1)S(1)}, u32[]{:S(2)}, u32[]{:S(2)}) collective-permute-start(bf16[128,512]{1,0:T(8,128)(2,1)S(1)} %collective-permute-done.refs_3_), channel_id=1, source_target_pairs={{0,1},{1,0},{2,3},{3,2},{4,5},{5,4},{6,7},{7,6},{8,9},{9,8},{10,11... | collective-permute-start | bytes 393224 | tf_op jit(solution)/shard_map/ppermute | solution.py:73
  29.1 13.8 %collective-permute-start.5 = (bf16[128,512]{1,0:T(8,128)(2,1)S(1)}, bf16[128,512]{1,0:T(8,128)(2,1)}, u32[]{:S(2)}, u32[]{:S(2)}) collective-permute-start(bf16[128,512]{1,0:T(8,128)(2,1)S(1)} %collective-permute-done.1.refs_4_), channel_id=1, source_target_pairs={{0,1},{1,0},{2,3},{3,2},{4,5},{5,4},{6,7},{7,6},{8,9},{9,8},{10,11... | collective-permute-start | bytes 393224 | tf_op jit(solution)/shard_map/ppermute | solution.py:73
  29.2 13.7 %collective-permute-start.6 = (bf16[128,512]{1,0:T(8,128)(2,1)S(1)}, bf16[128,512]{1,0:T(8,128)(2,1)}, u32[]{:S(2)}, u32[]{:S(2)}) collective-permute-start(bf16[128,512]{1,0:T(8,128)(2,1)S(1)} %collective-permute-done.2.refs_5_), channel_id=1, source_target_pairs={{0,1},{1,0},{2,3},{3,2},{4,5},{5,4},{6,7},{7,6},{8,9},{9,8},{10,11... | collective-permute-start | bytes 393224 | tf_op jit(solution)/shard_map/ppermute | solution.py:73
  42.9 11.1 %copy-start.25 = (bf16[128,128]{1,0:T(8,128)(2,1)}, bf16[128,128]{1,0:T(8,128)(2,1)S(1)}, u32[]{:S(2)}) copy-start(bf16[128,128]{1,0:T(8,128)(2,1)S(1)} %get-tuple-element.71.refs_6_) | copy-start | bytes 98308
  42.9 19.6 %copy-start.11 = (f32[128,512]{1,0:T(8,128)}, f32[128,512]{1,0:T(8,128)S(1)}, u32[]{:S(2)}) copy-start(f32[128,512]{1,0:T(8,128)S(1)} %get-tuple-element.62.refs_12_.refs_4_) | copy-start | bytes 786436
  42.9 29.3 %copy-start.1 = (bf16[128,512]{1,0:T(8,128)(2,1)}, bf16[128,512]{1,0:T(8,128)(2,1)S(1)}, u32[]{:S(2)}) copy-start(bf16[128,512]{1,0:T(8,128)(2,1)S(1)} %get-tuple-element.59.normed_ref.refs_1_.refs_10_) | copy-start | bytes 393220
  42.9 19.6 %copy-start.32 = (bf16[128,512]{1,0:T(8,128)(2,1)}, bf16[128,512]{1,0:T(8,128)(2,1)S(1)}, u32[]{:S(2)}) copy-start(bf16[128,512]{1,0:T(8,128)(2,1)S(1)} %collective-permute-done.3.refs_6_) | copy-start | bytes 393220
  42.9 19.5 %copy-start.33 = (bf16[128,512]{1,0:T(8,128)(2,1)}, bf16[128,512]{1,0:T(8,128)(2,1)S(1)}, u32[]{:S(2)}) copy-start(bf16[128,512]{1,0:T(8,128)(2,1)S(1)} %collective-permute-done.4.refs_7_) | copy-start | bytes 393220
  42.9 5.8 %collective-permute-start.7 = (bf16[128,512]{1,0:T(8,128)(2,1)S(1)}, bf16[128,512]{1,0:T(8,128)(2,1)S(1)}, u32[]{:S(2)}, u32[]{:S(2)}) collective-permute-start(bf16[128,512]{1,0:T(8,128)(2,1)S(1)} %get-tuple-element.59.normed_ref.refs_1_.refs_10_), channel_id=1, source_target_pairs={{0,2},{1,3},{2,0},{3,1},{4,6},{5,7},{6,4},{7,5},{8,10},{9,11},{10,... | collective-permute-start | bytes 393224 | tf_op jit(solution)/shard_map/ppermute | solution.py:73
  43.2 8.5 %collective-permute-start.8 = (bf16[128,512]{1,0:T(8,128)(2,1)S(1)}, bf16[128,512]{1,0:T(8,128)(2,1)S(1)}, u32[]{:S(2)}, u32[]{:S(2)}) collective-permute-start(bf16[128,512]{1,0:T(8,128)(2,1)S(1)} %get-tuple-element.59.normed_ref.refs_1_.refs_10_), channel_id=1, source_target_pairs={{0,4},{1,5},{2,6},{3,7},{4,0},{5,1},{6,2},{7,3},{8,12},{9,13},{10,... | collective-permute-start | bytes 393224 | tf_op jit(solution)/shard_map/ppermute | solution.py:73
  44.7 7.0 %collective-permute-start.9 = (bf16[128,512]{1,0:T(8,128)(2,1)S(1)}, bf16[128,512]{1,0:T(8,128)(2,1)S(1)}, u32[]{:S(2)}, u32[]{:S(2)}) collective-permute-start(bf16[128,512]{1,0:T(8,128)(2,1)S(1)} %get-tuple-element.59.normed_ref.refs_1_.refs_10_), channel_id=1, source_target_pairs={{0,6},{1,7},{2,4},{3,5},{4,2},{5,3},{6,0},{7,1},{8,14},{9,15},{10,... | collective-permute-start | bytes 393224 | tf_op jit(solution)/shard_map/ppermute | solution.py:73
  46.5 7.4 %collective-permute-start.10 = (bf16[128,512]{1,0:T(8,128)(2,1)S(1)}, bf16[128,512]{1,0:T(8,128)(2,1)S(1)}, u32[]{:S(2)}, u32[]{:S(2)}) collective-permute-start(bf16[128,512]{1,0:T(8,128)(2,1)S(1)} %get-tuple-element.59.normed_ref.refs_1_.refs_10_), channel_id=1, source_target_pairs={{0,1},{1,0},{2,3},{3,2},{4,5},{5,4},{6,7},{7,6},{8,9},{9,8},{10,11... | collective-permute-start | bytes 393224 | tf_op jit(solution)/shard_map/ppermute | solution.py:73
  48.7 23.4 %copy-start.3 = (bf16[128,512]{1,0:T(8,128)(2,1)}, bf16[128,512]{1,0:T(8,128)(2,1)S(1)}, u32[]{:S(2)}) copy-start(bf16[128,512]{1,0:T(8,128)(2,1)S(1)} %collective-permute-done.7.refs_2_.refs_11_) | copy-start | bytes 393220
  48.7 5.2 %collective-permute-start.11 = (bf16[128,512]{1,0:T(8,128)(2,1)S(1)}, bf16[128,512]{1,0:T(8,128)(2,1)S(1)}, u32[]{:S(2)}, u32[]{:S(2)}) collective-permute-start(bf16[128,512]{1,0:T(8,128)(2,1)S(1)} %collective-permute-done.7.refs_2_.refs_11_), channel_id=1, source_target_pairs={{0,1},{1,0},{2,3},{3,2},{4,5},{5,4},{6,7},{7,6},{8,9},{9,8},{10,11... | collective-permute-start | bytes 393224 | tf_op jit(solution)/shard_map/ppermute | solution.py:73
  51.7 20.5 %copy-start.4 = (bf16[128,512]{1,0:T(8,128)(2,1)}, bf16[128,512]{1,0:T(8,128)(2,1)S(1)}, u32[]{:S(2)}) copy-start(bf16[128,512]{1,0:T(8,128)(2,1)S(1)} %collective-permute-done.8.refs_3_.refs_12_) | copy-start | bytes 393220
  51.7 2.3 %collective-permute-start.12 = (bf16[128,512]{1,0:T(8,128)(2,1)S(1)}, bf16[128,512]{1,0:T(8,128)(2,1)S(1)}, u32[]{:S(2)}, u32[]{:S(2)}) collective-permute-start(bf16[128,512]{1,0:T(8,128)(2,1)S(1)} %collective-permute-done.8.refs_3_.refs_12_), channel_id=1, source_target_pairs={{0,1},{1,0},{2,3},{3,2},{4,5},{5,4},{6,7},{7,6},{8,9},{9,8},{10,11... | collective-permute-start | bytes 393224 | tf_op jit(solution)/shard_map/ppermute | solution.py:73
  51.7 20.5 %copy-start.5 = (bf16[128,512]{1,0:T(8,128)(2,1)}, bf16[128,512]{1,0:T(8,128)(2,1)S(1)}, u32[]{:S(2)}) copy-start(bf16[128,512]{1,0:T(8,128)(2,1)S(1)} %collective-permute-done.9.refs_4_.refs_13_) | copy-start | bytes 393220
  51.7 2.3 %collective-permute-start.13 = (bf16[128,512]{1,0:T(8,128)(2,1)S(1)}, bf16[128,512]{1,0:T(8,128)(2,1)S(1)}, u32[]{:S(2)}, u32[]{:S(2)}) collective-permute-start(bf16[128,512]{1,0:T(8,128)(2,1)S(1)} %collective-permute-done.9.refs_4_.refs_13_), channel_id=1, source_target_pairs={{0,1},{1,0},{2,3},{3,2},{4,5},{5,4},{6,7},{7,6},{8,9},{9,8},{10,11... | collective-permute-start | bytes 393224 | tf_op jit(solution)/shard_map/ppermute | solution.py:73
  53.9 18.2 %copy-start.6 = (bf16[128,512]{1,0:T(8,128)(2,1)}, bf16[128,512]{1,0:T(8,128)(2,1)S(1)}, u32[]{:S(2)}) copy-start(bf16[128,512]{1,0:T(8,128)(2,1)S(1)} %collective-permute-done.10.refs_5_.refs_14_) | copy-start | bytes 393220
  53.9 18.2 %copy-start.7 = (bf16[128,512]{1,0:T(8,128)(2,1)}, bf16[128,512]{1,0:T(8,128)(2,1)S(1)}, u32[]{:S(2)}) copy-start(bf16[128,512]{1,0:T(8,128)(2,1)S(1)} %collective-permute-done.11.refs_6_.refs_15_) | copy-start | bytes 393220
  54.0 18.2 %copy-start.8 = (bf16[128,512]{1,0:T(8,128)(2,1)}, bf16[128,512]{1,0:T(8,128)(2,1)S(1)}, u32[]{:S(2)}) copy-start(bf16[128,512]{1,0:T(8,128)(2,1)S(1)} %collective-permute-done.12.refs_7_.refs_16_) | copy-start | bytes 393220
  54.0 18.2 %copy-start.9 = (bf16[128,512]{1,0:T(8,128)(2,1)}, bf16[128,512]{1,0:T(8,128)(2,1)S(1)}, u32[]{:S(2)}) copy-start(bf16[128,512]{1,0:T(8,128)(2,1)S(1)} %collective-permute-done.13.refs_8_.refs_17_) | copy-start | bytes 393220
  55.2 17.0 %copy-start.23 = (s32[2]{0:T(128)S(1)}, s32[2]{0:T(128)}, u32[]{:S(2)}) copy-start(s32[2]{0:T(128)} %copy-done.21) | copy-start | bytes 28
  62.5 16.0 %copy-start.19 = (bf16[128,512]{1,0:T(8,128)(2,1)}, bf16[128,512]{1,0:T(8,128)(2,1)S(1)}, u32[]{:S(2)}) copy-start(bf16[128,512]{1,0:T(8,128)(2,1)S(1)} %get-tuple-element.64.refs_1_) | copy-start | bytes 393220
  62.5 6.3 %collective-permute-start.14 = (bf16[128,512]{1,0:T(8,128)(2,1)S(1)}, bf16[128,512]{1,0:T(8,128)(2,1)S(1)}, u32[]{:S(2)}, u32[]{:S(2)}) collective-permute-start(bf16[128,512]{1,0:T(8,128)(2,1)S(1)} %get-tuple-element.65.refs_12_.refs_1_), channel_id=1, source_target_pairs={{0,2},{1,3},{2,0},{3,1},{4,6},{5,7},{6,4},{7,5},{8,10},{9,11},{10,... | collective-permute-start | bytes 393224 | tf_op jit(solution)/shard_map/ppermute | solution.py:73
  63.6 8.0 %collective-permute-start.15 = (bf16[128,512]{1,0:T(8,128)(2,1)S(1)}, bf16[128,512]{1,0:T(8,128)(2,1)S(1)}, u32[]{:S(2)}, u32[]{:S(2)}) collective-permute-start(bf16[128,512]{1,0:T(8,128)(2,1)S(1)} %get-tuple-element.65.refs_12_.refs_1_), channel_id=1, source_target_pairs={{0,4},{1,5},{2,6},{3,7},{4,0},{5,1},{6,2},{7,3},{8,12},{9,13},{10,... | collective-permute-start | bytes 393224 | tf_op jit(solution)/shard_map/ppermute | solution.py:73
  64.4 7.2 %collective-permute-start.16 = (bf16[128,512]{1,0:T(8,128)(2,1)S(1)}, bf16[128,512]{1,0:T(8,128)(2,1)S(1)}, u32[]{:S(2)}, u32[]{:S(2)}) collective-permute-start(bf16[128,512]{1,0:T(8,128)(2,1)S(1)} %get-tuple-element.65.refs_12_.refs_1_), channel_id=1, source_target_pairs={{0,6},{1,7},{2,4},{3,5},{4,2},{5,3},{6,0},{7,1},{8,14},{9,15},{10,... | collective-permute-start | bytes 393224 | tf_op jit(solution)/shard_map/ppermute | solution.py:73
  66.0 12.5 %collective-permute-start.17 = (bf16[128,512]{1,0:T(8,128)(2,1)S(1)}, bf16[128,512]{1,0:T(8,128)(2,1)S(1)}, u32[]{:S(2)}, u32[]{:S(2)}) collective-permute-start(bf16[128,512]{1,0:T(8,128)(2,1)S(1)} %get-tuple-element.65.refs_12_.refs_1_), channel_id=1, source_target_pairs={{0,1},{1,0},{2,3},{3,2},{4,5},{5,4},{6,7},{7,6},{8,9},{9,8},{10,11... | collective-permute-start | bytes 393224 | tf_op jit(solution)/shard_map/ppermute | solution.py:73
  68.8 9.7 %collective-permute-start.18 = (bf16[128,512]{1,0:T(8,128)(2,1)S(1)}, bf16[128,512]{1,0:T(8,128)(2,1)S(1)}, u32[]{:S(2)}, u32[]{:S(2)}) collective-permute-start(bf16[128,512]{1,0:T(8,128)(2,1)S(1)} %collective-permute-done.14.refs_2_), channel_id=1, source_target_pairs={{0,1},{1,0},{2,3},{3,2},{4,5},{5,4},{6,7},{7,6},{8,9},{9,8},{10,11... | collective-permute-start | bytes 393224 | tf_op jit(solution)/shard_map/ppermute | solution.py:73
  71.6 6.9 %collective-permute-start.19 = (bf16[128,512]{1,0:T(8,128)(2,1)S(1)}, bf16[128,512]{1,0:T(8,128)(2,1)S(1)}, u32[]{:S(2)}, u32[]{:S(2)}) collective-permute-start(bf16[128,512]{1,0:T(8,128)(2,1)S(1)} %collective-permute-done.15.refs_3_), channel_id=1, source_target_pairs={{0,1},{1,0},{2,3},{3,2},{4,5},{5,4},{6,7},{7,6},{8,9},{9,8},{10,11... | collective-permute-start | bytes 393224 | tf_op jit(solution)/shard_map/ppermute | solution.py:73
  71.6 6.9 %collective-permute-start.20 = (bf16[128,512]{1,0:T(8,128)(2,1)S(1)}, bf16[128,512]{1,0:T(8,128)(2,1)S(1)}, u32[]{:S(2)}, u32[]{:S(2)}) collective-permute-start(bf16[128,512]{1,0:T(8,128)(2,1)S(1)} %collective-permute-done.16.refs_4_), channel_id=1, source_target_pairs={{0,1},{1,0},{2,3},{3,2},{4,5},{5,4},{6,7},{7,6},{8,9},{9,8},{10,11... | collective-permute-start | bytes 393224 | tf_op jit(solution)/shard_map/ppermute | solution.py:73
  85.4 14.6 %all-to-all-start.4 = ((bf16[8,320,128]{2,1,0:T(8,128)(2,1)}), bf16[8,320,128]{2,1,0:T(8,128)(2,1)S(1)}, u32[]{:S(2)}, u32[]{:S(2)}) async-start(bf16[8,320,128]{2,1,0:T(8,128)(2,1)} %get-tuple-element.75), calls=%async_computation.4 | async-start | bytes 1310720 | tf_op jit(solution)/shard_map/all_to_all | solution.py:581
  100.0 2.8 %copy-start.27 = (bf16[8,320,128]{2,1,0:T(8,128)(2,1)}, bf16[8,320,128]{2,1,0:T(8,128)(2,1)S(1)}, u32[]{:S(2)}) copy-start(bf16[8,320,128]{2,1,0:T(8,128)(2,1)S(1)} %all-to-all-done.4.refs_1_) | copy-start | bytes 1966084
  100.0 37.1 %all-to-all-start.2 = ((bf16[32,56,128]{2,1,0:T(8,128)(2,1)}), bf16[32,56,128]{2,1,0:T(8,128)(2,1)S(1)}, u32[]{:S(2)}, u32[]{:S(2)}) async-start(bf16[32,56,128]{2,1,0:T(8,128)(2,1)} %bitcast.9), calls=%async_computation.2 | async-start | bytes 917504 | tf_op jit(solution)/shard_map/all_to_all | solution.py:602
  106.2 52.4 %copy-start.24 = (s32[2]{0:T(128)S(1)}, s32[2]{0:T(128)}, u32[]{:S(2)}) copy-start(s32[2]{0:T(128)} %copy-done.21) | copy-start | bytes 28
  106.2 6.9 %collective-permute-start.21 = (bf16[80,512]{1,0:T(8,128)(2,1)}, bf16[80,512]{1,0:T(8,128)(2,1)S(1)}, u32[]{:S(2)}, u32[]{:S(2)}) collective-permute-start(bf16[80,512]{1,0:T(8,128)(2,1)} %get-tuple-element.85), channel_id=1, source_target_pairs={{0,8},{8,0},{16,24},{24,16},{1,9},{9,1},{17,25},{25,17},{2,10},{10... | collective-permute-start | bytes 245768 | tf_op jit(solution)/shard_map/ppermute | solution.py:73
  107.8 14.2 %collective-permute-start.22 = (bf16[80,512]{1,0:T(8,128)(2,1)}, bf16[80,512]{1,0:T(8,128)(2,1)S(1)}, u32[]{:S(2)}, u32[]{:S(2)}) collective-permute-start(bf16[80,512]{1,0:T(8,128)(2,1)} %get-tuple-element.86), channel_id=1, source_target_pairs={{0,16},{8,24},{16,0},{24,8},{1,17},{9,25},{17,1},{25,9},{2,18},{10... | collective-permute-start | bytes 245768 | tf_op jit(solution)/shard_map/ppermute | solution.py:73
  110.3 11.7 %collective-permute-start.23 = (bf16[80,512]{1,0:T(8,128)(2,1)}, bf16[80,512]{1,0:T(8,128)(2,1)S(1)}, u32[]{:S(2)}, u32[]{:S(2)}) collective-permute-start(bf16[80,512]{1,0:T(8,128)(2,1)} %get-tuple-element.87), channel_id=1, source_target_pairs={{0,24},{8,16},{16,8},{24,0},{1,25},{9,17},{17,9},{25,1},{2,26},{10... | collective-permute-start | bytes 245768 | tf_op jit(solution)/shard_map/ppermute | solution.py:73
  123.0 4.6 %collective-permute-start.24 = (bf16[80,512]{1,0:T(8,128)(2,1)S(1)}, bf16[80,512]{1,0:T(8,128)(2,1)S(1)}, u32[]{:S(2)}, u32[]{:S(2)}) collective-permute-start(bf16[80,512]{1,0:T(8,128)(2,1)S(1)} %add_convert_fusion), channel_id=1, source_target_pairs={{0,8},{8,0},{16,24},{24,16},{1,9},{9,1},{17,25},{25,17},{2,10},{10... | collective-permute-start | bytes 245768 | tf_op jit(solution)/shard_map/ppermute | solution.py:73
  124.8 8.7 %collective-permute-start.25 = (bf16[80,512]{1,0:T(8,128)(2,1)S(1)}, bf16[80,512]{1,0:T(8,128)(2,1)S(1)}, u32[]{:S(2)}, u32[]{:S(2)}) collective-permute-start(bf16[80,512]{1,0:T(8,128)(2,1)S(1)} %add_convert_fusion), channel_id=1, source_target_pairs={{0,16},{8,24},{16,0},{24,8},{1,17},{9,25},{17,1},{25,9},{2,18},{10... | collective-permute-start | bytes 245768 | tf_op jit(solution)/shard_map/ppermute | solution.py:73
  124.8 8.7 %collective-permute-start.26 = (bf16[80,512]{1,0:T(8,128)(2,1)S(1)}, bf16[80,512]{1,0:T(8,128)(2,1)S(1)}, u32[]{:S(2)}, u32[]{:S(2)}) collective-permute-start(bf16[80,512]{1,0:T(8,128)(2,1)S(1)} %add_convert_fusion), channel_id=1, source_target_pairs={{0,24},{8,16},{16,8},{24,0},{1,25},{9,17},{17,9},{25,1},{2,26},{10... | collective-permute-start | bytes 245768 | tf_op jit(solution)/shard_map/ppermute | solution.py:73
  133.6 13.8 %collective-permute-start.27 = (bf16[320,512]{1,0:T(8,128)(2,1)S(1)}, bf16[320,512]{1,0:T(8,128)(2,1)S(1)}, u32[]{:S(2)}, u32[]{:S(2)}) collective-permute-start(bf16[320,512]{1,0:T(8,128)(2,1)S(1)} %pad_maximum_fusion.refs_1_), channel_id=1, source_target_pairs={{0,2},{1,3},{2,0},{3,1},{4,6},{5,7},{6,4},{7,5},{8,10},{9,11},{10,... | collective-permute-start | bytes 983048 | tf_op jit(solution)/shard_map/ppermute | solution.py:73
  135.1 14.9 %collective-permute-start.28 = (bf16[320,512]{1,0:T(8,128)(2,1)S(1)}, bf16[320,512]{1,0:T(8,128)(2,1)S(1)}, u32[]{:S(2)}, u32[]{:S(2)}) collective-permute-start(bf16[320,512]{1,0:T(8,128)(2,1)S(1)} %pad_maximum_fusion.refs_1_), channel_id=1, source_target_pairs={{0,4},{1,5},{2,6},{3,7},{4,0},{5,1},{6,2},{7,3},{8,12},{9,13},{10,... | collective-permute-start | bytes 983048 | tf_op jit(solution)/shard_map/ppermute | solution.py:73
  136.7 13.4 %collective-permute-start.29 = (bf16[320,512]{1,0:T(8,128)(2,1)S(1)}, bf16[320,512]{1,0:T(8,128)(2,1)S(1)}, u32[]{:S(2)}, u32[]{:S(2)}) collective-permute-start(bf16[320,512]{1,0:T(8,128)(2,1)S(1)} %pad_maximum_fusion.refs_1_), channel_id=1, source_target_pairs={{0,6},{1,7},{2,4},{3,5},{4,2},{5,3},{6,0},{7,1},{8,14},{9,15},{10,... | collective-permute-start | bytes 983048 | tf_op jit(solution)/shard_map/ppermute | solution.py:73
  143.3 12.3 %all-to-all-start.3 = ((bf16[32,4,512]{2,1,0:T(4,128)(2,1)}), bf16[32,4,512]{2,1,0:T(4,128)(2,1)S(1)}, u32[]{:S(2)}, u32[]{:S(2)}) async-start(bf16[32,4,512]{2,1,0:T(4,128)(2,1)} %broadcast_in_dim.10), calls=%async_computation.3 | async-start | bytes 262144 | tf_op jit(solution)/shard_map/all_to_all | solution.py:630
  155.6 1.9 %collective-permute-start.30 = (bf16[320,512]{1,0:T(8,128)(2,1)S(1)}, bf16[320,512]{1,0:T(8,128)(2,1)S(1)}, u32[]{:S(2)}, u32[]{:S(2)}) collective-permute-start(bf16[320,512]{1,0:T(8,128)(2,1)S(1)} %pad_maximum_fusion.refs_1_), channel_id=1, source_target_pairs={{0,1},{1,0},{2,3},{3,2},{4,5},{5,4},{6,7},{7,6},{8,9},{9,8},{10,11... | collective-permute-start | bytes 983048 | tf_op jit(solution)/shard_map/ppermute | solution.py:73
  155.8 1.9 %collective-permute-start.31 = (bf16[320,512]{1,0:T(8,128)(2,1)S(1)}, bf16[320,512]{1,0:T(8,128)(2,1)S(1)}, u32[]{:S(2)}, u32[]{:S(2)}) collective-permute-start(bf16[320,512]{1,0:T(8,128)(2,1)S(1)} %collective-permute-done.27.refs_2_), channel_id=1, source_target_pairs={{0,1},{1,0},{2,3},{3,2},{4,5},{5,4},{6,7},{7,6},{8,9},{9,8},{10,11... | collective-permute-start | bytes 983048 | tf_op jit(solution)/shard_map/ppermute | solution.py:73
  156.1 2.1 %collective-permute-start.32 = (bf16[320,512]{1,0:T(8,128)(2,1)S(1)}, bf16[320,512]{1,0:T(8,128)(2,1)S(1)}, u32[]{:S(2)}, u32[]{:S(2)}) collective-permute-start(bf16[320,512]{1,0:T(8,128)(2,1)S(1)} %collective-permute-done.28.refs_3_), channel_id=1, source_target_pairs={{0,1},{1,0},{2,3},{3,2},{4,5},{5,4},{6,7},{7,6},{8,9},{9,8},{10,11... | collective-permute-start | bytes 983048 | tf_op jit(solution)/shard_map/ppermute | solution.py:73
  156.3 2.3 %collective-permute-start.33 = (bf16[320,512]{1,0:T(8,128)(2,1)S(1)}, bf16[320,512]{1,0:T(8,128)(2,1)S(1)}, u32[]{:S(2)}, u32[]{:S(2)}) collective-permute-start(bf16[320,512]{1,0:T(8,128)(2,1)S(1)} %collective-permute-done.29.refs_4_), channel_id=1, source_target_pairs={{0,1},{1,0},{2,3},{3,2},{4,5},{5,4},{6,7},{7,6},{8,9},{9,8},{10,11... | collective-permute-start | bytes 983048 | tf_op jit(solution)/shard_map/ppermute | solution.py:73
  (8 other events, 7.0 us)

commit v2 on v1

--- a/solution.py
+++ b/solution.py
@@ -154,10 +154,12 @@
     return flags.astype(f32).astype(low)
 
 
-def request_kernel(here_ref, owner_ref, slot_ref, request_ref, rank_ref, column_ref):
-    tokens = owner_ref.shape[0]
+def request_kernel(here_ref, owner_ref, slot_ref, request_ref, rank_ref, column_ref, owners_ref):
+    tokens = owner_ref.shape[1]
     devices = request_ref.shape[0]
-    named = owner_ref[...] == lax.broadcasted_iota(jnp.int32, (tokens, devices), 1)
+    owners = as_column(owner_ref[...])
+    owners_ref[...] = owners
+    named = owners == lax.broadcasted_iota(jnp.int32, (tokens, devices), 1)
     row = lax.broadcasted_iota(jnp.int32, (tokens, tokens), 0)
     lower = selected(row > lax.broadcasted_iota(jnp.int32, (tokens, tokens), 1))
     earlier = dot(lower, selected(named))
@@ -221,9 +223,9 @@
 
 def forward_kernel(group, scale, head_size, *refs):
     here_ref, pieces = refs[0], refs[1 : 1 + group]
-    weight_ref, active_ref, hidden_ref, embedded_ref, mix_ref, cotangent_ref = refs[1 + group : 7 + group]
-    out_ref, delta_ref, gate_ref, early_ref, all_ref, normed_scr, mask_scr, att_scr = refs[7 + group :]
-    tokens, width = embedded_ref.shape
+    weight_ref, active_ref, hidden_ref, mix_ref, cotangent_ref = refs[1 + group : 6 + group]
+    gated_ref, delta_ref, gate_ref, early_ref, all_ref, normed_scr, mask_scr, att_scr = refs[6 + group :]
+    tokens, width = cotangent_ref.shape
     order = arrival_order(group)
     here = here_ref[0]
     for n in range(1, group):
@@ -254,11 +256,11 @@
         att_scr[:, tile(n)] = merge(masks, parts)
         return carry
 
-    lax.fori_loop(0, width // LANES, attend, 0)
+    lax.fori_loop(0, width // LANES, attend, 0, unroll=True)
     mixed, inverse_mix = layer_normalize(att_scr[...])
     gate = active_ref[:, :width].astype(f32)
     gated = (mixed * gate).astype(low)
-    out_ref[...] = (embedded_ref[...] + dot(gated, mix_ref[...])).astype(low)
+    gated_ref[...] = gated
     delta_gated = dot(cotangent_ref[...], mix_ref[...], (1, 1))
     delta_ref[...] = normalize_back(delta_gated * gate, mixed, inverse_mix).astype(low)
     gate_hidden = (delta_gated * mixed * silu_slope(hidden_ref[:, :width])).astype(low)
@@ -269,6 +271,10 @@
     for n in range(group):
         early_ref[n, 0:share] = gated_t[n * share : (n + 1) * share]
         early_ref[n, share : 2 * share] = hidden_t[n * share : (n + 1) * share]
+
+
+def out_kernel(here_ref, gated_ref, mix_ref, embedded_ref, out_ref):
+    out_ref[...] = (embedded_ref[...] + dot(gated_ref[...], mix_ref[...])).astype(low)
 
 
 def query_kernel(group, scale, head_size, *refs):
@@ -304,13 +310,14 @@
         out_ref[:, tile(n)] = (merge(masks, parts) * slope).astype(low)
         return carry
 
-    lax.fori_loop(0, width // LANES, step, 0)
+    lax.fori_loop(0, width // LANES, step, 0, unroll=True)
 
 
 def key_kernel(group, scale, head_size, *refs):
     here_ref, pieces = refs[0], refs[1 : 1 + group]
     active_ref, queries_ref, hidden_ref, query_ref, early_ref = refs[1 + group : 6 + group]
-    rest_ref, columns_ref, delta_scr, mask_scr = refs[6 + group :]
+    rest_ref, columns = refs[6 + group], refs[7 + group : 7 + 2 * group]
+    column_scr, delta_scr, mask_scr = refs[7 + 2 * group :]
     tokens, width = query_ref.shape
     for n in range(group):
         delta_scr[n * tokens : (n + 1) * tokens, :] = pieces[n][...]
@@ -338,13 +345,15 @@
             rest_ref[:, tile(n + at * tiles)] = (merge(masks, parts) * slope).astype(low)
         return carry
 
-    lax.fori_loop(0, tiles, step, 0)
+    lax.fori_loop(0, tiles, step, 0, unroll=True)
     rest_ref[:, width : 2 * width] = query_ref[...]
     late = rest_ref[...].astype(f32).T.astype(low)
     share = width // group
     for n in range(group):
-        columns_ref[n, : 2 * share] = early_ref[n]
-        columns_ref[n, 2 * share :] = late[3 * n * share : 3 * (n + 1) * share]
+        column_scr[n, : 2 * share] = early_ref[n]
+        column_scr[n, 2 * share :] = late[3 * n * share : 3 * (n + 1) * share]
+    for n, step in enumerate(arrival_order(group)):
+        columns[n][...] = column_scr[target_of(here_ref[0], step, group)]
 
 
 def row_kernel(head_rows, capacity, stride, *refs):
@@ -382,19 +391,18 @@
 
 
 def weight_kernel(group, count, *refs):
-    here_ref, moved_ref = refs[:2]
-    cotangents, normeds = refs[2 : 2 + group], refs[2 + group : 2 + 2 * group]
-    own_ref = refs[2 + 2 * group]
-    sends = refs[3 + 2 * group : 2 + 2 * group + count]
-    part_scr = refs[2 + 2 * group + count]
-    here, outer = here_ref[0], here_ref[1]
-    share = moved_ref.shape[1] // 5
+    here_ref, moved = refs[0], refs[1 : 1 + group]
+    cotangents, normeds = refs[1 + group : 1 + 2 * group], refs[1 + 2 * group : 1 + 3 * group]
+    own_ref = refs[1 + 3 * group]
+    sends = refs[2 + 3 * group : 1 + 3 * group + count]
+    part_scr = refs[1 + 3 * group + count]
+    outer = here_ref[1]
+    share = moved[0].shape[0] // 5
     chunk = own_ref.shape[0]
     top = bottom = None
-    for n, step in enumerate(arrival_order(group)):
-        source = source_of(here, step, group)
-        first = dot(moved_ref[source, :share], cotangents[n][...])
-        second = dot(moved_ref[source, share:], normeds[n][...])
+    for n in range(group):
+        first = dot(moved[n][:share], cotangents[n][...])
+        second = dot(moved[n][share:], normeds[n][...])
         top = first if n == 0 else top + first
         bottom = second if n == 0 else bottom + second
     total = jnp.concatenate([top, bottom], axis=0)
@@ -449,7 +457,7 @@
     hot_ref[...] = dot(asked_select(asked, capacity, 0, hot_count), rows, (0, 0))
     chosen = asked_select(asked, capacity, hot_count, cold_count)
     cold_ref[...] = dot(chosen, rows[:, :cold_width], (0, 0))
-    mine_ref[...] = jnp.concatenate(sums, axis=1).astype(low)
+    mine_ref[...] = jnp.broadcast_to(jnp.concatenate(sums, axis=1)[None], mine_ref.shape).astype(low)
 
 
 def assemble(position, pieces, norm_scale, width):
@@ -504,11 +512,12 @@
     stride = capacity + each
     while tiles * stride % 8:
         stride += 1
-    requests, rank, slot = call(
+    requests, rank, slot, owners = call(
         request_kernel,
-        [position, row_owner, slot_row[None, :]],
+        [position, row_owner.reshape(1, tokens), slot_row[None, :]],
         [
             shaped((devices, 1, LANES), jnp.int32),
+            shaped((tokens, 1), jnp.int32),
             shaped((tokens, 1), jnp.int32),
             shaped((tokens, 1), jnp.int32),
         ],
@@ -522,6 +531,7 @@
         functools.partial(pick_kernel, capacity),
         [position, asked, hot_table, cold_table],
         [shaped((devices * tiles * capacity, LANES), low)],
+        limit=56,
     )[0]
     rows_back = lax.all_to_all(
         picked.reshape(devices, tiles * capacity, LANES),
@@ -532,7 +542,7 @@
     ).reshape(picked.shape)
     vector, embedded, normed_low = call(
         functools.partial(embed_kernel, capacity, hot_count),
-        [position, row_owner, rank, slot, rows_back, cold_projection],
+        [position, owners, rank, slot, rows_back, cold_projection],
         [
             shaped((tokens, cold_width), low),
             shaped((tokens, width), f32),
@@ -550,9 +560,9 @@
     share = width // group
     work = 2 * tokens * length * width
     mask = pltpu.VMEM((tokens, length), f32)
-    layer_out, delta_attended, gate_hidden, early, everything = call(
+    gated, delta_attended, gate_hidden, early, everything = call(
         functools.partial(forward_kernel, group, score_scale, head_size),
-        [position, *normeds, joined_weight, active, hidden, embedded, output_weight, cotangent],
+        [position, *normeds, joined_weight, active, hidden, output_weight, cotangent],
         [
             shaped((tokens, width), low),
             shaped((tokens, width), low),
@@ -571,14 +581,16 @@
         3 * work,
     )
     deltas = gather_pieces(delta_attended, "cp")
-    rest_hidden, columns = call(
+    rest_hidden, *columns = call(
         functools.partial(key_kernel, group, score_scale, head_size),
         [position, *deltas, active, all_queries, hidden, query_hidden, early],
-        [shaped((tokens, 3 * width), low), shaped((group, 5 * share, tokens), low)],
-        [pltpu.VMEM((length, width), low), mask],
+        [shaped((tokens, 3 * width), low)] + [shaped((5 * share, tokens), low)] * group,
+        [pltpu.VMEM((group, 5 * share, tokens), low), pltpu.VMEM((length, width), low), mask],
         4 * work,
     )
-    moved = lax.all_to_all(columns, "cp", split_axis=0, concat_axis=0, tiled=True)
+    moved = columns[:1]
+    for step, block in zip(arrival_order(group)[1:], columns[1:]):
+        moved.append(exchange(block, "cp", step))
     sent = call(
         functools.partial(row_kernel, hot_count, capacity, stride),
         [
@@ -589,7 +601,7 @@
             embedded,
             cotangent,
             vector,
-            row_owner,
+            owners,
             rank,
             slot,
             cold_projection,
@@ -600,33 +612,41 @@
     )[0]
     sent = sent.reshape(devices, tiles * stride, LANES)
     arrived = lax.all_to_all(sent, everyone, split_axis=0, concat_axis=0, tiled=True)
+    layer_out = call(
+        out_kernel,
+        [position, gated, output_weight, embedded],
+        [shaped((tokens, width), low)],
+        limit=56,
+    )[0]
     count = lax.axis_size("dp")
     chunk = 5 * share // count
     own, *sends = call(
         functools.partial(weight_kernel, group, count),
-        [position, moved, *cotangents, *normeds],
+        [position, *moved, *cotangents, *normeds],
         [shaped((chunk, width), f32)] + [shaped((chunk, width), low)] * (count - 1),
         [pltpu.VMEM((count, chunk, width), f32)],
         10 * share * length * width,
         limit=56,
     )
     for step, block in enumerate(sends, start=1):
-        own = own + exchange(block, "dp", step).astype(f32)
+        block = exchange(block, "dp", step)
+        own = own + block.astype(f32)
     mine = own.astype(low)
-    line = [mine] + [exchange(mine, "dp", step) for step in range(1, count)]
+    line = [mine]
+    for step in range(1, count):
+        line.append(exchange(mine, "dp", step))
     line = jnp.concatenate(line, axis=0)
-    hot_gradient, cold_gradient, total = call(
+    hot_gradient, cold_gradient, copies = call(
         functools.partial(scatter_kernel, capacity, stride, each),
         [position, asked, arrived.reshape(devices * tiles * stride, LANES)],
         [
             shaped((hot_count, width), f32),
             shaped((cold_count, cold_width), f32),
-            shaped((each, width), low),
+            shaped((devices, each, width), low),
         ],
         flops=4 * devices * capacity * hot_count * width,
         limit=56,
     )
-    copies = jnp.broadcast_to(total[None], (devices, each, width))
     projection = lax.all_to_all(copies, everyone, split_axis=0, concat_axis=0, tiled=True)
     pieces = gather_pieces(line, "cp", (projection, hot_gradient, cold_gradient))
     norm_scale = (tokens * devices) ** (-0.5)

time: 164 us -> 161 us (0.982)
  waiting for transfers between devices: 54.7 us -> 51.1 us
  starting transfers between devices: 40.3 us -> 42.3 us
    ppermute x34 -> x41, starting transfers between devices: 27.3 us -> 33.9 us  [exchange(): return lax.ppermute(block, axis, pairs)]
    all_to_all x1 -> x0, waiting for transfers between devices: 6.16 us -> none  [local(): lax.all_to_all(columns, 'cp', split_axis=0, concat_axis=0, tiled=True)]
    ppermute x34 -> x41, waiting for transfers between devices: 32.1 us -> 37.4 us  [exchange(): return lax.ppermute(block, axis, pairs)]
    all_to_all x1 -> x0, starting transfers between devices: 3.54 us -> none  [local(): lax.all_to_all(columns, 'cp', split_axis=0, concat_axis=0, tiled=True)]
    all_to_all x1, waiting for transfers between devices: 5.51 us -> 2.81 us  [local(): lax.all_to_all(copies, everyone, split_axis=0, concat_axis=0, tiled=True)]
    unnamed x69 -> x76, local copies, waits for them, and re-layouts: 7.87 us -> 8.68 us
    pallas_call x11 -> x12, Pallas kernels: 42.4 us -> 42.4 us  [call(): pl.pallas_call(kernel, out_shape=outs, in_specs=[SMEM] * scalars + [VMEM]...]
  transfers between devices with their start and end apart: 38 -> 44, of which waited for: 15 -> 15; matrix products, arithmetic and copies ran while one was open for 2% -> 1% of each run, Pallas kernels for 13% -> 12%
where the time goes in v2:
time: 161 us
  waiting for transfers between devices  51.1 us (32%)
  Pallas kernels  42.4 us (26%)
  starting transfers between devices  42.3 us (26%)
  blocking collectives  13.3 us (8%)
  local copies, waits for them, and re-layouts  9.47 us (6%)
    pallas_call x12, Pallas kernels, call(): pl.pallas_call(kernel, out_shape=outs, in_specs=[SMEM] * scalars + [VMEM]...  42.4 us
    ppermute x41, waiting for transfers between devices, exchange(): return lax.ppermute(block, axis, pairs)  37.4 us
    ppermute x41, starting transfers between devices, exchange(): return lax.ppermute(block, axis, pairs)  33.9 us
    all_to_all x1, blocking collectives, local(): lax.all_to_all(requests, everyone, split_axis=0, concat_axis=0, tiled=True)  13.3 us
    all_to_all x1, waiting for transfers between devices, local(): lax.all_to_all(picked.reshape(devices, tiles * capacity, LANES), everyone...  10.9 us
    unnamed x76, local copies, waits for them, and re-layouts  8.68 us
  transfers between devices with their start and end apart: 44, of which 15 were waited for; matrix products, arithmetic and copies ran while one was open for 1% of the time, Pallas kernels for 12%

profile of v2, /device:TPU:0, one launch (start us, length us, event | category | flops | bytes accessed | tf_op | source)
XLA Modules:
  0.0 160.9 jit_solution(3444083536946062186)
XLA Ops:
  0.7 4.0 %collective-permute-start.2 = (bf16[128,512]{1,0:T(8,128)(2,1)}, bf16[128,512]{1,0:T(8,128)(2,1)S(1)}, u32[]{:S(2)}, u32[]{:S(2)}) collective-permute-start(bf16[128,512]{1,0:T(8,128)(2,1)} %refs_9_.4), channel_id=1, source_target_pairs={{0,6},{1,7},{2,4},{3,5},{4,2},{5,3},{6,0},{7,1},{8,14},{9,15},{10,... | collective-permute-start | bytes 393224 | tf_op jit(solution)/shard_map/ppermute | solution.py:73
  5.4 0.7 copy-done.25
  6.0 0.7 copy-done.26
  6.7 1.0 shard_map.127
  7.7 13.3 %all_to_all.20.asked_ref.refs_1_ = s32[32,1,128]{2,1,0:T(1,128)} all-to-all(s32[32,1,128]{2,1,0:T(1,128)S(1)} %get-tuple-element.61), channel_id=1, replica_groups=mesh['dp'=4,'cp'=8] {'dp','cp'}, dimensions={0} | all-to-all | bytes 32768 | tf_op jit(solution)/shard_map/all_to_all | solution.py:525
  21.1 0.6 copy-done.29
  21.7 0.7 copy-done.30
  22.4 3.4 %shard_map.128 = bf16[1280,128]{1,0:T(8,128)(2,1)} custom-call(s32[2]{0:T(128)} %copy-done.20, s32[32,1,128]{2,1,0:T(1,128)} %all_to_all.20.asked_ref.refs_1_, bf16[512,512]{1,0:T(8,128)(2,1)} %hot_ref.1, bf16[2048,128]{1,0:T(8,128)(2,1)} %cold_ref.1), custom_call_target="tpu_custom_call" | custom-call | bytes 1392648 | tf_op jit(solution)/shard_map/pallas_call | solution.py:96
  25.8 2.7 %all-to-all-start.1 = ((bf16[32,40,128]{2,1,0:T(8,128)(2,1)}), bf16[32,40,128]{2,1,0:T(8,128)(2,1)S(1)}, u32[]{:S(2)}, u32[]{:S(2)}) async-start(bf16[32,40,128]{2,1,0:T(8,128)(2,1)} %bitcast.12), calls=%async_computation.1 | async-start | bytes 655360 | tf_op jit(solution)/shard_map/all_to_all | solution.py:536
  29.6 10.9 %all-to-all-done.1 = bf16[32,40,128]{2,1,0:T(8,128)(2,1)S(1)} async-done(((bf16[32,40,128]{2,1,0:T(8,128)(2,1)}), bf16[32,40,128]{2,1,0:T(8,128)(2,1)S(1)}, u32[]{:S(2)}, u32[]{:S(2)}) %all-to-all-start.1) | async-done | bytes 327712 | tf_op jit(solution)/shard_map/all_to_all | solution.py:536
  40.6 0.6 copy-done.21
  41.2 1.4 shard_map.129
  42.6 0.7 copy-done.11
  43.3 0.6 copy-done.24
  43.9 1.2 collective-permute-start.9
  45.1 0.5 collective-permute-start.8
  45.6 1.8 %collective-permute-start.7 = (bf16[128,512]{1,0:T(8,128)(2,1)S(1)}, bf16[128,512]{1,0:T(8,128)(2,1)S(1)}, u32[]{:S(2)}, u32[]{:S(2)}) collective-permute-start(bf16[128,512]{1,0:T(8,128)(2,1)S(1)} %get-tuple-element.68.normed_ref.refs_1_.refs_17_), channel_id=1, source_target_pairs={{0,2},{1,3},{2,0},{3,1},{4,6},{5,7},{6,4},{7,5},{8,10},{9,11},{10,... | collective-permute-start | bytes 393224 | tf_op jit(solution)/shard_map/ppermute | solution.py:73
  47.5 3.7 %collective-permute-done.9.refs_4_.refs_20_ = bf16[128,512]{1,0:T(8,128)(2,1)S(1)} collective-permute-done((bf16[128,512]{1,0:T(8,128)(2,1)S(1)}, bf16[128,512]{1,0:T(8,128)(2,1)S(1)}, u32[]{:S(2)}, u32[]{:S(2)}) %collective-permute-start.9) | collective-permute-done | bytes 131104 | tf_op jit(solution)/shard_map/ppermute | solution.py:73
  51.2 1.4 collective-permute-done.8.refs_3_.refs_19_
  53.1 0.6 copy-done.22
  53.7 1.0 shard_map.130
  54.9 5.9 %shard_map.131 = (bf16[128,512]{1,0:T(8,128)(2,1)S(1)}, bf16[128,512]{1,0:T(8,128)(2,1)S(1)}, bf16[128,512]{1,0:T(8,128)(2,1)S(1)}, bf16[8,128,128]{2,1,0:T(8,128)(2,1)S(1)}, bf16[1024,1024]{1,0:T(8,128)(2,1)S(1)}) custom-call(s32[2]{0:T(128)S(1)} %copy-done.22, bf16[128,512]{1,0:T(8,128)(2,1)S(1)} %get-tuple-element.68.normed_ref.refs_1_.refs_17_, ...), custom_call_target="tpu_custom_call" | custom-call | flops 1342177280 | bytes 8126472 | tf_op jit(solution)/shard_map/pallas_call | solution.py:96
  60.8 0.6 copy-done.18
  61.5 1.3 collective-permute-start.16
  62.8 1.4 collective-permute-start.15
  64.2 0.8 collective-permute-start.14
  65.0 3.8 %collective-permute-done.16.refs_4_ = bf16[128,512]{1,0:T(8,128)(2,1)S(1)} collective-permute-done((bf16[128,512]{1,0:T(8,128)(2,1)S(1)}, bf16[128,512]{1,0:T(8,128)(2,1)S(1)}, u32[]{:S(2)}, u32[]{:S(2)}) %collective-permute-start.16) | collective-permute-done | bytes 131104 | tf_op jit(solution)/shard_map/ppermute | solution.py:73
  68.8 1.9 %collective-permute-done.15.refs_3_ = bf16[128,512]{1,0:T(8,128)(2,1)S(1)} collective-permute-done((bf16[128,512]{1,0:T(8,128)(2,1)S(1)}, bf16[128,512]{1,0:T(8,128)(2,1)S(1)}, u32[]{:S(2)}, u32[]{:S(2)}) %collective-permute-start.15) | collective-permute-done | bytes 131104 | tf_op jit(solution)/shard_map/ppermute | solution.py:73
  71.2 6.0 %shard_map.133 = (bf16[128,512]{1,0:T(8,128)(2,1)S(1)}, bf16[1024,512]{1,0:T(8,128)(2,1)S(1)}) custom-call(s32[2]{0:T(128)S(1)} %copy-done.22, bf16[128,512]{1,0:T(8,128)(2,1)S(1)} %get-tuple-element.68.normed_ref.refs_1_.refs_17_, bf16[128,512]{1,0:T(8,128)(2,1)S(1)} %collective-permute-done.7.refs_2_.refs_18_, ...), custom_call_target="tpu_custom_call" | custom-call | flops 402653184 | bytes 8126472 | tf_op jit(solution)/shard_map/pallas_call | solution.py:96
  77.3 4.9 %shard_map.134 = (bf16[128,1536]{1,0:T(8,128)(2,1)S(1)}, bf16[320,128]{1,0:T(8,128)(2,1)S(1)}, bf16[320,128]{1,0:T(8,128)(2,1)S(1)}, bf16[320,128]{1,0:T(8,128)(...) custom-call(s32[2]{0:T(128)S(1)} %copy-done.22, ...), custom_call_target="tpu_custom_call" | custom-call | flops 536870912 | bytes 5111816 | tf_op jit(solution)/shard_map/pallas_call | solution.py:96
  82.2 0.7 copy-done.13
  83.0 0.6 copy-done.19
  83.6 4.9 %shard_map.135 = bf16[1792,128]{1,0:T(8,128)(2,1)} custom-call(s32[2]{0:T(128)} %copy-done.20, bf16[128,512]{1,0:T(8,128)(2,1)} %copy-done.17, bf16[128,1536]{1,0:T(8,128)(2,1)} %copy-done.13, bf16[512,2048]{1,0:T(8,128)(2,1)} %refs_3_.1, f32[128,512]{1,0:T(8,128)} %copy-done.11, bf16[128,512]{1,0:T(8,128)(2,1)} %refs_9_.4, bf16[128,128]{1,0:T(8,128)(2,1)} %copy-done.24, ...), custom_call_target="tpu_custom_call" | custom-call | flops 268435456 | bytes 3638792 | tf_op jit(solution)/shard_map/pallas_call | solution.py:96
  88.5 2.8 %all-to-all-start.2 = ((bf16[32,56,128]{2,1,0:T(8,128)(2,1)}), bf16[32,56,128]{2,1,0:T(8,128)(2,1)S(1)}, u32[]{:S(2)}, u32[]{:S(2)}) async-start(bf16[32,56,128]{2,1,0:T(8,128)(2,1)} %bitcast.11), calls=%async_computation.2 | async-start | bytes 917504 | tf_op jit(solution)/shard_map/all_to_all | solution.py:614
  91.3 1.5 collective-permute-start.21
  92.8 1.5 collective-permute-start.22
  94.3 0.6 collective-permute-start.23
  94.9 1.6 collective-permute-start.25
  96.4 3.4 %collective-permute-done.21.refs_2_ = bf16[320,128]{1,0:T(8,128)(2,1)S(1)} collective-permute-done((bf16[320,128]{1,0:T(8,128)(2,1)S(1)}, bf16[320,128]{1,0:T(8,128)(2,1)S(1)}, u32[]{:S(2)}, u32[]{:S(2)}) %collective-permute-start.21) | collective-permute-done | bytes 81952 | tf_op jit(solution)/shard_map/ppermute | solution.py:73
  99.8 1.5 collective-permute-start.27
  101.3 1.8 %collective-permute-done.23.refs_4_ = bf16[320,128]{1,0:T(8,128)(2,1)S(1)} collective-permute-done((bf16[320,128]{1,0:T(8,128)(2,1)S(1)}, bf16[320,128]{1,0:T(8,128)(2,1)S(1)}, u32[]{:S(2)}, u32[]{:S(2)}) %collective-permute-start.23) | collective-permute-done | bytes 81952 | tf_op jit(solution)/shard_map/ppermute | solution.py:73
  103.1 4.0 %collective-permute-done.26.refs_7_ = bf16[320,128]{1,0:T(8,128)(2,1)S(1)} collective-permute-done((bf16[320,128]{1,0:T(8,128)(2,1)S(1)}, bf16[320,128]{1,0:T(8,128)(2,1)S(1)}, u32[]{:S(2)}, u32[]{:S(2)}) %collective-permute-start.26) | collective-permute-done | bytes 81952 | tf_op jit(solution)/shard_map/ppermute | solution.py:73
  107.2 0.6 copy-done.36
  107.8 3.4 %shard_map.137 = (f32[80,512]{1,0:T(8,128)}, bf16[80,512]{1,0:T(8,128)(2,1)}, bf16[80,512]{1,0:T(8,128)(2,1)}, bf16[80,512]{1,0:T(8,128)(2,1)}) custom-call(s32[2]{0:T(128)} %copy-done.20, bf16[320,128]{1,0:T(8,128)(2,1)} %copy-done.19, bf16[320,128]{1,0:T(8,128)(2,1)} %copy-done.31, bf16[320,128]{1,0:T(8,128)(2,1)} %copy-done.32, ...), custom_call_target="tpu_custom_call" | custom-call | flops 335544320 | bytes 3162120 | tf_op jit(solution)/shard_map/pallas_call | solution.py:96
  111.2 1.3 collective-permute-start.28
  112.4 1.5 collective-permute-start.29
  113.9 1.7 %collective-permute-start.30 = (bf16[80,512]{1,0:T(8,128)(2,1)}, bf16[80,512]{1,0:T(8,128)(2,1)S(1)}, u32[]{:S(2)}, u32[]{:S(2)}) collective-permute-start(bf16[80,512]{1,0:T(8,128)(2,1)} %get-tuple-element.103), channel_id=1, source_target_pairs={{0,24},{8,16},{16,8},{24,0},{1,25},{9,17},{17,9},{25,1},{2,26},{10... | collective-permute-start | bytes 245768 | tf_op jit(solution)/shard_map/ppermute | solution.py:73
  115.9 6.2 %collective-permute-done.29 = bf16[80,512]{1,0:T(8,128)(2,1)S(1)} collective-permute-done((bf16[80,512]{1,0:T(8,128)(2,1)}, bf16[80,512]{1,0:T(8,128)(2,1)S(1)}, u32[]{:S(2)}, u32[]{:S(2)}) %collective-permute-start.29) | collective-permute-done | bytes 81952 | tf_op jit(solution)/shard_map/ppermute | solution.py:73
  122.1 1.0 add_convert_fusion
  123.1 2.4 %collective-permute-start.33 = (bf16[80,512]{1,0:T(8,128)(2,1)S(1)}, bf16[80,512]{1,0:T(8,128)(2,1)S(1)}, u32[]{:S(2)}, u32[]{:S(2)}) collective-permute-start(bf16[80,512]{1,0:T(8,128)(2,1)S(1)} %add_convert_fusion), channel_id=1, source_target_pairs={{0,24},{8,16},{16,8},{24,0},{1,25},{9,17},{17,9},{25,1},{2,26},{10... | collective-permute-start | bytes 245768 | tf_op jit(solution)/shard_map/ppermute | solution.py:73
  125.4 0.7 collective-permute-start.32
  126.1 1.4 collective-permute-start.31
  127.5 2.8 %collective-permute-done.33 = bf16[80,512]{1,0:T(8,128)(2,1)S(1)} collective-permute-done((bf16[80,512]{1,0:T(8,128)(2,1)S(1)}, bf16[80,512]{1,0:T(8,128)(2,1)S(1)}, u32[]{:S(2)}, u32[]{:S(2)}) %collective-permute-start.33) | collective-permute-done | bytes 81952 | tf_op jit(solution)/shard_map/ppermute | solution.py:73
  130.3 2.7 %collective-permute-done.32 = bf16[80,512]{1,0:T(8,128)(2,1)S(1)} collective-permute-done((bf16[80,512]{1,0:T(8,128)(2,1)S(1)}, bf16[80,512]{1,0:T(8,128)(2,1)S(1)}, u32[]{:S(2)}, u32[]{:S(2)}) %collective-permute-start.32) | collective-permute-done | bytes 81952 | tf_op jit(solution)/shard_map/ppermute | solution.py:73
  133.1 1.4 collective-permute-start.35
  134.6 2.0 %collective-permute-start.34 = (bf16[320,512]{1,0:T(8,128)(2,1)S(1)}, bf16[320,512]{1,0:T(8,128)(2,1)S(1)}, u32[]{:S(2)}, u32[]{:S(2)}) collective-permute-start(bf16[320,512]{1,0:T(8,128)(2,1)S(1)} %pad_maximum_fusion.refs_1_), channel_id=1, source_target_pairs={{0,2},{1,3},{2,0},{3,1},{4,6},{5,7},{6,4},{7,5},{8,10},{9,11},{10,... | collective-permute-start | bytes 983048 | tf_op jit(solution)/shard_map/ppermute | solution.py:73
  136.6 0.8 copy-done.27
  137.4 4.1 %shard_map.136 = (f32[512,512]{1,0:T(8,128)}, f32[2048,128]{1,0:T(8,128)}, bf16[32,4,512]{2,1,0:T(4,128)(2,1)}) custom-call(s32[2]{0:T(128)} %copy-done.20, s32[32,1,128]{2,1,0:T(1,128)} %all_to_all.20.asked_ref.refs_1_, bf16[1792,128]{1,0:T(8,128)(2,1)} %bitcast.13), custom_call_target="tpu_custom_call" | custom-call | flops 335544320 | bytes 2703368 | tf_op jit(solution)/shard_map/pallas_call | solution.py:96
  141.4 2.9 %all-to-all-start.3 = ((bf16[32,4,512]{2,1,0:T(4,128)(2,1)}), bf16[32,4,512]{2,1,0:T(4,128)(2,1)S(1)}, u32[]{:S(2)}, u32[]{:S(2)}) async-start(bf16[32,4,512]{2,1,0:T(4,128)(2,1)} %get-tuple-element.83), calls=%async_computation.3 | async-start | bytes 262144 | tf_op jit(solution)/shard_map/all_to_all | solution.py:650
  144.6 5.1 %collective-permute-done.35.refs_3_ = bf16[320,512]{1,0:T(8,128)(2,1)S(1)} collective-permute-done((bf16[320,512]{1,0:T(8,128)(2,1)S(1)}, bf16[320,512]{1,0:T(8,128)(2,1)S(1)}, u32[]{:S(2)}, u32[]{:S(2)}) %collective-permute-start.35) | collective-permute-done | bytes 327712 | tf_op jit(solution)/shard_map/ppermute | solution.py:73
  149.7 2.8 %all-to-all-done.3 = bf16[32,4,512]{2,1,0:T(4,128)(2,1)S(1)} async-done(((bf16[32,4,512]{2,1,0:T(4,128)(2,1)}), bf16[32,4,512]{2,1,0:T(4,128)(2,1)S(1)}, u32[]{:S(2)}, u32[]{:S(2)}) %all-to-all-start.3) | async-done | bytes 131104 | tf_op jit(solution)/shard_map/all_to_all | solution.py:650
  153.6 2.0 %shard_map.132 = bf16[128,512]{1,0:T(8,128)(2,1)} custom-call(s32[2]{0:T(128)} %copy-done.20, bf16[128,512]{1,0:T(8,128)(2,1)} %copy-done.18, bf16[512,512]{1,0:T(8,128)(2,1)} %mix_ref.1, f32[128,512]{1,0:T(8,128)} %copy-done.11), custom_call_target="tpu_custom_call" | custom-call | bytes 1048584 | tf_op jit(solution)/shard_map/pallas_call | solution.py:96
  155.7 0.8 mul.11
  156.5 4.4 %shard_map.138 = (f32[512,2048]{1,0:T(8,128)}, f32[512,512]{1,0:T(8,128)}) custom-call(s32[2]{0:T(128)S(1)} %copy-done.23, bf16[320,512]{1,0:T(8,128)(2,1)S(1)} %pad_maximum_fusion.refs_1_, bf16[320,512]{1,0:T(8,128)(2,1)S(1)} %collective-permute-done.34.refs_2_, bf16[320,512]{1,0:T(8,128)(2,1)S(1)} %collective-permute-done.35.refs_3_, ...), custom_call_target="tpu_custom_call" | custom-call | bytes 7864328 | tf_op jit(solution)/shard_map/pallas_call | solution.py:96
  (118 shorter events, 4.8 us)
Async XLA Ops:
  0.6 27.9 %copy-start.3 = (bf16[128,512]{1,0:T(8,128)(2,1)S(1)}, bf16[128,512]{1,0:T(8,128)(2,1)}, u32[]{:S(2)}) copy-start(bf16[128,512]{1,0:T(8,128)(2,1)} %refs_9_.4) | copy-start | bytes 393220
  0.6 39.9 %copy-start.12 = (bf16[128,512]{1,0:T(8,128)(2,1)S(1)}, bf16[128,512]{1,0:T(8,128)(2,1)}, u32[]{:S(2)}) copy-start(bf16[128,512]{1,0:T(8,128)(2,1)} %refs_10_.1) | copy-start | bytes 393220
  0.7 52.4 %copy-start = (bf16[512,2048]{1,0:T(8,128)(2,1)S(1)}, bf16[512,2048]{1,0:T(8,128)(2,1)}, u32[]{:S(2)}) copy-start(bf16[512,2048]{1,0:T(8,128)(2,1)} %refs_3_.1) | copy-start | bytes 6291460
  0.7 20.4 %collective-permute-start.2 = (bf16[128,512]{1,0:T(8,128)(2,1)}, bf16[128,512]{1,0:T(8,128)(2,1)S(1)}, u32[]{:S(2)}, u32[]{:S(2)}) collective-permute-start(bf16[128,512]{1,0:T(8,128)(2,1)} %refs_9_.4), channel_id=1, source_target_pairs={{0,6},{1,7},{2,4},{3,5},{4,2},{5,3},{6,0},{7,1},{8,14},{9,15},{10,... | collective-permute-start | bytes 393224 | tf_op jit(solution)/shard_map/ppermute | solution.py:73
  4.7 16.4 %collective-permute-start.1 = (bf16[128,512]{1,0:T(8,128)(2,1)}, bf16[128,512]{1,0:T(8,128)(2,1)S(1)}, u32[]{:S(2)}, u32[]{:S(2)}) collective-permute-start(bf16[128,512]{1,0:T(8,128)(2,1)} %refs_9_.4), channel_id=1, source_target_pairs={{0,4},{1,5},{2,6},{3,7},{4,0},{5,1},{6,2},{7,3},{8,12},{9,13},{10,... | collective-permute-start | bytes 393224 | tf_op jit(solution)/shard_map/ppermute | solution.py:73
  5.2 15.9 %collective-permute-start = (bf16[128,512]{1,0:T(8,128)(2,1)}, bf16[128,512]{1,0:T(8,128)(2,1)S(1)}, u32[]{:S(2)}, u32[]{:S(2)}) collective-permute-start(bf16[128,512]{1,0:T(8,128)(2,1)} %refs_9_.4), channel_id=1, source_target_pairs={{0,2},{1,3},{2,0},{3,1},{4,6},{5,7},{6,4},{7,5},{8,10},{9,11},{10,... | collective-permute-start | bytes 393224 | tf_op jit(solution)/shard_map/ppermute | solution.py:73
  5.4 15.7 %copy-start.20 = (s32[2]{0:T(128)}, s32[2]{0:T(128)S(1)}, u32[]{:S(2)}) copy-start(s32[2]{0:T(128)S(1)} %pad_add_fusion.here_ref.refs_0_) | copy-start | bytes 28
  7.7 37.9 %copy-start.15 = (s32[128,1]{1,0:T(8,128)}, s32[128,1]{1,0:T(8,128)S(1)}, u32[]{:S(2)}) copy-start(s32[128,1]{1,0:T(8,128)S(1)} %get-tuple-element.60.refs_3_.refs_9_) | copy-start | bytes 1540
  7.7 37.9 %copy-start.16 = (s32[128,1]{1,0:T(8,128)}, s32[128,1]{1,0:T(8,128)S(1)}, u32[]{:S(2)}) copy-start(s32[128,1]{1,0:T(8,128)S(1)} %get-tuple-element.58.refs_1_.refs_7_) | copy-start | bytes 1540
  7.7 47.1 %copy-start.14 = (s32[128,1]{1,0:T(8,128)}, s32[128,1]{1,0:T(8,128)S(1)}, u32[]{:S(2)}) copy-start(s32[128,1]{1,0:T(8,128)S(1)} %get-tuple-element.59.refs_2_.refs_8_) | copy-start | bytes 1540
  21.1 33.7 %copy-start.28 = (bf16[128,512]{1,0:T(8,128)(2,1)}, bf16[128,512]{1,0:T(8,128)(2,1)S(1)}, u32[]{:S(2)}) copy-start(bf16[128,512]{1,0:T(8,128)(2,1)S(1)} %collective-permute-done.2.refs_12_) | copy-start | bytes 393220
  25.8 29.1 %copy-start.2 = (bf16[512,512]{1,0:T(8,128)(2,1)S(1)}, bf16[512,512]{1,0:T(8,128)(2,1)}, u32[]{:S(2)}) copy-start(bf16[512,512]{1,0:T(8,128)(2,1)} %mix_ref.1) | copy-start | bytes 1572868
  25.8 14.8 %all-to-all-start.1 = ((bf16[32,40,128]{2,1,0:T(8,128)(2,1)}), bf16[32,40,128]{2,1,0:T(8,128)(2,1)S(1)}, u32[]{:S(2)}, u32[]{:S(2)}) async-start(bf16[32,40,128]{2,1,0:T(8,128)(2,1)} %bitcast.12), calls=%async_computation.1 | async-start | bytes 655360 | tf_op jit(solution)/shard_map/all_to_all | solution.py:536
  28.5 15.4 %collective-permute-start.3 = (bf16[128,512]{1,0:T(8,128)(2,1)S(1)}, bf16[128,512]{1,0:T(8,128)(2,1)}, u32[]{:S(2)}, u32[]{:S(2)}) collective-permute-start(bf16[128,512]{1,0:T(8,128)(2,1)S(1)} %copy-done.3), channel_id=1, source_target_pairs={{0,1},{1,0},{2,3},{3,2},{4,5},{5,4},{6,7},{7,6},{8,9},{9,8},{10,11... | collective-permute-start | bytes 393224 | tf_op jit(solution)/shard_map/ppermute | solution.py:73
  28.7 15.2 %collective-permute-start.6 = (bf16[128,512]{1,0:T(8,128)(2,1)S(1)}, bf16[128,512]{1,0:T(8,128)(2,1)}, u32[]{:S(2)}, u32[]{:S(2)}) collective-permute-start(bf16[128,512]{1,0:T(8,128)(2,1)S(1)} %collective-permute-done.2.refs_12_), channel_id=1, source_target_pairs={{0,1},{1,0},{2,3},{3,2},{4,5},{5,4},{6,7},{7,6},{8,9},{9,8},{10,11... | collective-permute-start | bytes 393224 | tf_op jit(solution)/shard_map/ppermute | solution.py:73
  29.1 14.8 %collective-permute-start.5 = (bf16[128,512]{1,0:T(8,128)(2,1)}, bf16[128,512]{1,0:T(8,128)(2,1)}, u32[]{:S(2)}, u32[]{:S(2)}) collective-permute-start(bf16[128,512]{1,0:T(8,128)(2,1)} %copy-done.29), channel_id=1, source_target_pairs={{0,1},{1,0},{2,3},{3,2},{4,5},{5,4},{6,7},{7,6},{8,9},{9,8},{10,11... | collective-permute-start | bytes 393224 | tf_op jit(solution)/shard_map/ppermute | solution.py:73
  29.2 14.7 %collective-permute-start.4 = (bf16[128,512]{1,0:T(8,128)(2,1)}, bf16[128,512]{1,0:T(8,128)(2,1)}, u32[]{:S(2)}, u32[]{:S(2)}) collective-permute-start(bf16[128,512]{1,0:T(8,128)(2,1)} %copy-done.30), channel_id=1, source_target_pairs={{0,1},{1,0},{2,3},{3,2},{4,5},{5,4},{6,7},{7,6},{8,9},{9,8},{10,11... | collective-permute-start | bytes 393224 | tf_op jit(solution)/shard_map/ppermute | solution.py:73
  43.9 27.3 %copy-start.1 = (bf16[128,512]{1,0:T(8,128)(2,1)}, bf16[128,512]{1,0:T(8,128)(2,1)S(1)}, u32[]{:S(2)}) copy-start(bf16[128,512]{1,0:T(8,128)(2,1)S(1)} %get-tuple-element.68.normed_ref.refs_1_.refs_17_) | copy-start | bytes 393220
  43.9 7.2 %collective-permute-start.9 = (bf16[128,512]{1,0:T(8,128)(2,1)S(1)}, bf16[128,512]{1,0:T(8,128)(2,1)S(1)}, u32[]{:S(2)}, u32[]{:S(2)}) collective-permute-start(bf16[128,512]{1,0:T(8,128)(2,1)S(1)} %get-tuple-element.68.normed_ref.refs_1_.refs_17_), channel_id=1, source_target_pairs={{0,6},{1,7},{2,4},{3,5},{4,2},{5,3},{6,0},{7,1},{8,14},{9,15},{10,... | collective-permute-start | bytes 393224 | tf_op jit(solution)/shard_map/ppermute | solution.py:73
  45.1 7.5 %collective-permute-start.8 = (bf16[128,512]{1,0:T(8,128)(2,1)S(1)}, bf16[128,512]{1,0:T(8,128)(2,1)S(1)}, u32[]{:S(2)}, u32[]{:S(2)}) collective-permute-start(bf16[128,512]{1,0:T(8,128)(2,1)S(1)} %get-tuple-element.68.normed_ref.refs_1_.refs_17_), channel_id=1, source_target_pairs={{0,4},{1,5},{2,6},{3,7},{4,0},{5,1},{6,2},{7,3},{8,12},{9,13},{10,... | collective-permute-start | bytes 393224 | tf_op jit(solution)/shard_map/ppermute | solution.py:73
  45.6 6.9 %collective-permute-start.7 = (bf16[128,512]{1,0:T(8,128)(2,1)S(1)}, bf16[128,512]{1,0:T(8,128)(2,1)S(1)}, u32[]{:S(2)}, u32[]{:S(2)}) collective-permute-start(bf16[128,512]{1,0:T(8,128)(2,1)S(1)} %get-tuple-element.68.normed_ref.refs_1_.refs_17_), channel_id=1, source_target_pairs={{0,2},{1,3},{2,0},{3,1},{4,6},{5,7},{6,4},{7,5},{8,10},{9,11},{10,... | collective-permute-start | bytes 393224 | tf_op jit(solution)/shard_map/ppermute | solution.py:73
  47.5 7.3 %collective-permute-start.10 = (bf16[128,512]{1,0:T(8,128)(2,1)S(1)}, bf16[128,512]{1,0:T(8,128)(2,1)S(1)}, u32[]{:S(2)}, u32[]{:S(2)}) collective-permute-start(bf16[128,512]{1,0:T(8,128)(2,1)S(1)} %get-tuple-element.68.normed_ref.refs_1_.refs_17_), channel_id=1, source_target_pairs={{0,1},{1,0},{2,3},{3,2},{4,5},{5,4},{6,7},{7,6},{8,9},{9,8},{10,11... | collective-permute-start | bytes 393224 | tf_op jit(solution)/shard_map/ppermute | solution.py:73
  51.2 20.0 %copy-start.4 = (bf16[128,512]{1,0:T(8,128)(2,1)}, bf16[128,512]{1,0:T(8,128)(2,1)S(1)}, u32[]{:S(2)}) copy-start(bf16[128,512]{1,0:T(8,128)(2,1)S(1)} %collective-permute-done.9.refs_4_.refs_20_) | copy-start | bytes 393220
  51.2 3.6 %collective-permute-start.13 = (bf16[128,512]{1,0:T(8,128)(2,1)S(1)}, bf16[128,512]{1,0:T(8,128)(2,1)S(1)}, u32[]{:S(2)}, u32[]{:S(2)}) collective-permute-start(bf16[128,512]{1,0:T(8,128)(2,1)S(1)} %collective-permute-done.9.refs_4_.refs_20_), channel_id=1, source_target_pairs={{0,1},{1,0},{2,3},{3,2},{4,5},{5,4},{6,7},{7,6},{8,9},{9,8},{10,11... | collective-permute-start | bytes 393224 | tf_op jit(solution)/shard_map/ppermute | solution.py:73
  52.6 18.6 %copy-start.5 = (bf16[128,512]{1,0:T(8,128)(2,1)}, bf16[128,512]{1,0:T(8,128)(2,1)S(1)}, u32[]{:S(2)}) copy-start(bf16[128,512]{1,0:T(8,128)(2,1)S(1)} %collective-permute-done.8.refs_3_.refs_19_) | copy-start | bytes 393220
  52.6 2.3 %collective-permute-start.12 = (bf16[128,512]{1,0:T(8,128)(2,1)S(1)}, bf16[128,512]{1,0:T(8,128)(2,1)S(1)}, u32[]{:S(2)}, u32[]{:S(2)}) collective-permute-start(bf16[128,512]{1,0:T(8,128)(2,1)S(1)} %collective-permute-done.8.refs_3_.refs_19_), channel_id=1, source_target_pairs={{0,1},{1,0},{2,3},{3,2},{4,5},{5,4},{6,7},{7,6},{8,9},{9,8},{10,11... | collective-permute-start | bytes 393224 | tf_op jit(solution)/shard_map/ppermute | solution.py:73
  52.6 18.6 %copy-start.6 = (bf16[128,512]{1,0:T(8,128)(2,1)}, bf16[128,512]{1,0:T(8,128)(2,1)S(1)}, u32[]{:S(2)}) copy-start(bf16[128,512]{1,0:T(8,128)(2,1)S(1)} %collective-permute-done.7.refs_2_.refs_18_) | copy-start | bytes 393220
  52.6 2.3 %collective-permute-start.11 = (bf16[128,512]{1,0:T(8,128)(2,1)S(1)}, bf16[128,512]{1,0:T(8,128)(2,1)S(1)}, u32[]{:S(2)}, u32[]{:S(2)}) collective-permute-start(bf16[128,512]{1,0:T(8,128)(2,1)S(1)} %collective-permute-done.7.refs_2_.refs_18_), channel_id=1, source_target_pairs={{0,1},{1,0},{2,3},{3,2},{4,5},{5,4},{6,7},{7,6},{8,9},{9,8},{10,11... | collective-permute-start | bytes 393224 | tf_op jit(solution)/shard_map/ppermute | solution.py:73
  54.8 16.4 %copy-start.7 = (bf16[128,512]{1,0:T(8,128)(2,1)}, bf16[128,512]{1,0:T(8,128)(2,1)S(1)}, u32[]{:S(2)}) copy-start(bf16[128,512]{1,0:T(8,128)(2,1)S(1)} %collective-permute-done.10.refs_5_.refs_21_) | copy-start | bytes 393220
  54.8 16.4 %copy-start.8 = (bf16[128,512]{1,0:T(8,128)(2,1)}, bf16[128,512]{1,0:T(8,128)(2,1)S(1)}, u32[]{:S(2)}) copy-start(bf16[128,512]{1,0:T(8,128)(2,1)S(1)} %collective-permute-done.13.refs_8_.refs_24_) | copy-start | bytes 393220
  54.8 16.4 %copy-start.9 = (bf16[128,512]{1,0:T(8,128)(2,1)}, bf16[128,512]{1,0:T(8,128)(2,1)S(1)}, u32[]{:S(2)}) copy-start(bf16[128,512]{1,0:T(8,128)(2,1)S(1)} %collective-permute-done.12.refs_7_.refs_23_) | copy-start | bytes 393220
  54.9 16.4 %copy-start.10 = (bf16[128,512]{1,0:T(8,128)(2,1)}, bf16[128,512]{1,0:T(8,128)(2,1)S(1)}, u32[]{:S(2)}) copy-start(bf16[128,512]{1,0:T(8,128)(2,1)S(1)} %collective-permute-done.11.refs_6_.refs_22_) | copy-start | bytes 393220
  61.5 15.8 %copy-start.17 = (bf16[128,512]{1,0:T(8,128)(2,1)}, bf16[128,512]{1,0:T(8,128)(2,1)S(1)}, u32[]{:S(2)}) copy-start(bf16[128,512]{1,0:T(8,128)(2,1)S(1)} %get-tuple-element.73.refs_1_) | copy-start | bytes 393220
  61.5 7.3 %collective-permute-start.16 = (bf16[128,512]{1,0:T(8,128)(2,1)S(1)}, bf16[128,512]{1,0:T(8,128)(2,1)S(1)}, u32[]{:S(2)}, u32[]{:S(2)}) collective-permute-start(bf16[128,512]{1,0:T(8,128)(2,1)S(1)} %get-tuple-element.74.refs_12_.refs_1_), channel_id=1, source_target_pairs={{0,6},{1,7},{2,4},{3,5},{4,2},{5,3},{6,0},{7,1},{8,14},{9,15},{10,... | collective-permute-start | bytes 393224 | tf_op jit(solution)/shard_map/ppermute | solution.py:73
  62.8 7.9 %collective-permute-start.15 = (bf16[128,512]{1,0:T(8,128)(2,1)S(1)}, bf16[128,512]{1,0:T(8,128)(2,1)S(1)}, u32[]{:S(2)}, u32[]{:S(2)}) collective-permute-start(bf16[128,512]{1,0:T(8,128)(2,1)S(1)} %get-tuple-element.74.refs_12_.refs_1_), channel_id=1, source_target_pairs={{0,4},{1,5},{2,6},{3,7},{4,0},{5,1},{6,2},{7,3},{8,12},{9,13},{10,... | collective-permute-start | bytes 393224 | tf_op jit(solution)/shard_map/ppermute | solution.py:73
  64.2 6.5 %collective-permute-start.14 = (bf16[128,512]{1,0:T(8,128)(2,1)S(1)}, bf16[128,512]{1,0:T(8,128)(2,1)S(1)}, u32[]{:S(2)}, u32[]{:S(2)}) collective-permute-start(bf16[128,512]{1,0:T(8,128)(2,1)S(1)} %get-tuple-element.74.refs_12_.refs_1_), channel_id=1, source_target_pairs={{0,2},{1,3},{2,0},{3,1},{4,6},{5,7},{6,4},{7,5},{8,10},{9,11},{10,... | collective-permute-start | bytes 393224 | tf_op jit(solution)/shard_map/ppermute | solution.py:73
  65.0 12.3 %collective-permute-start.17 = (bf16[128,512]{1,0:T(8,128)(2,1)S(1)}, bf16[128,512]{1,0:T(8,128)(2,1)S(1)}, u32[]{:S(2)}, u32[]{:S(2)}) collective-permute-start(bf16[128,512]{1,0:T(8,128)(2,1)S(1)} %get-tuple-element.74.refs_12_.refs_1_), channel_id=1, source_target_pairs={{0,1},{1,0},{2,3},{3,2},{4,5},{5,4},{6,7},{7,6},{8,9},{9,8},{10,11... | collective-permute-start | bytes 393224 | tf_op jit(solution)/shard_map/ppermute | solution.py:73
  68.8 8.5 %collective-permute-start.20 = (bf16[128,512]{1,0:T(8,128)(2,1)S(1)}, bf16[128,512]{1,0:T(8,128)(2,1)S(1)}, u32[]{:S(2)}, u32[]{:S(2)}) collective-permute-start(bf16[128,512]{1,0:T(8,128)(2,1)S(1)} %collective-permute-done.16.refs_4_), channel_id=1, source_target_pairs={{0,1},{1,0},{2,3},{3,2},{4,5},{5,4},{6,7},{7,6},{8,9},{9,8},{10,11... | collective-permute-start | bytes 393224 | tf_op jit(solution)/shard_map/ppermute | solution.py:73
  70.7 6.6 %collective-permute-start.19 = (bf16[128,512]{1,0:T(8,128)(2,1)S(1)}, bf16[128,512]{1,0:T(8,128)(2,1)S(1)}, u32[]{:S(2)}, u32[]{:S(2)}) collective-permute-start(bf16[128,512]{1,0:T(8,128)(2,1)S(1)} %collective-permute-done.15.refs_3_), channel_id=1, source_target_pairs={{0,1},{1,0},{2,3},{3,2},{4,5},{5,4},{6,7},{7,6},{8,9},{9,8},{10,11... | collective-permute-start | bytes 393224 | tf_op jit(solution)/shard_map/ppermute | solution.py:73
  70.7 6.6 %collective-permute-start.18 = (bf16[128,512]{1,0:T(8,128)(2,1)S(1)}, bf16[128,512]{1,0:T(8,128)(2,1)S(1)}, u32[]{:S(2)}, u32[]{:S(2)}) collective-permute-start(bf16[128,512]{1,0:T(8,128)(2,1)S(1)} %collective-permute-done.14.refs_2_), channel_id=1, source_target_pairs={{0,1},{1,0},{2,3},{3,2},{4,5},{5,4},{6,7},{7,6},{8,9},{9,8},{10,11... | collective-permute-start | bytes 393224 | tf_op jit(solution)/shard_map/ppermute | solution.py:73
  88.5 48.1 %all-to-all-start.2 = ((bf16[32,56,128]{2,1,0:T(8,128)(2,1)}), bf16[32,56,128]{2,1,0:T(8,128)(2,1)S(1)}, u32[]{:S(2)}, u32[]{:S(2)}) async-start(bf16[32,56,128]{2,1,0:T(8,128)(2,1)} %bitcast.11), calls=%async_computation.2 | async-start | bytes 917504 | tf_op jit(solution)/shard_map/all_to_all | solution.py:614
  91.3 8.5 %collective-permute-start.21 = (bf16[320,128]{1,0:T(8,128)(2,1)S(1)}, bf16[320,128]{1,0:T(8,128)(2,1)S(1)}, u32[]{:S(2)}, u32[]{:S(2)}) collective-permute-start(bf16[320,128]{1,0:T(8,128)(2,1)S(1)} %get-tuple-element.85), channel_id=1, source_target_pairs={{0,2},{1,3},{2,0},{3,1},{4,6},{5,7},{6,4},{7,5},{8,10},{9,11},{10,... | collective-permute-start | bytes 245768 | tf_op jit(solution)/shard_map/ppermute | solution.py:73
  92.8 7.0 %collective-permute-start.22 = (bf16[320,128]{1,0:T(8,128)(2,1)S(1)}, bf16[320,128]{1,0:T(8,128)(2,1)S(1)}, u32[]{:S(2)}, u32[]{:S(2)}) collective-permute-start(bf16[320,128]{1,0:T(8,128)(2,1)S(1)} %get-tuple-element.86), channel_id=1, source_target_pairs={{0,4},{1,5},{2,6},{3,7},{4,0},{5,1},{6,2},{7,3},{8,12},{9,13},{10,... | collective-permute-start | bytes 245768 | tf_op jit(solution)/shard_map/ppermute | solution.py:73
  94.3 8.8 %collective-permute-start.23 = (bf16[320,128]{1,0:T(8,128)(2,1)S(1)}, bf16[320,128]{1,0:T(8,128)(2,1)S(1)}, u32[]{:S(2)}, u32[]{:S(2)}) collective-permute-start(bf16[320,128]{1,0:T(8,128)(2,1)S(1)} %get-tuple-element.87), channel_id=1, source_target_pairs={{0,6},{1,7},{2,4},{3,5},{4,2},{5,3},{6,0},{7,1},{8,14},{9,15},{10,... | collective-permute-start | bytes 245768 | tf_op jit(solution)/shard_map/ppermute | solution.py:73
  94.9 8.2 %collective-permute-start.24 = (bf16[320,128]{1,0:T(8,128)(2,1)S(1)}, bf16[320,128]{1,0:T(8,128)(2,1)S(1)}, u32[]{:S(2)}, u32[]{:S(2)}) collective-permute-start(bf16[320,128]{1,0:T(8,128)(2,1)S(1)} %get-tuple-element.88), channel_id=1, source_target_pairs={{0,1},{1,0},{2,3},{3,2},{4,5},{5,4},{6,7},{7,6},{8,9},{9,8},{10,11... | collective-permute-start | bytes 245768 | tf_op jit(solution)/shard_map/ppermute | solution.py:73
  94.9 8.3 %collective-permute-start.25 = (bf16[320,128]{1,0:T(8,128)(2,1)S(1)}, bf16[320,128]{1,0:T(8,128)(2,1)S(1)}, u32[]{:S(2)}, u32[]{:S(2)}) collective-permute-start(bf16[320,128]{1,0:T(8,128)(2,1)S(1)} %get-tuple-element.89), channel_id=1, source_target_pairs={{0,3},{1,2},{2,1},{3,0},{4,7},{5,6},{6,5},{7,4},{8,11},{9,10},{10,... | collective-permute-start | bytes 245768 | tf_op jit(solution)/shard_map/ppermute | solution.py:73
  99.8 7.3 %copy-start.31 = (bf16[320,128]{1,0:T(8,128)(2,1)}, bf16[320,128]{1,0:T(8,128)(2,1)S(1)}, u32[]{:S(2)}) copy-start(bf16[320,128]{1,0:T(8,128)(2,1)S(1)} %collective-permute-done.21.refs_2_) | copy-start | bytes 245764
  99.8 7.3 %collective-permute-start.26 = (bf16[320,128]{1,0:T(8,128)(2,1)S(1)}, bf16[320,128]{1,0:T(8,128)(2,1)S(1)}, u32[]{:S(2)}, u32[]{:S(2)}) collective-permute-start(bf16[320,128]{1,0:T(8,128)(2,1)S(1)} %get-tuple-element.90), channel_id=1, source_target_pairs={{0,5},{1,4},{2,7},{3,6},{4,1},{5,0},{6,3},{7,2},{8,13},{9,12},{10,... | collective-permute-start | bytes 245768 | tf_op jit(solution)/shard_map/ppermute | solution.py:73
  99.8 7.3 %collective-permute-start.27 = (bf16[320,128]{1,0:T(8,128)(2,1)S(1)}, bf16[320,128]{1,0:T(8,128)(2,1)S(1)}, u32[]{:S(2)}, u32[]{:S(2)}) collective-permute-start(bf16[320,128]{1,0:T(8,128)(2,1)S(1)} %get-tuple-element.91), channel_id=1, source_target_pairs={{0,7},{1,6},{2,5},{3,4},{4,3},{5,2},{6,1},{7,0},{8,15},{9,14},{10,... | collective-permute-start | bytes 245768 | tf_op jit(solution)/shard_map/ppermute | solution.py:73
  111.2 4.7 %collective-permute-start.28 = (bf16[80,512]{1,0:T(8,128)(2,1)}, bf16[80,512]{1,0:T(8,128)(2,1)S(1)}, u32[]{:S(2)}, u32[]{:S(2)}) collective-permute-start(bf16[80,512]{1,0:T(8,128)(2,1)} %get-tuple-element.101), channel_id=1, source_target_pairs={{0,8},{8,0},{16,24},{24,16},{1,9},{9,1},{17,25},{25,17},{2,10},{10... | collective-permute-start | bytes 245768 | tf_op jit(solution)/shard_map/ppermute | solution.py:73
  112.4 9.7 %collective-permute-start.29 = (bf16[80,512]{1,0:T(8,128)(2,1)}, bf16[80,512]{1,0:T(8,128)(2,1)S(1)}, u32[]{:S(2)}, u32[]{:S(2)}) collective-permute-start(bf16[80,512]{1,0:T(8,128)(2,1)} %get-tuple-element.102), channel_id=1, source_target_pairs={{0,16},{8,24},{16,0},{24,8},{1,17},{9,25},{17,1},{25,9},{2,18},{10... | collective-permute-start | bytes 245768 | tf_op jit(solution)/shard_map/ppermute | solution.py:73
  113.9 8.2 %collective-permute-start.30 = (bf16[80,512]{1,0:T(8,128)(2,1)}, bf16[80,512]{1,0:T(8,128)(2,1)S(1)}, u32[]{:S(2)}, u32[]{:S(2)}) collective-permute-start(bf16[80,512]{1,0:T(8,128)(2,1)} %get-tuple-element.103), channel_id=1, source_target_pairs={{0,24},{8,16},{16,8},{24,0},{1,25},{9,17},{17,9},{25,1},{2,26},{10... | collective-permute-start | bytes 245768 | tf_op jit(solution)/shard_map/ppermute | solution.py:73
  123.1 33.4 %copy-start.23 = (s32[2]{0:T(128)S(1)}, s32[2]{0:T(128)}, u32[]{:S(2)}) copy-start(s32[2]{0:T(128)} %copy-done.20) | copy-start | bytes 28
  123.1 7.2 %collective-permute-start.33 = (bf16[80,512]{1,0:T(8,128)(2,1)S(1)}, bf16[80,512]{1,0:T(8,128)(2,1)S(1)}, u32[]{:S(2)}, u32[]{:S(2)}) collective-permute-start(bf16[80,512]{1,0:T(8,128)(2,1)S(1)} %add_convert_fusion), channel_id=1, source_target_pairs={{0,24},{8,16},{16,8},{24,0},{1,25},{9,17},{17,9},{25,1},{2,26},{10... | collective-permute-start | bytes 245768 | tf_op jit(solution)/shard_map/ppermute | solution.py:73
  125.4 7.6 %collective-permute-start.32 = (bf16[80,512]{1,0:T(8,128)(2,1)S(1)}, bf16[80,512]{1,0:T(8,128)(2,1)S(1)}, u32[]{:S(2)}, u32[]{:S(2)}) collective-permute-start(bf16[80,512]{1,0:T(8,128)(2,1)S(1)} %add_convert_fusion), channel_id=1, source_target_pairs={{0,16},{8,24},{16,0},{24,8},{1,17},{9,25},{17,1},{25,9},{2,18},{10... | collective-permute-start | bytes 245768 | tf_op jit(solution)/shard_map/ppermute | solution.py:73
  126.1 6.9 %collective-permute-start.31 = (bf16[80,512]{1,0:T(8,128)(2,1)S(1)}, bf16[80,512]{1,0:T(8,128)(2,1)S(1)}, u32[]{:S(2)}, u32[]{:S(2)}) collective-permute-start(bf16[80,512]{1,0:T(8,128)(2,1)S(1)} %add_convert_fusion), channel_id=1, source_target_pairs={{0,8},{8,0},{16,24},{24,16},{1,9},{9,1},{17,25},{25,17},{2,10},{10... | collective-permute-start | bytes 245768 | tf_op jit(solution)/shard_map/ppermute | solution.py:73
  133.1 11.5 %collective-permute-start.36 = (bf16[320,512]{1,0:T(8,128)(2,1)S(1)}, bf16[320,512]{1,0:T(8,128)(2,1)S(1)}, u32[]{:S(2)}, u32[]{:S(2)}) collective-permute-start(bf16[320,512]{1,0:T(8,128)(2,1)S(1)} %pad_maximum_fusion.refs_1_), channel_id=1, source_target_pairs={{0,6},{1,7},{2,4},{3,5},{4,2},{5,3},{6,0},{7,1},{8,14},{9,15},{10,... | collective-permute-start | bytes 983048 | tf_op jit(solution)/shard_map/ppermute | solution.py:73
  133.1 16.6 %collective-permute-start.35 = (bf16[320,512]{1,0:T(8,128)(2,1)S(1)}, bf16[320,512]{1,0:T(8,128)(2,1)S(1)}, u32[]{:S(2)}, u32[]{:S(2)}) collective-permute-start(bf16[320,512]{1,0:T(8,128)(2,1)S(1)} %pad_maximum_fusion.refs_1_), channel_id=1, source_target_pairs={{0,4},{1,5},{2,6},{3,7},{4,0},{5,1},{6,2},{7,3},{8,12},{9,13},{10,... | collective-permute-start | bytes 983048 | tf_op jit(solution)/shard_map/ppermute | solution.py:73
  134.6 15.2 %collective-permute-start.34 = (bf16[320,512]{1,0:T(8,128)(2,1)S(1)}, bf16[320,512]{1,0:T(8,128)(2,1)S(1)}, u32[]{:S(2)}, u32[]{:S(2)}) collective-permute-start(bf16[320,512]{1,0:T(8,128)(2,1)S(1)} %pad_maximum_fusion.refs_1_), channel_id=1, source_target_pairs={{0,2},{1,3},{2,0},{3,1},{4,6},{5,7},{6,4},{7,5},{8,10},{9,11},{10,... | collective-permute-start | bytes 983048 | tf_op jit(solution)/shard_map/ppermute | solution.py:73
  141.4 11.1 %all-to-all-start.3 = ((bf16[32,4,512]{2,1,0:T(4,128)(2,1)}), bf16[32,4,512]{2,1,0:T(4,128)(2,1)S(1)}, u32[]{:S(2)}, u32[]{:S(2)}) async-start(bf16[32,4,512]{2,1,0:T(4,128)(2,1)} %get-tuple-element.83), calls=%async_computation.3 | async-start | bytes 262144 | tf_op jit(solution)/shard_map/all_to_all | solution.py:650
  152.6 3.9 %collective-permute-start.37 = (bf16[320,512]{1,0:T(8,128)(2,1)S(1)}, bf16[320,512]{1,0:T(8,128)(2,1)S(1)}, u32[]{:S(2)}, u32[]{:S(2)}) collective-permute-start(bf16[320,512]{1,0:T(8,128)(2,1)S(1)} %pad_maximum_fusion.refs_1_), channel_id=1, source_target_pairs={{0,1},{1,0},{2,3},{3,2},{4,5},{5,4},{6,7},{7,6},{8,9},{9,8},{10,11... | collective-permute-start | bytes 983048 | tf_op jit(solution)/shard_map/ppermute | solution.py:73
  152.8 3.7 %collective-permute-start.38 = (bf16[320,512]{1,0:T(8,128)(2,1)S(1)}, bf16[320,512]{1,0:T(8,128)(2,1)S(1)}, u32[]{:S(2)}, u32[]{:S(2)}) collective-permute-start(bf16[320,512]{1,0:T(8,128)(2,1)S(1)} %collective-permute-done.34.refs_2_), channel_id=1, source_target_pairs={{0,1},{1,0},{2,3},{3,2},{4,5},{5,4},{6,7},{7,6},{8,9},{9,8},{10,11... | collective-permute-start | bytes 983048 | tf_op jit(solution)/shard_map/ppermute | solution.py:73
  153.1 3.4 %collective-permute-start.39 = (bf16[320,512]{1,0:T(8,128)(2,1)S(1)}, bf16[320,512]{1,0:T(8,128)(2,1)S(1)}, u32[]{:S(2)}, u32[]{:S(2)}) collective-permute-start(bf16[320,512]{1,0:T(8,128)(2,1)S(1)} %collective-permute-done.35.refs_3_), channel_id=1, source_target_pairs={{0,1},{1,0},{2,3},{3,2},{4,5},{5,4},{6,7},{7,6},{8,9},{9,8},{10,11... | collective-permute-start | bytes 983048 | tf_op jit(solution)/shard_map/ppermute | solution.py:73
  153.3 3.2 %collective-permute-start.40 = (bf16[320,512]{1,0:T(8,128)(2,1)S(1)}, bf16[320,512]{1,0:T(8,128)(2,1)S(1)}, u32[]{:S(2)}, u32[]{:S(2)}) collective-permute-start(bf16[320,512]{1,0:T(8,128)(2,1)S(1)} %collective-permute-done.36.refs_4_), channel_id=1, source_target_pairs={{0,1},{1,0},{2,3},{3,2},{4,5},{5,4},{6,7},{7,6},{8,9},{9,8},{10,11... | collective-permute-start | bytes 983048 | tf_op jit(solution)/shard_map/ppermute | solution.py:73
  (18 other events, 28.7 us)

commit v3 on v2

--- a/solution.py
+++ b/solution.py
@@ -439,8 +439,17 @@
         joined_ref[:, (n + 1) * width : (n + 2) * width] = columns
 
 
-def scatter_kernel(capacity, stride, each, *refs):
-    _, asked_ref, arrived_ref, hot_ref, cold_ref, mine_ref = refs
+def mine_kernel(capacity, stride, here_ref, arrived_ref, mine_ref):
+    devices, each, width = mine_ref.shape
+    total = arrived_ref[0].astype(f32)
+    for n in range(1, devices):
+        total = total + arrived_ref[n].astype(f32)
+    first = range(capacity, (width // LANES) * stride, stride)
+    sums = jnp.concatenate([total[n : n + each] for n in first], axis=1)
+    mine_ref[...] = jnp.broadcast_to(sums[None], mine_ref.shape).astype(low)
+
+
+def scatter_kernel(capacity, stride, here_ref, asked_ref, arrived_ref, hot_ref, cold_ref):
     devices = asked_ref.shape[0]
     hot_count, width = hot_ref.shape
     cold_count, cold_width = cold_ref.shape
@@ -448,16 +457,14 @@
     asked = asked_ref[...].reshape(devices, LANES)
     stack = arrived_ref[...].astype(f32).reshape(devices, tiles * stride, LANES)
     stack = jnp.swapaxes(stack, 0, 1)
-    rows, sums = [], []
+    rows = []
     for n in range(tiles):
         part = stack[n * stride : n * stride + capacity]
         rows.append(part.reshape(capacity * devices, LANES).astype(low))
-        sums.append(jnp.sum(stack[n * stride + capacity : n * stride + capacity + each], axis=1))
     rows = jnp.concatenate(rows, axis=1)
     hot_ref[...] = dot(asked_select(asked, capacity, 0, hot_count), rows, (0, 0))
     chosen = asked_select(asked, capacity, hot_count, cold_count)
     cold_ref[...] = dot(chosen, rows[:, :cold_width], (0, 0))
-    mine_ref[...] = jnp.broadcast_to(jnp.concatenate(sums, axis=1)[None], mine_ref.shape).astype(low)
 
 
 def assemble(position, pieces, norm_scale, width):
@@ -524,22 +531,15 @@
     )
     asked = lax.all_to_all(requests, everyone, split_axis=0, concat_axis=0, tiled=True)
     cotangents = gather_pieces(cotangent, "cp")
-    near = (group + 1) // 2
-    asked, *front = lax.optimization_barrier((asked, *cotangents[:near]))
-    cotangents = front + cotangents[near:]
     picked = call(
         functools.partial(pick_kernel, capacity),
         [position, asked, hot_table, cold_table],
         [shaped((devices * tiles * capacity, LANES), low)],
         limit=56,
     )[0]
-    rows_back = lax.all_to_all(
-        picked.reshape(devices, tiles * capacity, LANES),
-        everyone,
-        split_axis=0,
-        concat_axis=0,
-        tiled=True,
-    ).reshape(picked.shape)
+    picked = picked.reshape(devices, tiles * capacity, LANES)
+    rows_back = lax.all_to_all(picked, everyone, split_axis=0, concat_axis=0, tiled=True)
+    rows_back = rows_back.reshape(devices * tiles * capacity, LANES)
     vector, embedded, normed_low = call(
         functools.partial(embed_kernel, capacity, hot_count),
         [position, owners, rank, slot, rows_back, cold_projection],
@@ -636,18 +636,19 @@
     for step in range(1, count):
         line.append(exchange(mine, "dp", step))
     line = jnp.concatenate(line, axis=0)
-    hot_gradient, cold_gradient, copies = call(
-        functools.partial(scatter_kernel, capacity, stride, each),
+    copies = call(
+        functools.partial(mine_kernel, capacity, stride),
+        [position, arrived],
+        [shaped((devices, each, width), low)],
+    )[0]
+    projection = lax.all_to_all(copies, everyone, split_axis=0, concat_axis=0, tiled=True)
+    hot_gradient, cold_gradient = call(
+        functools.partial(scatter_kernel, capacity, stride),
         [position, asked, arrived.reshape(devices * tiles * stride, LANES)],
-        [
-            shaped((hot_count, width), f32),
-            shaped((cold_count, cold_width), f32),
-            shaped((devices, each, width), low),
-        ],
+        [shaped((hot_count, width), f32), shaped((cold_count, cold_width), f32)],
         flops=4 * devices * capacity * hot_count * width,
         limit=56,
     )
-    projection = lax.all_to_all(copies, everyone, split_axis=0, concat_axis=0, tiled=True)
     pieces = gather_pieces(line, "cp", (projection, hot_gradient, cold_gradient))
     norm_scale = (tokens * devices) ** (-0.5)
     joined_gradient, output_gradient = assemble(position, pieces, norm_scale, width)

time: 161 us -> 159 us (0.988)
  waiting for transfers between devices: 51.1 us -> 47.9 us
  local copies, waits for them, and re-layouts: 9.47 us -> 7.51 us
    all_to_all x1, waiting for transfers between devices: 10.9 us -> 0.01 us  [local(): lax.all_to_all(picked, everyone, split_axis=0, concat_axis=0, tiled=True)]
    ppermute x41, waiting for transfers between devices: 37.4 us -> 46.9 us  [exchange(): return lax.ppermute(block, axis, pairs)]
    unnamed x76 -> x74, local copies, waits for them, and re-layouts: 8.68 us -> 6.72 us
    all_to_all x1, waiting for transfers between devices: 2.81 us -> 1.04 us  [local(): lax.all_to_all(copies, everyone, split_axis=0, concat_axis=0, tiled=True)]
    pallas_call x12 -> x13, Pallas kernels: 42.4 us -> 43.5 us  [call(): pl.pallas_call(kernel, out_shape=outs, in_specs=[SMEM] * scalars + [VMEM]...]
where the time goes in v3:
time: 159 us; the launch traced here: 158 us
  waiting for transfers between devices  47.9 us (30%)
  Pallas kernels  43.5 us (27%)
  starting transfers between devices  42.5 us (27%)
  blocking collectives  14.4 us (9%)
  local copies, waits for them, and re-layouts  7.51 us (5%)
    ppermute x41, waiting for transfers between devices, exchange(): return lax.ppermute(block, axis, pairs)  46.9 us
    pallas_call x13, Pallas kernels, call(): pl.pallas_call(kernel, out_shape=outs, in_specs=[SMEM] * scalars + [VMEM]...  43.5 us
    ppermute x41, starting transfers between devices, exchange(): return lax.ppermute(block, axis, pairs)  32.5 us
    all_to_all x1, blocking collectives, local(): lax.all_to_all(requests, everyone, split_axis=0, concat_axis=0, tiled=True)  14.4 us
    unnamed x74, local copies, waits for them, and re-layouts  6.72 us
    all_to_all x1, starting transfers between devices, local(): lax.all_to_all(sent, everyone, split_axis=0, concat_axis=0, tiled=True)  4.17 us
  transfers between devices with their start and end apart: 44, of which 15 were waited for; matrix products, arithmetic and copies ran while one was open for 1% of the time, Pallas kernels for 12%

profile of v3, /device:TPU:0, one launch (start us, length us, event | category | flops | bytes accessed | tf_op | source)
XLA Modules:
  0.0 158.1 jit_solution(3908333052430310861)
XLA Ops:
  0.8 0.8 copy-done.27
  1.6 0.7 copy-done.28
  2.2 1.0 shard_map.127
  3.2 14.4 %all_to_all.20.asked_ref = s32[32,1,128]{2,1,0:T(1,128)} all-to-all(s32[32,1,128]{2,1,0:T(1,128)S(1)} %get-tuple-element.55), channel_id=1, replica_groups=mesh['dp'=4,'cp'=8] {'dp','cp'}, dimensions={0} | all-to-all | bytes 32768 | tf_op jit(solution)/shard_map/all_to_all | solution.py:532
  17.7 3.4 %shard_map.128 = bf16[1280,128]{1,0:T(8,128)(2,1)} custom-call(s32[2]{0:T(128)} %copy-done.21, s32[32,1,128]{2,1,0:T(1,128)} %all_to_all.20.asked_ref, bf16[512,512]{1,0:T(8,128)(2,1)} %hot_ref.1, bf16[2048,128]{1,0:T(8,128)(2,1)} %cold_ref.1), custom_call_target="tpu_custom_call" | custom-call | bytes 1392648 | tf_op jit(solution)/shard_map/pallas_call | solution.py:96
  21.1 2.7 %all-to-all-start.1 = ((bf16[32,40,128]{2,1,0:T(8,128)(2,1)}), bf16[32,40,128]{2,1,0:T(8,128)(2,1)S(1)}, u32[]{:S(2)}, u32[]{:S(2)}) async-start(bf16[32,40,128]{2,1,0:T(8,128)(2,1)} %bitcast.13), calls=%async_computation.1 | async-start | bytes 655360 | tf_op jit(solution)/shard_map/all_to_all | solution.py:541
  23.8 2.6 %collective-permute-start.2 = (bf16[128,512]{1,0:T(8,128)(2,1)S(1)}, bf16[128,512]{1,0:T(8,128)(2,1)S(1)}, u32[]{:S(2)}, u32[]{:S(2)}) collective-permute-start(bf16[128,512]{1,0:T(8,128)(2,1)S(1)} %copy-done.4), channel_id=1, source_target_pairs={{0,6},{1,7},{2,4},{3,5},{4,2},{5,3},{6,0},{7,1},{8,14},{9,15},{10,... | collective-permute-start | bytes 393224 | tf_op jit(solution)/shard_map/ppermute | solution.py:73
  26.4 0.5 collective-permute-start.1
  27.4 6.4 %collective-permute-done.2.refs_12_ = bf16[128,512]{1,0:T(8,128)(2,1)S(1)} collective-permute-done((bf16[128,512]{1,0:T(8,128)(2,1)S(1)}, bf16[128,512]{1,0:T(8,128)(2,1)S(1)}, u32[]{:S(2)}, u32[]{:S(2)}) %collective-permute-start.2) | collective-permute-done | bytes 131104 | tf_op jit(solution)/shard_map/ppermute | solution.py:73
  33.8 2.6 %collective-permute-done.1.refs_11_ = bf16[128,512]{1,0:T(8,128)(2,1)} collective-permute-done((bf16[128,512]{1,0:T(8,128)(2,1)S(1)}, bf16[128,512]{1,0:T(8,128)(2,1)}, u32[]{:S(2)}, u32[]{:S(2)}) %collective-permute-start.1) | collective-permute-done | bytes 131104 | tf_op jit(solution)/shard_map/ppermute | solution.py:73
  37.0 0.6 copy-done.22
  37.6 1.4 shard_map.129
  39.0 0.7 copy-done.12
  39.6 0.6 copy-done.26
  40.3 1.0 collective-permute-start.9
  41.3 1.5 collective-permute-start.8
  42.8 1.0 collective-permute-start.7
  43.8 3.8 %collective-permute-done.9.refs_4_.refs_20_ = bf16[128,512]{1,0:T(8,128)(2,1)S(1)} collective-permute-done((bf16[128,512]{1,0:T(8,128)(2,1)S(1)}, bf16[128,512]{1,0:T(8,128)(2,1)S(1)}, u32[]{:S(2)}, u32[]{:S(2)}) %collective-permute-start.9) | collective-permute-done | bytes 131104 | tf_op jit(solution)/shard_map/ppermute | solution.py:73
  47.7 1.7 %collective-permute-done.8.refs_3_.refs_19_ = bf16[128,512]{1,0:T(8,128)(2,1)S(1)} collective-permute-done((bf16[128,512]{1,0:T(8,128)(2,1)S(1)}, bf16[128,512]{1,0:T(8,128)(2,1)S(1)}, u32[]{:S(2)}, u32[]{:S(2)}) %collective-permute-start.8) | collective-permute-done | bytes 131104 | tf_op jit(solution)/shard_map/ppermute | solution.py:73
  49.9 0.6 copy-done.23
  50.5 1.0 shard_map.130
  51.6 5.9 %shard_map.131 = (bf16[128,512]{1,0:T(8,128)(2,1)S(1)}, bf16[128,512]{1,0:T(8,128)(2,1)S(1)}, bf16[128,512]{1,0:T(8,128)(2,1)S(1)}, bf16[8,128,128]{2,1,0:T(8,128)(2,1)S(1)}, bf16[1024,1024]{1,0:T(8,128)(2,1)S(1)}) custom-call(s32[2]{0:T(128)S(1)} %copy-done.23, bf16[128,512]{1,0:T(8,128)(2,1)S(1)} %get-tuple-element.57.normed_ref.refs_1_.refs_17_, ...), custom_call_target="tpu_custom_call" | custom-call | flops 1342177280 | bytes 8126472 | tf_op jit(solution)/shard_map/pallas_call | solution.py:96
  57.6 0.6 copy-done.19
  58.2 1.2 collective-permute-start.16
  59.4 1.4 collective-permute-start.15
  60.8 0.9 collective-permute-start.14
  61.7 3.8 %collective-permute-done.16.refs_4_ = bf16[128,512]{1,0:T(8,128)(2,1)S(1)} collective-permute-done((bf16[128,512]{1,0:T(8,128)(2,1)S(1)}, bf16[128,512]{1,0:T(8,128)(2,1)S(1)}, u32[]{:S(2)}, u32[]{:S(2)}) %collective-permute-start.16) | collective-permute-done | bytes 131104 | tf_op jit(solution)/shard_map/ppermute | solution.py:73
  65.6 1.9 %collective-permute-done.15.refs_3_ = bf16[128,512]{1,0:T(8,128)(2,1)S(1)} collective-permute-done((bf16[128,512]{1,0:T(8,128)(2,1)S(1)}, bf16[128,512]{1,0:T(8,128)(2,1)S(1)}, u32[]{:S(2)}, u32[]{:S(2)}) %collective-permute-start.15) | collective-permute-done | bytes 131104 | tf_op jit(solution)/shard_map/ppermute | solution.py:73
  68.0 6.0 %shard_map.133 = (bf16[128,512]{1,0:T(8,128)(2,1)S(1)}, bf16[1024,512]{1,0:T(8,128)(2,1)S(1)}) custom-call(s32[2]{0:T(128)S(1)} %copy-done.23, bf16[128,512]{1,0:T(8,128)(2,1)S(1)} %get-tuple-element.57.normed_ref.refs_1_.refs_17_, bf16[128,512]{1,0:T(8,128)(2,1)S(1)} %collective-permute-done.7.refs_2_.refs_18_, ...), custom_call_target="tpu_custom_call" | custom-call | flops 402653184 | bytes 8126472 | tf_op jit(solution)/shard_map/pallas_call | solution.py:96
  74.1 4.9 %shard_map.134 = (bf16[128,1536]{1,0:T(8,128)(2,1)S(1)}, bf16[320,128]{1,0:T(8,128)(2,1)S(1)}, bf16[320,128]{1,0:T(8,128)(2,1)S(1)}, bf16[320,128]{1,0:T(8,128)(...) custom-call(s32[2]{0:T(128)S(1)} %copy-done.23, ...), custom_call_target="tpu_custom_call" | custom-call | flops 536870912 | bytes 5111816 | tf_op jit(solution)/shard_map/pallas_call | solution.py:96
  79.0 0.7 copy-done.14
  79.7 0.6 copy-done.20
  80.3 4.9 %shard_map.135 = bf16[1792,128]{1,0:T(8,128)(2,1)} custom-call(s32[2]{0:T(128)} %copy-done.21, bf16[128,512]{1,0:T(8,128)(2,1)} %copy-done.18, bf16[128,1536]{1,0:T(8,128)(2,1)} %copy-done.14, bf16[512,2048]{1,0:T(8,128)(2,1)} %refs_3_.1, f32[128,512]{1,0:T(8,128)} %copy-done.12, bf16[128,512]{1,0:T(8,128)(2,1)} %refs_9_.4, bf16[128,128]{1,0:T(8,128)(2,1)} %copy-done.26, ...), custom_call_target="tpu_custom_call" | custom-call | flops 268435456 | bytes 3638792 | tf_op jit(solution)/shard_map/pallas_call | solution.py:96
  85.2 4.2 %all-to-all-start.2 = ((bf16[32,56,128]{2,1,0:T(8,128)(2,1)}), bf16[32,56,128]{2,1,0:T(8,128)(2,1)S(1)}, u32[]{:S(2)}, u32[]{:S(2)}) async-start(bf16[32,56,128]{2,1,0:T(8,128)(2,1)} %bitcast.12), calls=%async_computation.2 | async-start | bytes 917504 | tf_op jit(solution)/shard_map/all_to_all | solution.py:614
  89.4 1.8 %collective-permute-start.21 = (bf16[320,128]{1,0:T(8,128)(2,1)S(1)}, bf16[320,128]{1,0:T(8,128)(2,1)S(1)}, u32[]{:S(2)}, u32[]{:S(2)}) collective-permute-start(bf16[320,128]{1,0:T(8,128)(2,1)S(1)} %get-tuple-element.73), channel_id=1, source_target_pairs={{0,2},{1,3},{2,0},{3,1},{4,6},{5,7},{6,4},{7,5},{8,10},{9,11},{10,... | collective-permute-start | bytes 245768 | tf_op jit(solution)/shard_map/ppermute | solution.py:73
  91.3 1.5 collective-permute-start.22
  93.0 1.9 %collective-permute-start.25 = (bf16[320,128]{1,0:T(8,128)(2,1)S(1)}, bf16[320,128]{1,0:T(8,128)(2,1)S(1)}, u32[]{:S(2)}, u32[]{:S(2)}) collective-permute-start(bf16[320,128]{1,0:T(8,128)(2,1)S(1)} %get-tuple-element.77), channel_id=1, source_target_pairs={{0,3},{1,2},{2,1},{3,0},{4,7},{5,6},{6,5},{7,4},{8,11},{9,10},{10,... | collective-permute-start | bytes 245768 | tf_op jit(solution)/shard_map/ppermute | solution.py:73
  94.9 3.4 %collective-permute-done.21.refs_2_ = bf16[320,128]{1,0:T(8,128)(2,1)S(1)} collective-permute-done((bf16[320,128]{1,0:T(8,128)(2,1)S(1)}, bf16[320,128]{1,0:T(8,128)(2,1)S(1)}, u32[]{:S(2)}, u32[]{:S(2)}) %collective-permute-start.21) | collective-permute-done | bytes 81952 | tf_op jit(solution)/shard_map/ppermute | solution.py:73
  98.3 1.5 collective-permute-start.27
  99.8 1.8 %collective-permute-done.23.refs_4_ = bf16[320,128]{1,0:T(8,128)(2,1)S(1)} collective-permute-done((bf16[320,128]{1,0:T(8,128)(2,1)S(1)}, bf16[320,128]{1,0:T(8,128)(2,1)S(1)}, u32[]{:S(2)}, u32[]{:S(2)}) %collective-permute-start.23) | collective-permute-done | bytes 81952 | tf_op jit(solution)/shard_map/ppermute | solution.py:73
  101.6 3.9 %collective-permute-done.26.refs_7_ = bf16[320,128]{1,0:T(8,128)(2,1)S(1)} collective-permute-done((bf16[320,128]{1,0:T(8,128)(2,1)S(1)}, bf16[320,128]{1,0:T(8,128)(2,1)S(1)}, u32[]{:S(2)}, u32[]{:S(2)}) %collective-permute-start.26) | collective-permute-done | bytes 81952 | tf_op jit(solution)/shard_map/ppermute | solution.py:73
  105.6 0.6 copy-done.35
  106.2 3.4 %shard_map.138 = (f32[80,512]{1,0:T(8,128)}, bf16[80,512]{1,0:T(8,128)(2,1)}, bf16[80,512]{1,0:T(8,128)(2,1)}, bf16[80,512]{1,0:T(8,128)(2,1)}) custom-call(s32[2]{0:T(128)} %copy-done.21, bf16[320,128]{1,0:T(8,128)(2,1)} %copy-done.20, bf16[320,128]{1,0:T(8,128)(2,1)} %copy-done.30, bf16[320,128]{1,0:T(8,128)(2,1)} %copy-done.31, ...), custom_call_target="tpu_custom_call" | custom-call | flops 335544320 | bytes 3162120 | tf_op jit(solution)/shard_map/pallas_call | solution.py:96
  109.6 1.3 collective-permute-start.28
  110.8 1.6 collective-permute-start.29
  112.4 1.6 %collective-permute-start.30 = (bf16[80,512]{1,0:T(8,128)(2,1)}, bf16[80,512]{1,0:T(8,128)(2,1)S(1)}, u32[]{:S(2)}, u32[]{:S(2)}) collective-permute-start(bf16[80,512]{1,0:T(8,128)(2,1)} %get-tuple-element.91), channel_id=1, source_target_pairs={{0,24},{8,16},{16,8},{24,0},{1,25},{9,17},{17,9},{25,1},{2,26},{10... | collective-permute-start | bytes 245768 | tf_op jit(solution)/shard_map/ppermute | solution.py:73
  114.3 6.2 %collective-permute-done.29 = bf16[80,512]{1,0:T(8,128)(2,1)S(1)} collective-permute-done((bf16[80,512]{1,0:T(8,128)(2,1)}, bf16[80,512]{1,0:T(8,128)(2,1)S(1)}, u32[]{:S(2)}, u32[]{:S(2)}) %collective-permute-start.29) | collective-permute-done | bytes 81952 | tf_op jit(solution)/shard_map/ppermute | solution.py:73
  120.5 1.0 add_convert_fusion
  121.4 2.4 %collective-permute-start.33 = (bf16[80,512]{1,0:T(8,128)(2,1)S(1)}, bf16[80,512]{1,0:T(8,128)(2,1)S(1)}, u32[]{:S(2)}, u32[]{:S(2)}) collective-permute-start(bf16[80,512]{1,0:T(8,128)(2,1)S(1)} %add_convert_fusion), channel_id=1, source_target_pairs={{0,24},{8,16},{16,8},{24,0},{1,25},{9,17},{17,9},{25,1},{2,26},{10... | collective-permute-start | bytes 245768 | tf_op jit(solution)/shard_map/ppermute | solution.py:73
  123.8 0.6 collective-permute-start.32
  124.5 1.4 collective-permute-start.31
  125.9 2.8 %collective-permute-done.33 = bf16[80,512]{1,0:T(8,128)(2,1)S(1)} collective-permute-done((bf16[80,512]{1,0:T(8,128)(2,1)S(1)}, bf16[80,512]{1,0:T(8,128)(2,1)S(1)}, u32[]{:S(2)}, u32[]{:S(2)}) %collective-permute-start.33) | collective-permute-done | bytes 81952 | tf_op jit(solution)/shard_map/ppermute | solution.py:73
  128.7 2.7 %collective-permute-done.32 = bf16[80,512]{1,0:T(8,128)(2,1)S(1)} collective-permute-done((bf16[80,512]{1,0:T(8,128)(2,1)S(1)}, bf16[80,512]{1,0:T(8,128)(2,1)S(1)}, u32[]{:S(2)}, u32[]{:S(2)}) %collective-permute-start.32) | collective-permute-done | bytes 81952 | tf_op jit(solution)/shard_map/ppermute | solution.py:73
  131.5 1.5 collective-permute-start.35
  133.0 2.0 %collective-permute-start.34 = (bf16[320,512]{1,0:T(8,128)(2,1)S(1)}, bf16[320,512]{1,0:T(8,128)(2,1)S(1)}, u32[]{:S(2)}, u32[]{:S(2)}) collective-permute-start(bf16[320,512]{1,0:T(8,128)(2,1)S(1)} %pad_maximum_fusion.refs_1_), channel_id=1, source_target_pairs={{0,2},{1,3},{2,0},{3,1},{4,6},{5,7},{6,4},{7,5},{8,10},{9,11},{10,... | collective-permute-start | bytes 983048 | tf_op jit(solution)/shard_map/ppermute | solution.py:73
  135.0 1.3 shard_map.137
  136.2 3.1 %all-to-all-start.3 = ((bf16[32,4,512]{2,1,0:T(4,128)(2,1)}), bf16[32,4,512]{2,1,0:T(4,128)(2,1)S(1)}, u32[]{:S(2)}, u32[]{:S(2)}) async-start(bf16[32,4,512]{2,1,0:T(4,128)(2,1)} %shard_map.137), calls=%async_computation.3 | async-start | bytes 262144 | tf_op jit(solution)/shard_map/all_to_all | solution.py:644
  139.3 3.9 %shard_map.136 = (f32[512,512]{1,0:T(8,128)}, f32[2048,128]{1,0:T(8,128)}) custom-call(s32[2]{0:T(128)} %copy-done.21, s32[32,1,128]{2,1,0:T(1,128)} %all_to_all.20.asked_ref, bf16[1792,128]{1,0:T(8,128)(2,1)} %bitcast.8), custom_call_target="tpu_custom_call" | custom-call | flops 335544320 | bytes 2572296 | tf_op jit(solution)/shard_map/pallas_call | solution.py:96
  143.3 5.5 %collective-permute-done.35.refs_3_ = bf16[320,512]{1,0:T(8,128)(2,1)S(1)} collective-permute-done((bf16[320,512]{1,0:T(8,128)(2,1)S(1)}, bf16[320,512]{1,0:T(8,128)(2,1)S(1)}, u32[]{:S(2)}, u32[]{:S(2)}) %collective-permute-start.35) | collective-permute-done | bytes 327712 | tf_op jit(solution)/shard_map/ppermute | solution.py:73
  148.8 1.0 all-to-all-done.3
  149.8 0.5 collective-permute-start.38
  150.8 2.0 %shard_map.132 = bf16[128,512]{1,0:T(8,128)(2,1)} custom-call(s32[2]{0:T(128)} %copy-done.21, bf16[128,512]{1,0:T(8,128)(2,1)} %copy-done.19, bf16[512,512]{1,0:T(8,128)(2,1)} %mix_ref.1, f32[128,512]{1,0:T(8,128)} %copy-done.12), custom_call_target="tpu_custom_call" | custom-call | bytes 1048584 | tf_op jit(solution)/shard_map/pallas_call | solution.py:96
  152.9 0.8 mul.11
  153.8 4.4 %shard_map.139 = (f32[512,2048]{1,0:T(8,128)}, f32[512,512]{1,0:T(8,128)}) custom-call(s32[2]{0:T(128)S(1)} %copy-done.25, bf16[320,512]{1,0:T(8,128)(2,1)S(1)} %pad_maximum_fusion.refs_1_, bf16[320,512]{1,0:T(8,128)(2,1)S(1)} %collective-permute-done.34.refs_2_, bf16[320,512]{1,0:T(8,128)(2,1)S(1)} %collective-permute-done.35.refs_3_, ...), custom_call_target="tpu_custom_call" | custom-call | bytes 7864328 | tf_op jit(solution)/shard_map/pallas_call | solution.py:96
  (117 shorter events, 3.4 us)
Async XLA Ops:
  0.6 23.2 %copy-start.4 = (bf16[128,512]{1,0:T(8,128)(2,1)S(1)}, bf16[128,512]{1,0:T(8,128)(2,1)}, u32[]{:S(2)}) copy-start(bf16[128,512]{1,0:T(8,128)(2,1)} %refs_9_.4) | copy-start | bytes 393220
  0.6 36.3 %copy-start.13 = (bf16[128,512]{1,0:T(8,128)(2,1)S(1)}, bf16[128,512]{1,0:T(8,128)(2,1)}, u32[]{:S(2)}) copy-start(bf16[128,512]{1,0:T(8,128)(2,1)} %refs_10_.1) | copy-start | bytes 393220
  0.7 49.2 %copy-start = (bf16[512,2048]{1,0:T(8,128)(2,1)S(1)}, bf16[512,2048]{1,0:T(8,128)(2,1)}, u32[]{:S(2)}) copy-start(bf16[512,2048]{1,0:T(8,128)(2,1)} %refs_3_.1) | copy-start | bytes 6291460
  0.7 16.9 %copy-start.21 = (s32[2]{0:T(128)}, s32[2]{0:T(128)S(1)}, u32[]{:S(2)}) copy-start(s32[2]{0:T(128)S(1)} %pad_add_fusion.here_ref.refs_0_) | copy-start | bytes 28
  3.2 39.6 %copy-start.16 = (s32[128,1]{1,0:T(8,128)}, s32[128,1]{1,0:T(8,128)S(1)}, u32[]{:S(2)}) copy-start(s32[128,1]{1,0:T(8,128)S(1)} %get-tuple-element.54.refs_3_.refs_9_) | copy-start | bytes 1540
  3.2 39.6 %copy-start.17 = (s32[128,1]{1,0:T(8,128)}, s32[128,1]{1,0:T(8,128)S(1)}, u32[]{:S(2)}) copy-start(s32[128,1]{1,0:T(8,128)S(1)} %get-tuple-element.52.refs_1_.refs_7_) | copy-start | bytes 1540
  3.2 48.3 %copy-start.15 = (s32[128,1]{1,0:T(8,128)}, s32[128,1]{1,0:T(8,128)S(1)}, u32[]{:S(2)}) copy-start(s32[128,1]{1,0:T(8,128)S(1)} %get-tuple-element.53.refs_2_.refs_8_) | copy-start | bytes 1540
  21.1 30.6 %copy-start.2 = (bf16[512,512]{1,0:T(8,128)(2,1)S(1)}, bf16[512,512]{1,0:T(8,128)(2,1)}, u32[]{:S(2)}) copy-start(bf16[512,512]{1,0:T(8,128)(2,1)} %mix_ref.1) | copy-start | bytes 1572868
  21.1 15.9 %all-to-all-start.1 = ((bf16[32,40,128]{2,1,0:T(8,128)(2,1)}), bf16[32,40,128]{2,1,0:T(8,128)(2,1)S(1)}, u32[]{:S(2)}, u32[]{:S(2)}) async-start(bf16[32,40,128]{2,1,0:T(8,128)(2,1)} %bitcast.13), calls=%async_computation.1 | async-start | bytes 655360 | tf_op jit(solution)/shard_map/all_to_all | solution.py:541
  23.8 10.0 %collective-permute-start.2 = (bf16[128,512]{1,0:T(8,128)(2,1)S(1)}, bf16[128,512]{1,0:T(8,128)(2,1)S(1)}, u32[]{:S(2)}, u32[]{:S(2)}) collective-permute-start(bf16[128,512]{1,0:T(8,128)(2,1)S(1)} %copy-done.4), channel_id=1, source_target_pairs={{0,6},{1,7},{2,4},{3,5},{4,2},{5,3},{6,0},{7,1},{8,14},{9,15},{10,... | collective-permute-start | bytes 393224 | tf_op jit(solution)/shard_map/ppermute | solution.py:73
  26.4 10.0 %collective-permute-start.1 = (bf16[128,512]{1,0:T(8,128)(2,1)S(1)}, bf16[128,512]{1,0:T(8,128)(2,1)}, u32[]{:S(2)}, u32[]{:S(2)}) collective-permute-start(bf16[128,512]{1,0:T(8,128)(2,1)S(1)} %copy-done.4), channel_id=1, source_target_pairs={{0,4},{1,5},{2,6},{3,7},{4,0},{5,1},{6,2},{7,3},{8,12},{9,13},{10,... | collective-permute-start | bytes 393224 | tf_op jit(solution)/shard_map/ppermute | solution.py:73
  27.0 9.5 %collective-permute-start = (bf16[128,512]{1,0:T(8,128)(2,1)S(1)}, bf16[128,512]{1,0:T(8,128)(2,1)}, u32[]{:S(2)}, u32[]{:S(2)}) collective-permute-start(bf16[128,512]{1,0:T(8,128)(2,1)S(1)} %copy-done.4), channel_id=1, source_target_pairs={{0,2},{1,3},{2,0},{3,1},{4,6},{5,7},{6,4},{7,5},{8,10},{9,11},{10,... | collective-permute-start | bytes 393224 | tf_op jit(solution)/shard_map/ppermute | solution.py:73
  27.4 12.9 %collective-permute-start.3 = (bf16[128,512]{1,0:T(8,128)(2,1)S(1)}, bf16[128,512]{1,0:T(8,128)(2,1)}, u32[]{:S(2)}, u32[]{:S(2)}) collective-permute-start(bf16[128,512]{1,0:T(8,128)(2,1)S(1)} %copy-done.4), channel_id=1, source_target_pairs={{0,1},{1,0},{2,3},{3,2},{4,5},{5,4},{6,7},{7,6},{8,9},{9,8},{10,11... | collective-permute-start | bytes 393224 | tf_op jit(solution)/shard_map/ppermute | solution.py:73
  33.8 23.8 %copy-start.29 = (bf16[128,512]{1,0:T(8,128)(2,1)}, bf16[128,512]{1,0:T(8,128)(2,1)S(1)}, u32[]{:S(2)}) copy-start(bf16[128,512]{1,0:T(8,128)(2,1)S(1)} %collective-permute-done.2.refs_12_) | copy-start | bytes 393220
  33.8 6.5 %collective-permute-start.6 = (bf16[128,512]{1,0:T(8,128)(2,1)S(1)}, bf16[128,512]{1,0:T(8,128)(2,1)}, u32[]{:S(2)}, u32[]{:S(2)}) collective-permute-start(bf16[128,512]{1,0:T(8,128)(2,1)S(1)} %collective-permute-done.2.refs_12_), channel_id=1, source_target_pairs={{0,1},{1,0},{2,3},{3,2},{4,5},{5,4},{6,7},{7,6},{8,9},{9,8},{10,11... | collective-permute-start | bytes 393224 | tf_op jit(solution)/shard_map/ppermute | solution.py:73
  36.4 3.8 %collective-permute-start.5 = (bf16[128,512]{1,0:T(8,128)(2,1)}, bf16[128,512]{1,0:T(8,128)(2,1)}, u32[]{:S(2)}, u32[]{:S(2)}) collective-permute-start(bf16[128,512]{1,0:T(8,128)(2,1)} %collective-permute-done.1.refs_11_), channel_id=1, source_target_pairs={{0,1},{1,0},{2,3},{3,2},{4,5},{5,4},{6,7},{7,6},{8,9},{9,8},{10,11... | collective-permute-start | bytes 393224 | tf_op jit(solution)/shard_map/ppermute | solution.py:73
  36.5 3.8 %collective-permute-start.4 = (bf16[128,512]{1,0:T(8,128)(2,1)}, bf16[128,512]{1,0:T(8,128)(2,1)}, u32[]{:S(2)}, u32[]{:S(2)}) collective-permute-start(bf16[128,512]{1,0:T(8,128)(2,1)} %collective-permute-done.refs_10_), channel_id=1, source_target_pairs={{0,1},{1,0},{2,3},{3,2},{4,5},{5,4},{6,7},{7,6},{8,9},{9,8},{10,11... | collective-permute-start | bytes 393224 | tf_op jit(solution)/shard_map/ppermute | solution.py:73
  40.2 27.7 %copy-start.1 = (bf16[128,512]{1,0:T(8,128)(2,1)}, bf16[128,512]{1,0:T(8,128)(2,1)S(1)}, u32[]{:S(2)}) copy-start(bf16[128,512]{1,0:T(8,128)(2,1)S(1)} %get-tuple-element.57.normed_ref.refs_1_.refs_17_) | copy-start | bytes 393220
  40.3 7.4 %collective-permute-start.9 = (bf16[128,512]{1,0:T(8,128)(2,1)S(1)}, bf16[128,512]{1,0:T(8,128)(2,1)S(1)}, u32[]{:S(2)}, u32[]{:S(2)}) collective-permute-start(bf16[128,512]{1,0:T(8,128)(2,1)S(1)} %get-tuple-element.57.normed_ref.refs_1_.refs_17_), channel_id=1, source_target_pairs={{0,6},{1,7},{2,4},{3,5},{4,2},{5,3},{6,0},{7,1},{8,14},{9,15},{10,... | collective-permute-start | bytes 393224 | tf_op jit(solution)/shard_map/ppermute | solution.py:73
  41.3 8.1 %collective-permute-start.8 = (bf16[128,512]{1,0:T(8,128)(2,1)S(1)}, bf16[128,512]{1,0:T(8,128)(2,1)S(1)}, u32[]{:S(2)}, u32[]{:S(2)}) collective-permute-start(bf16[128,512]{1,0:T(8,128)(2,1)S(1)} %get-tuple-element.57.normed_ref.refs_1_.refs_17_), channel_id=1, source_target_pairs={{0,4},{1,5},{2,6},{3,7},{4,0},{5,1},{6,2},{7,3},{8,12},{9,13},{10,... | collective-permute-start | bytes 393224 | tf_op jit(solution)/shard_map/ppermute | solution.py:73
  42.8 6.6 %collective-permute-start.7 = (bf16[128,512]{1,0:T(8,128)(2,1)S(1)}, bf16[128,512]{1,0:T(8,128)(2,1)S(1)}, u32[]{:S(2)}, u32[]{:S(2)}) collective-permute-start(bf16[128,512]{1,0:T(8,128)(2,1)S(1)} %get-tuple-element.57.normed_ref.refs_1_.refs_17_), channel_id=1, source_target_pairs={{0,2},{1,3},{2,0},{3,1},{4,6},{5,7},{6,4},{7,5},{8,10},{9,11},{10,... | collective-permute-start | bytes 393224 | tf_op jit(solution)/shard_map/ppermute | solution.py:73
  43.8 7.7 %collective-permute-start.10 = (bf16[128,512]{1,0:T(8,128)(2,1)S(1)}, bf16[128,512]{1,0:T(8,128)(2,1)S(1)}, u32[]{:S(2)}, u32[]{:S(2)}) collective-permute-start(bf16[128,512]{1,0:T(8,128)(2,1)S(1)} %get-tuple-element.57.normed_ref.refs_1_.refs_17_), channel_id=1, source_target_pairs={{0,1},{1,0},{2,3},{3,2},{4,5},{5,4},{6,7},{7,6},{8,9},{9,8},{10,11... | collective-permute-start | bytes 393224 | tf_op jit(solution)/shard_map/ppermute | solution.py:73
  47.7 20.3 %copy-start.5 = (bf16[128,512]{1,0:T(8,128)(2,1)}, bf16[128,512]{1,0:T(8,128)(2,1)S(1)}, u32[]{:S(2)}) copy-start(bf16[128,512]{1,0:T(8,128)(2,1)S(1)} %collective-permute-done.9.refs_4_.refs_20_) | copy-start | bytes 393220
  47.7 3.9 %collective-permute-start.13 = (bf16[128,512]{1,0:T(8,128)(2,1)S(1)}, bf16[128,512]{1,0:T(8,128)(2,1)S(1)}, u32[]{:S(2)}, u32[]{:S(2)}) collective-permute-start(bf16[128,512]{1,0:T(8,128)(2,1)S(1)} %collective-permute-done.9.refs_4_.refs_20_), channel_id=1, source_target_pairs={{0,1},{1,0},{2,3},{3,2},{4,5},{5,4},{6,7},{7,6},{8,9},{9,8},{10,11... | collective-permute-start | bytes 393224 | tf_op jit(solution)/shard_map/ppermute | solution.py:73
  49.4 18.6 %copy-start.6 = (bf16[128,512]{1,0:T(8,128)(2,1)}, bf16[128,512]{1,0:T(8,128)(2,1)S(1)}, u32[]{:S(2)}) copy-start(bf16[128,512]{1,0:T(8,128)(2,1)S(1)} %collective-permute-done.8.refs_3_.refs_19_) | copy-start | bytes 393220
  49.4 2.2 %collective-permute-start.12 = (bf16[128,512]{1,0:T(8,128)(2,1)S(1)}, bf16[128,512]{1,0:T(8,128)(2,1)S(1)}, u32[]{:S(2)}, u32[]{:S(2)}) collective-permute-start(bf16[128,512]{1,0:T(8,128)(2,1)S(1)} %collective-permute-done.8.refs_3_.refs_19_), channel_id=1, source_target_pairs={{0,1},{1,0},{2,3},{3,2},{4,5},{5,4},{6,7},{7,6},{8,9},{9,8},{10,11... | collective-permute-start | bytes 393224 | tf_op jit(solution)/shard_map/ppermute | solution.py:73
  49.4 18.6 %copy-start.7 = (bf16[128,512]{1,0:T(8,128)(2,1)}, bf16[128,512]{1,0:T(8,128)(2,1)S(1)}, u32[]{:S(2)}) copy-start(bf16[128,512]{1,0:T(8,128)(2,1)S(1)} %collective-permute-done.7.refs_2_.refs_18_) | copy-start | bytes 393220
  49.4 2.2 %collective-permute-start.11 = (bf16[128,512]{1,0:T(8,128)(2,1)S(1)}, bf16[128,512]{1,0:T(8,128)(2,1)S(1)}, u32[]{:S(2)}, u32[]{:S(2)}) collective-permute-start(bf16[128,512]{1,0:T(8,128)(2,1)S(1)} %collective-permute-done.7.refs_2_.refs_18_), channel_id=1, source_target_pairs={{0,1},{1,0},{2,3},{3,2},{4,5},{5,4},{6,7},{7,6},{8,9},{9,8},{10,11... | collective-permute-start | bytes 393224 | tf_op jit(solution)/shard_map/ppermute | solution.py:73
  51.6 16.4 %copy-start.8 = (bf16[128,512]{1,0:T(8,128)(2,1)}, bf16[128,512]{1,0:T(8,128)(2,1)S(1)}, u32[]{:S(2)}) copy-start(bf16[128,512]{1,0:T(8,128)(2,1)S(1)} %collective-permute-done.10.refs_5_.refs_21_) | copy-start | bytes 393220
  51.6 16.4 %copy-start.9 = (bf16[128,512]{1,0:T(8,128)(2,1)}, bf16[128,512]{1,0:T(8,128)(2,1)S(1)}, u32[]{:S(2)}) copy-start(bf16[128,512]{1,0:T(8,128)(2,1)S(1)} %collective-permute-done.13.refs_8_.refs_24_) | copy-start | bytes 393220
  51.6 16.4 %copy-start.10 = (bf16[128,512]{1,0:T(8,128)(2,1)}, bf16[128,512]{1,0:T(8,128)(2,1)S(1)}, u32[]{:S(2)}) copy-start(bf16[128,512]{1,0:T(8,128)(2,1)S(1)} %collective-permute-done.12.refs_7_.refs_23_) | copy-start | bytes 393220
  51.6 16.4 %copy-start.11 = (bf16[128,512]{1,0:T(8,128)(2,1)}, bf16[128,512]{1,0:T(8,128)(2,1)S(1)}, u32[]{:S(2)}) copy-start(bf16[128,512]{1,0:T(8,128)(2,1)S(1)} %collective-permute-done.11.refs_6_.refs_22_) | copy-start | bytes 393220
  58.2 15.8 %copy-start.18 = (bf16[128,512]{1,0:T(8,128)(2,1)}, bf16[128,512]{1,0:T(8,128)(2,1)S(1)}, u32[]{:S(2)}) copy-start(bf16[128,512]{1,0:T(8,128)(2,1)S(1)} %get-tuple-element.62.refs_1_) | copy-start | bytes 393220
  58.2 7.3 %collective-permute-start.16 = (bf16[128,512]{1,0:T(8,128)(2,1)S(1)}, bf16[128,512]{1,0:T(8,128)(2,1)S(1)}, u32[]{:S(2)}, u32[]{:S(2)}) collective-permute-start(bf16[128,512]{1,0:T(8,128)(2,1)S(1)} %get-tuple-element.63.refs_12_.refs_1_), channel_id=1, source_target_pairs={{0,6},{1,7},{2,4},{3,5},{4,2},{5,3},{6,0},{7,1},{8,14},{9,15},{10,... | collective-permute-start | bytes 393224 | tf_op jit(solution)/shard_map/ppermute | solution.py:73
  59.4 8.0 %collective-permute-start.15 = (bf16[128,512]{1,0:T(8,128)(2,1)S(1)}, bf16[128,512]{1,0:T(8,128)(2,1)S(1)}, u32[]{:S(2)}, u32[]{:S(2)}) collective-permute-start(bf16[128,512]{1,0:T(8,128)(2,1)S(1)} %get-tuple-element.63.refs_12_.refs_1_), channel_id=1, source_target_pairs={{0,4},{1,5},{2,6},{3,7},{4,0},{5,1},{6,2},{7,3},{8,12},{9,13},{10,... | collective-permute-start | bytes 393224 | tf_op jit(solution)/shard_map/ppermute | solution.py:73
  60.8 6.7 %collective-permute-start.14 = (bf16[128,512]{1,0:T(8,128)(2,1)S(1)}, bf16[128,512]{1,0:T(8,128)(2,1)S(1)}, u32[]{:S(2)}, u32[]{:S(2)}) collective-permute-start(bf16[128,512]{1,0:T(8,128)(2,1)S(1)} %get-tuple-element.63.refs_12_.refs_1_), channel_id=1, source_target_pairs={{0,2},{1,3},{2,0},{3,1},{4,6},{5,7},{6,4},{7,5},{8,10},{9,11},{10,... | collective-permute-start | bytes 393224 | tf_op jit(solution)/shard_map/ppermute | solution.py:73
  61.7 12.3 %collective-permute-start.17 = (bf16[128,512]{1,0:T(8,128)(2,1)S(1)}, bf16[128,512]{1,0:T(8,128)(2,1)S(1)}, u32[]{:S(2)}, u32[]{:S(2)}) collective-permute-start(bf16[128,512]{1,0:T(8,128)(2,1)S(1)} %get-tuple-element.63.refs_12_.refs_1_), channel_id=1, source_target_pairs={{0,1},{1,0},{2,3},{3,2},{4,5},{5,4},{6,7},{7,6},{8,9},{9,8},{10,11... | collective-permute-start | bytes 393224 | tf_op jit(solution)/shard_map/ppermute | solution.py:73
  65.5 8.5 %collective-permute-start.20 = (bf16[128,512]{1,0:T(8,128)(2,1)S(1)}, bf16[128,512]{1,0:T(8,128)(2,1)S(1)}, u32[]{:S(2)}, u32[]{:S(2)}) collective-permute-start(bf16[128,512]{1,0:T(8,128)(2,1)S(1)} %collective-permute-done.16.refs_4_), channel_id=1, source_target_pairs={{0,1},{1,0},{2,3},{3,2},{4,5},{5,4},{6,7},{7,6},{8,9},{9,8},{10,11... | collective-permute-start | bytes 393224 | tf_op jit(solution)/shard_map/ppermute | solution.py:73
  67.4 6.6 %collective-permute-start.19 = (bf16[128,512]{1,0:T(8,128)(2,1)S(1)}, bf16[128,512]{1,0:T(8,128)(2,1)S(1)}, u32[]{:S(2)}, u32[]{:S(2)}) collective-permute-start(bf16[128,512]{1,0:T(8,128)(2,1)S(1)} %collective-permute-done.15.refs_3_), channel_id=1, source_target_pairs={{0,1},{1,0},{2,3},{3,2},{4,5},{5,4},{6,7},{7,6},{8,9},{9,8},{10,11... | collective-permute-start | bytes 393224 | tf_op jit(solution)/shard_map/ppermute | solution.py:73
  67.4 6.6 %collective-permute-start.18 = (bf16[128,512]{1,0:T(8,128)(2,1)S(1)}, bf16[128,512]{1,0:T(8,128)(2,1)S(1)}, u32[]{:S(2)}, u32[]{:S(2)}) collective-permute-start(bf16[128,512]{1,0:T(8,128)(2,1)S(1)} %collective-permute-done.14.refs_2_), channel_id=1, source_target_pairs={{0,1},{1,0},{2,3},{3,2},{4,5},{5,4},{6,7},{7,6},{8,9},{9,8},{10,11... | collective-permute-start | bytes 393224 | tf_op jit(solution)/shard_map/ppermute | solution.py:73
  85.2 49.7 %all-to-all-start.2 = ((bf16[32,56,128]{2,1,0:T(8,128)(2,1)}), bf16[32,56,128]{2,1,0:T(8,128)(2,1)S(1)}, u32[]{:S(2)}, u32[]{:S(2)}) async-start(bf16[32,56,128]{2,1,0:T(8,128)(2,1)} %bitcast.12), calls=%async_computation.2 | async-start | bytes 917504 | tf_op jit(solution)/shard_map/all_to_all | solution.py:614
  89.4 45.6 %copy-start.24 = (s32[2]{0:T(128)S(1)}, s32[2]{0:T(128)}, u32[]{:S(2)}) copy-start(s32[2]{0:T(128)} %copy-done.21) | copy-start | bytes 28
  89.4 8.8 %collective-permute-start.21 = (bf16[320,128]{1,0:T(8,128)(2,1)S(1)}, bf16[320,128]{1,0:T(8,128)(2,1)S(1)}, u32[]{:S(2)}, u32[]{:S(2)}) collective-permute-start(bf16[320,128]{1,0:T(8,128)(2,1)S(1)} %get-tuple-element.73), channel_id=1, source_target_pairs={{0,2},{1,3},{2,0},{3,1},{4,6},{5,7},{6,4},{7,5},{8,10},{9,11},{10,... | collective-permute-start | bytes 245768 | tf_op jit(solution)/shard_map/ppermute | solution.py:73
  91.3 7.0 %collective-permute-start.22 = (bf16[320,128]{1,0:T(8,128)(2,1)S(1)}, bf16[320,128]{1,0:T(8,128)(2,1)S(1)}, u32[]{:S(2)}, u32[]{:S(2)}) collective-permute-start(bf16[320,128]{1,0:T(8,128)(2,1)S(1)} %get-tuple-element.74), channel_id=1, source_target_pairs={{0,4},{1,5},{2,6},{3,7},{4,0},{5,1},{6,2},{7,3},{8,12},{9,13},{10,... | collective-permute-start | bytes 245768 | tf_op jit(solution)/shard_map/ppermute | solution.py:73
  92.7 8.8 %collective-permute-start.23 = (bf16[320,128]{1,0:T(8,128)(2,1)S(1)}, bf16[320,128]{1,0:T(8,128)(2,1)S(1)}, u32[]{:S(2)}, u32[]{:S(2)}) collective-permute-start(bf16[320,128]{1,0:T(8,128)(2,1)S(1)} %get-tuple-element.75), channel_id=1, source_target_pairs={{0,6},{1,7},{2,4},{3,5},{4,2},{5,3},{6,0},{7,1},{8,14},{9,15},{10,... | collective-permute-start | bytes 245768 | tf_op jit(solution)/shard_map/ppermute | solution.py:73
  93.0 8.6 %collective-permute-start.24 = (bf16[320,128]{1,0:T(8,128)(2,1)S(1)}, bf16[320,128]{1,0:T(8,128)(2,1)S(1)}, u32[]{:S(2)}, u32[]{:S(2)}) collective-permute-start(bf16[320,128]{1,0:T(8,128)(2,1)S(1)} %get-tuple-element.76), channel_id=1, source_target_pairs={{0,1},{1,0},{2,3},{3,2},{4,5},{5,4},{6,7},{7,6},{8,9},{9,8},{10,11... | collective-permute-start | bytes 245768 | tf_op jit(solution)/shard_map/ppermute | solution.py:73
  93.0 8.6 %collective-permute-start.25 = (bf16[320,128]{1,0:T(8,128)(2,1)S(1)}, bf16[320,128]{1,0:T(8,128)(2,1)S(1)}, u32[]{:S(2)}, u32[]{:S(2)}) collective-permute-start(bf16[320,128]{1,0:T(8,128)(2,1)S(1)} %get-tuple-element.77), channel_id=1, source_target_pairs={{0,3},{1,2},{2,1},{3,0},{4,7},{5,6},{6,5},{7,4},{8,11},{9,10},{10,... | collective-permute-start | bytes 245768 | tf_op jit(solution)/shard_map/ppermute | solution.py:73
  98.3 7.2 %collective-permute-start.26 = (bf16[320,128]{1,0:T(8,128)(2,1)S(1)}, bf16[320,128]{1,0:T(8,128)(2,1)S(1)}, u32[]{:S(2)}, u32[]{:S(2)}) collective-permute-start(bf16[320,128]{1,0:T(8,128)(2,1)S(1)} %get-tuple-element.78), channel_id=1, source_target_pairs={{0,5},{1,4},{2,7},{3,6},{4,1},{5,0},{6,3},{7,2},{8,13},{9,12},{10,... | collective-permute-start | bytes 245768 | tf_op jit(solution)/shard_map/ppermute | solution.py:73
  98.3 7.2 %collective-permute-start.27 = (bf16[320,128]{1,0:T(8,128)(2,1)S(1)}, bf16[320,128]{1,0:T(8,128)(2,1)S(1)}, u32[]{:S(2)}, u32[]{:S(2)}) collective-permute-start(bf16[320,128]{1,0:T(8,128)(2,1)S(1)} %get-tuple-element.79), channel_id=1, source_target_pairs={{0,7},{1,6},{2,5},{3,4},{4,3},{5,2},{6,1},{7,0},{8,15},{9,14},{10,... | collective-permute-start | bytes 245768 | tf_op jit(solution)/shard_map/ppermute | solution.py:73
  109.6 4.7 %collective-permute-start.28 = (bf16[80,512]{1,0:T(8,128)(2,1)}, bf16[80,512]{1,0:T(8,128)(2,1)S(1)}, u32[]{:S(2)}, u32[]{:S(2)}) collective-permute-start(bf16[80,512]{1,0:T(8,128)(2,1)} %get-tuple-element.89), channel_id=1, source_target_pairs={{0,8},{8,0},{16,24},{24,16},{1,9},{9,1},{17,25},{25,17},{2,10},{10... | collective-permute-start | bytes 245768 | tf_op jit(solution)/shard_map/ppermute | solution.py:73
  110.8 9.7 %collective-permute-start.29 = (bf16[80,512]{1,0:T(8,128)(2,1)}, bf16[80,512]{1,0:T(8,128)(2,1)S(1)}, u32[]{:S(2)}, u32[]{:S(2)}) collective-permute-start(bf16[80,512]{1,0:T(8,128)(2,1)} %get-tuple-element.90), channel_id=1, source_target_pairs={{0,16},{8,24},{16,0},{24,8},{1,17},{9,25},{17,1},{25,9},{2,18},{10... | collective-permute-start | bytes 245768 | tf_op jit(solution)/shard_map/ppermute | solution.py:73
  112.4 8.1 %collective-permute-start.30 = (bf16[80,512]{1,0:T(8,128)(2,1)}, bf16[80,512]{1,0:T(8,128)(2,1)S(1)}, u32[]{:S(2)}, u32[]{:S(2)}) collective-permute-start(bf16[80,512]{1,0:T(8,128)(2,1)} %get-tuple-element.91), channel_id=1, source_target_pairs={{0,24},{8,16},{16,8},{24,0},{1,25},{9,17},{17,9},{25,1},{2,26},{10... | collective-permute-start | bytes 245768 | tf_op jit(solution)/shard_map/ppermute | solution.py:73
  121.4 7.2 %collective-permute-start.33 = (bf16[80,512]{1,0:T(8,128)(2,1)S(1)}, bf16[80,512]{1,0:T(8,128)(2,1)S(1)}, u32[]{:S(2)}, u32[]{:S(2)}) collective-permute-start(bf16[80,512]{1,0:T(8,128)(2,1)S(1)} %add_convert_fusion), channel_id=1, source_target_pairs={{0,24},{8,16},{16,8},{24,0},{1,25},{9,17},{17,9},{25,1},{2,26},{10... | collective-permute-start | bytes 245768 | tf_op jit(solution)/shard_map/ppermute | solution.py:73
  123.8 7.5 %collective-permute-start.32 = (bf16[80,512]{1,0:T(8,128)(2,1)S(1)}, bf16[80,512]{1,0:T(8,128)(2,1)S(1)}, u32[]{:S(2)}, u32[]{:S(2)}) collective-permute-start(bf16[80,512]{1,0:T(8,128)(2,1)S(1)} %add_convert_fusion), channel_id=1, source_target_pairs={{0,16},{8,24},{16,0},{24,8},{1,17},{9,25},{17,1},{25,9},{2,18},{10... | collective-permute-start | bytes 245768 | tf_op jit(solution)/shard_map/ppermute | solution.py:73
  124.5 6.9 %collective-permute-start.31 = (bf16[80,512]{1,0:T(8,128)(2,1)S(1)}, bf16[80,512]{1,0:T(8,128)(2,1)S(1)}, u32[]{:S(2)}, u32[]{:S(2)}) collective-permute-start(bf16[80,512]{1,0:T(8,128)(2,1)S(1)} %add_convert_fusion), channel_id=1, source_target_pairs={{0,8},{8,0},{16,24},{24,16},{1,9},{9,1},{17,25},{25,17},{2,10},{10... | collective-permute-start | bytes 245768 | tf_op jit(solution)/shard_map/ppermute | solution.py:73
  131.4 22.3 %copy-start.25 = (s32[2]{0:T(128)S(1)}, s32[2]{0:T(128)}, u32[]{:S(2)}) copy-start(s32[2]{0:T(128)} %copy-done.21) | copy-start | bytes 28
  131.4 11.8 %collective-permute-start.36 = (bf16[320,512]{1,0:T(8,128)(2,1)S(1)}, bf16[320,512]{1,0:T(8,128)(2,1)S(1)}, u32[]{:S(2)}, u32[]{:S(2)}) collective-permute-start(bf16[320,512]{1,0:T(8,128)(2,1)S(1)} %pad_maximum_fusion.refs_1_), channel_id=1, source_target_pairs={{0,6},{1,7},{2,4},{3,5},{4,2},{5,3},{6,0},{7,1},{8,14},{9,15},{10,... | collective-permute-start | bytes 983048 | tf_op jit(solution)/shard_map/ppermute | solution.py:73
  131.5 17.3 %collective-permute-start.35 = (bf16[320,512]{1,0:T(8,128)(2,1)S(1)}, bf16[320,512]{1,0:T(8,128)(2,1)S(1)}, u32[]{:S(2)}, u32[]{:S(2)}) collective-permute-start(bf16[320,512]{1,0:T(8,128)(2,1)S(1)} %pad_maximum_fusion.refs_1_), channel_id=1, source_target_pairs={{0,4},{1,5},{2,6},{3,7},{4,0},{5,1},{6,2},{7,3},{8,12},{9,13},{10,... | collective-permute-start | bytes 983048 | tf_op jit(solution)/shard_map/ppermute | solution.py:73
  133.0 15.8 %collective-permute-start.34 = (bf16[320,512]{1,0:T(8,128)(2,1)S(1)}, bf16[320,512]{1,0:T(8,128)(2,1)S(1)}, u32[]{:S(2)}, u32[]{:S(2)}) collective-permute-start(bf16[320,512]{1,0:T(8,128)(2,1)S(1)} %pad_maximum_fusion.refs_1_), channel_id=1, source_target_pairs={{0,2},{1,3},{2,0},{3,1},{4,6},{5,7},{6,4},{7,5},{8,10},{9,11},{10,... | collective-permute-start | bytes 983048 | tf_op jit(solution)/shard_map/ppermute | solution.py:73
  136.2 13.6 %all-to-all-start.3 = ((bf16[32,4,512]{2,1,0:T(4,128)(2,1)}), bf16[32,4,512]{2,1,0:T(4,128)(2,1)S(1)}, u32[]{:S(2)}, u32[]{:S(2)}) async-start(bf16[32,4,512]{2,1,0:T(4,128)(2,1)} %shard_map.137), calls=%async_computation.3 | async-start | bytes 262144 | tf_op jit(solution)/shard_map/all_to_all | solution.py:644
  149.8 3.9 %collective-permute-start.37 = (bf16[320,512]{1,0:T(8,128)(2,1)S(1)}, bf16[320,512]{1,0:T(8,128)(2,1)S(1)}, u32[]{:S(2)}, u32[]{:S(2)}) collective-permute-start(bf16[320,512]{1,0:T(8,128)(2,1)S(1)} %pad_maximum_fusion.refs_1_), channel_id=1, source_target_pairs={{0,1},{1,0},{2,3},{3,2},{4,5},{5,4},{6,7},{7,6},{8,9},{9,8},{10,11... | collective-permute-start | bytes 983048 | tf_op jit(solution)/shard_map/ppermute | solution.py:73
  149.8 3.9 %collective-permute-start.38 = (bf16[320,512]{1,0:T(8,128)(2,1)S(1)}, bf16[320,512]{1,0:T(8,128)(2,1)S(1)}, u32[]{:S(2)}, u32[]{:S(2)}) collective-permute-start(bf16[320,512]{1,0:T(8,128)(2,1)S(1)} %collective-permute-done.34.refs_2_), channel_id=1, source_target_pairs={{0,1},{1,0},{2,3},{3,2},{4,5},{5,4},{6,7},{7,6},{8,9},{9,8},{10,11... | collective-permute-start | bytes 983048 | tf_op jit(solution)/shard_map/ppermute | solution.py:73
  150.3 3.4 %collective-permute-start.39 = (bf16[320,512]{1,0:T(8,128)(2,1)S(1)}, bf16[320,512]{1,0:T(8,128)(2,1)S(1)}, u32[]{:S(2)}, u32[]{:S(2)}) collective-permute-start(bf16[320,512]{1,0:T(8,128)(2,1)S(1)} %collective-permute-done.35.refs_3_), channel_id=1, source_target_pairs={{0,1},{1,0},{2,3},{3,2},{4,5},{5,4},{6,7},{7,6},{8,9},{9,8},{10,11... | collective-permute-start | bytes 983048 | tf_op jit(solution)/shard_map/ppermute | solution.py:73
  150.3 3.4 %collective-permute-start.40 = (bf16[320,512]{1,0:T(8,128)(2,1)S(1)}, bf16[320,512]{1,0:T(8,128)(2,1)S(1)}, u32[]{:S(2)}, u32[]{:S(2)}) collective-permute-start(bf16[320,512]{1,0:T(8,128)(2,1)S(1)} %collective-permute-done.36.refs_4_), channel_id=1, source_target_pairs={{0,1},{1,0},{2,3},{3,2},{4,5},{5,4},{6,7},{7,6},{8,9},{9,8},{10,11... | collective-permute-start | bytes 983048 | tf_op jit(solution)/shard_map/ppermute | solution.py:73
  (17 other events, 38.1 us)

commit v4 on v3

--- a/solution.py
+++ b/solution.py
@@ -87,17 +87,18 @@
     for step in range(2, count, 2):
         near.append(exchange(block, axis, step))
     if after is not None:
-        near = list(lax.optimization_barrier((*near, *after))[: len(near)])
+        held = lax.optimization_barrier((*near[1:], *after))
+        near = [block, *held[: len(near) - 1]]
     return near + [exchange(piece, axis, 1) for piece in near]
 
 
-def call(kernel, operands, outs, scratch=(), flops=0, scalars=1, limit=24):
+def call(kernel, operands, outs, scratch=(), flops=0, scalars=1, limit=24, place=VMEM):
     moved = sum(x.size * x.dtype.itemsize for x in list(operands) + list(outs))
     return pl.pallas_call(
         kernel,
         out_shape=outs,
         in_specs=[SMEM] * scalars + [VMEM] * (len(operands) - scalars),
-        out_specs=[VMEM] * len(outs),
+        out_specs=[place] * len(outs),
         scratch_shapes=list(scratch),
         cost_estimate=pl.CostEstimate(flops=flops, bytes_accessed=moved, transcendentals=0),
         compiler_params=pltpu.CompilerParams(vmem_limit_bytes=limit << 20),
@@ -415,7 +416,7 @@
 
 def final_kernel(group, count, norm_scale, *refs):
     here_ref, pieces = refs[0], refs[1 : 1 + group]
-    joined_ref, output_ref, piece_scr = refs[1 + group :]
+    joined_ref, output_ref, piece_scr, joined_scr, output_scr, done = refs[1 + group :]
     here, outer = here_ref[0], here_ref[1]
     width = output_ref.shape[0]
     chunk = piece_scr.shape[2]
@@ -430,13 +431,19 @@
     unit = (row == column).astype(f32).astype(low)
     blocks = [piece_scr[n].reshape(5 * share, width) for n in range(group)]
     for n in range(group):
-        output_ref[n * share : (n + 1) * share, :] = blocks[n][:share].astype(f32) * norm_scale
+        output_scr[n * share : (n + 1) * share, :] = blocks[n][:share].astype(f32) * norm_scale
+    copies = [pltpu.make_async_copy(output_scr, output_ref, done.at[4])]
+    copies[0].start()
     gate = jnp.concatenate([block[share : 2 * share] for block in blocks], axis=0)
-    joined_ref[:, :width] = dot(unit, gate, (1, 1)) * norm_scale
     rest = jnp.concatenate([block[2 * share :] for block in blocks], axis=0)
-    for n in range(3):
-        columns = dot(unit, rest[n * width : (n + 1) * width], (1, 1)) * norm_scale
-        joined_ref[:, (n + 1) * width : (n + 2) * width] = columns
+    for n in range(4):
+        rows = gate if n == 0 else rest[(n - 1) * width : n * width]
+        joined_scr[n] = dot(unit, rows, (1, 1)) * norm_scale
+        target = joined_ref.at[:, n * width : (n + 1) * width]
+        copies.append(pltpu.make_async_copy(joined_scr.at[n], target, done.at[n]))
+        copies[-1].start()
+    for copy in copies:
+        copy.wait()
 
 
 def mine_kernel(capacity, stride, here_ref, arrived_ref, mine_ref):
@@ -476,7 +483,13 @@
             functools.partial(final_kernel, group, count, norm_scale),
             [position] + pieces,
             [shaped((width, 4 * width), f32), shaped((width, width), f32)],
-            [pltpu.VMEM((group, count, size, width), low)],
+            [
+                pltpu.VMEM((group, count, size, width), low),
+                pltpu.VMEM((4, width, width), f32),
+                pltpu.VMEM((width, width), f32),
+                pltpu.SemaphoreType.DMA((5,)),
+            ],
+            place=pl.BlockSpec(memory_space=pl.ANY),
         )
     result = jnp.zeros((group, count, size, width), low)
     for step, piece in zip(arrival_order(group), pieces):
@@ -649,7 +662,7 @@
         flops=4 * devices * capacity * hot_count * width,
         limit=56,
     )
-    pieces = gather_pieces(line, "cp", (projection, hot_gradient, cold_gradient))
+    pieces = gather_pieces(line, "cp", (hot_gradient, cold_gradient))
     norm_scale = (tokens * devices) ** (-0.5)
     joined_gradient, output_gradient = assemble(position, pieces, norm_scale, width)
     return (

time: 159 us -> 157 us (0.987)
  transfers between devices with their start and end apart: 44 -> 44, of which waited for: 15 -> 14; matrix products, arithmetic and copies ran while one was open for 1% -> 1% of each run, Pallas kernels for 12% -> 12%
where the time goes in v4:
time: 157 us; the launch traced here: 156 us
  waiting for transfers between devices  46.8 us (30%)
  Pallas kernels  42.8 us (27%)
  starting transfers between devices  42.1 us (27%)
  blocking collectives  14.4 us (9%)
  local copies, waits for them, and re-layouts  7.51 us (5%)
    ppermute x41, waiting for transfers between devices, exchange(): return lax.ppermute(block, axis, pairs)  46.8 us
    pallas_call x13, Pallas kernels, call(): pl.pallas_call(kernel, out_shape=outs, in_specs=[SMEM] * scalars + [VMEM]...  42.8 us
    ppermute x41, starting transfers between devices, exchange(): return lax.ppermute(block, axis, pairs)  32.1 us
    all_to_all x1, blocking collectives, local(): lax.all_to_all(requests, everyone, split_axis=0, concat_axis=0, tiled=True)  14.4 us
    unnamed x74, local copies, waits for them, and re-layouts  6.72 us
    all_to_all x1, starting transfers between devices, local(): lax.all_to_all(sent, everyone, split_axis=0, concat_axis=0, tiled=True)  4.17 us
  transfers between devices with their start and end apart: 44, of which 14 were waited for; matrix products, arithmetic and copies ran while one was open for 1% of the time, Pallas kernels for 12%

profile of v4, /device:TPU:0, one launch (start us, length us, event | category | flops | bytes accessed | tf_op | source)
XLA Modules:
  0.0 156.1 jit_solution(15866610863410925876)
XLA Ops:
  0.8 0.8 copy-done.27
  1.6 0.7 copy-done.28
  2.2 1.0 shard_map.127
  3.2 14.4 %all_to_all.20.asked_ref = s32[32,1,128]{2,1,0:T(1,128)} all-to-all(s32[32,1,128]{2,1,0:T(1,128)S(1)} %get-tuple-element.54), channel_id=1, replica_groups=mesh['dp'=4,'cp'=8] {'dp','cp'}, dimensions={0} | all-to-all | bytes 32768 | tf_op jit(solution)/shard_map/all_to_all | solution.py:545
  17.7 3.4 %shard_map.128 = bf16[1280,128]{1,0:T(8,128)(2,1)} custom-call(s32[2]{0:T(128)} %copy-done.21, s32[32,1,128]{2,1,0:T(1,128)} %all_to_all.20.asked_ref, bf16[512,512]{1,0:T(8,128)(2,1)} %hot_ref.1, bf16[2048,128]{1,0:T(8,128)(2,1)} %cold_ref.1), custom_call_target="tpu_custom_call" | custom-call | bytes 1392648 | tf_op jit(solution)/shard_map/pallas_call | solution.py:97
  21.1 2.7 %all-to-all-start.1 = ((bf16[32,40,128]{2,1,0:T(8,128)(2,1)}), bf16[32,40,128]{2,1,0:T(8,128)(2,1)S(1)}, u32[]{:S(2)}, u32[]{:S(2)}) async-start(bf16[32,40,128]{2,1,0:T(8,128)(2,1)} %bitcast.13), calls=%async_computation.1 | async-start | bytes 655360 | tf_op jit(solution)/shard_map/all_to_all | solution.py:554
  23.8 2.6 %collective-permute-start.2 = (bf16[128,512]{1,0:T(8,128)(2,1)S(1)}, bf16[128,512]{1,0:T(8,128)(2,1)S(1)}, u32[]{:S(2)}, u32[]{:S(2)}) collective-permute-start(bf16[128,512]{1,0:T(8,128)(2,1)S(1)} %copy-done.4), channel_id=1, source_target_pairs={{0,6},{1,7},{2,4},{3,5},{4,2},{5,3},{6,0},{7,1},{8,14},{9,15},{10,... | collective-permute-start | bytes 393224 | tf_op jit(solution)/shard_map/ppermute | solution.py:73
  26.4 0.5 collective-permute-start.1
  27.4 6.4 %collective-permute-done.2.refs_12_ = bf16[128,512]{1,0:T(8,128)(2,1)S(1)} collective-permute-done((bf16[128,512]{1,0:T(8,128)(2,1)S(1)}, bf16[128,512]{1,0:T(8,128)(2,1)S(1)}, u32[]{:S(2)}, u32[]{:S(2)}) %collective-permute-start.2) | collective-permute-done | bytes 131104 | tf_op jit(solution)/shard_map/ppermute | solution.py:73
  33.8 2.6 %collective-permute-done.1.refs_11_ = bf16[128,512]{1,0:T(8,128)(2,1)} collective-permute-done((bf16[128,512]{1,0:T(8,128)(2,1)S(1)}, bf16[128,512]{1,0:T(8,128)(2,1)}, u32[]{:S(2)}, u32[]{:S(2)}) %collective-permute-start.1) | collective-permute-done | bytes 131104 | tf_op jit(solution)/shard_map/ppermute | solution.py:73
  37.0 0.6 copy-done.22
  37.6 1.4 shard_map.129
  39.0 0.7 copy-done.12
  39.6 0.6 copy-done.26
  40.3 1.0 collective-permute-start.9
  41.3 1.5 collective-permute-start.8
  42.8 1.0 collective-permute-start.7
  43.8 3.8 %collective-permute-done.9.refs_4_.refs_20_ = bf16[128,512]{1,0:T(8,128)(2,1)S(1)} collective-permute-done((bf16[128,512]{1,0:T(8,128)(2,1)S(1)}, bf16[128,512]{1,0:T(8,128)(2,1)S(1)}, u32[]{:S(2)}, u32[]{:S(2)}) %collective-permute-start.9) | collective-permute-done | bytes 131104 | tf_op jit(solution)/shard_map/ppermute | solution.py:73
  47.7 1.7 %collective-permute-done.8.refs_3_.refs_19_ = bf16[128,512]{1,0:T(8,128)(2,1)S(1)} collective-permute-done((bf16[128,512]{1,0:T(8,128)(2,1)S(1)}, bf16[128,512]{1,0:T(8,128)(2,1)S(1)}, u32[]{:S(2)}, u32[]{:S(2)}) %collective-permute-start.8) | collective-permute-done | bytes 131104 | tf_op jit(solution)/shard_map/ppermute | solution.py:73
  49.4 0.5 collective-permute-start.11
  49.9 0.6 copy-done.23
  50.5 1.0 shard_map.130
  51.6 5.9 %shard_map.131 = (bf16[128,512]{1,0:T(8,128)(2,1)S(1)}, bf16[128,512]{1,0:T(8,128)(2,1)S(1)}, bf16[128,512]{1,0:T(8,128)(2,1)S(1)}, bf16[8,128,128]{2,1,0:T(8,128)(2,1)S(1)}, bf16[1024,1024]{1,0:T(8,128)(2,1)S(1)}) custom-call(s32[2]{0:T(128)S(1)} %copy-done.23, bf16[128,512]{1,0:T(8,128)(2,1)S(1)} %get-tuple-element.56.normed_ref.refs_1_.refs_17_, ...), custom_call_target="tpu_custom_call" | custom-call | flops 1342177280 | bytes 8126472 | tf_op jit(solution)/shard_map/pallas_call | solution.py:97
  57.6 0.6 copy-done.19
  58.2 1.2 collective-permute-start.16
  59.4 1.4 collective-permute-start.15
  60.8 0.9 collective-permute-start.14
  61.7 3.8 %collective-permute-done.16.refs_4_ = bf16[128,512]{1,0:T(8,128)(2,1)S(1)} collective-permute-done((bf16[128,512]{1,0:T(8,128)(2,1)S(1)}, bf16[128,512]{1,0:T(8,128)(2,1)S(1)}, u32[]{:S(2)}, u32[]{:S(2)}) %collective-permute-start.16) | collective-permute-done | bytes 131104 | tf_op jit(solution)/shard_map/ppermute | solution.py:73
  65.6 1.9 %collective-permute-done.15.refs_3_ = bf16[128,512]{1,0:T(8,128)(2,1)S(1)} collective-permute-done((bf16[128,512]{1,0:T(8,128)(2,1)S(1)}, bf16[128,512]{1,0:T(8,128)(2,1)S(1)}, u32[]{:S(2)}, u32[]{:S(2)}) %collective-permute-start.15) | collective-permute-done | bytes 131104 | tf_op jit(solution)/shard_map/ppermute | solution.py:73
  68.0 6.0 %shard_map.133 = (bf16[128,512]{1,0:T(8,128)(2,1)S(1)}, bf16[1024,512]{1,0:T(8,128)(2,1)S(1)}) custom-call(s32[2]{0:T(128)S(1)} %copy-done.23, bf16[128,512]{1,0:T(8,128)(2,1)S(1)} %get-tuple-element.56.normed_ref.refs_1_.refs_17_, bf16[128,512]{1,0:T(8,128)(2,1)S(1)} %collective-permute-done.7.refs_2_.refs_18_, ...), custom_call_target="tpu_custom_call" | custom-call | flops 402653184 | bytes 8126472 | tf_op jit(solution)/shard_map/pallas_call | solution.py:97
  74.1 4.9 %shard_map.134 = (bf16[128,1536]{1,0:T(8,128)(2,1)S(1)}, bf16[320,128]{1,0:T(8,128)(2,1)S(1)}, bf16[320,128]{1,0:T(8,128)(2,1)S(1)}, bf16[320,128]{1,0:T(8,128)(...) custom-call(s32[2]{0:T(128)S(1)} %copy-done.23, ...), custom_call_target="tpu_custom_call" | custom-call | flops 536870912 | bytes 5111816 | tf_op jit(solution)/shard_map/pallas_call | solution.py:97
  79.0 0.7 copy-done.14
  79.7 0.6 copy-done.20
  80.3 4.9 %shard_map.135 = bf16[1792,128]{1,0:T(8,128)(2,1)} custom-call(s32[2]{0:T(128)} %copy-done.21, bf16[128,512]{1,0:T(8,128)(2,1)} %copy-done.18, bf16[128,1536]{1,0:T(8,128)(2,1)} %copy-done.14, bf16[512,2048]{1,0:T(8,128)(2,1)} %refs_3_.1, f32[128,512]{1,0:T(8,128)} %copy-done.12, bf16[128,512]{1,0:T(8,128)(2,1)} %refs_9_.4, bf16[128,128]{1,0:T(8,128)(2,1)} %copy-done.26, ...), custom_call_target="tpu_custom_call" | custom-call | flops 268435456 | bytes 3638792 | tf_op jit(solution)/shard_map/pallas_call | solution.py:97
  85.2 4.2 %all-to-all-start.2 = ((bf16[32,56,128]{2,1,0:T(8,128)(2,1)}), bf16[32,56,128]{2,1,0:T(8,128)(2,1)S(1)}, u32[]{:S(2)}, u32[]{:S(2)}) async-start(bf16[32,56,128]{2,1,0:T(8,128)(2,1)} %bitcast.12), calls=%async_computation.2 | async-start | bytes 917504 | tf_op jit(solution)/shard_map/all_to_all | solution.py:627
  89.4 1.8 %collective-permute-start.21 = (bf16[320,128]{1,0:T(8,128)(2,1)S(1)}, bf16[320,128]{1,0:T(8,128)(2,1)S(1)}, u32[]{:S(2)}, u32[]{:S(2)}) collective-permute-start(bf16[320,128]{1,0:T(8,128)(2,1)S(1)} %get-tuple-element.72), channel_id=1, source_target_pairs={{0,2},{1,3},{2,0},{3,1},{4,6},{5,7},{6,4},{7,5},{8,10},{9,11},{10,... | collective-permute-start | bytes 245768 | tf_op jit(solution)/shard_map/ppermute | solution.py:73
  91.3 1.5 collective-permute-start.22
  93.0 1.9 %collective-permute-start.25 = (bf16[320,128]{1,0:T(8,128)(2,1)S(1)}, bf16[320,128]{1,0:T(8,128)(2,1)S(1)}, u32[]{:S(2)}, u32[]{:S(2)}) collective-permute-start(bf16[320,128]{1,0:T(8,128)(2,1)S(1)} %get-tuple-element.76), channel_id=1, source_target_pairs={{0,3},{1,2},{2,1},{3,0},{4,7},{5,6},{6,5},{7,4},{8,11},{9,10},{10,... | collective-permute-start | bytes 245768 | tf_op jit(solution)/shard_map/ppermute | solution.py:73
  94.9 3.4 %collective-permute-done.21.refs_2_ = bf16[320,128]{1,0:T(8,128)(2,1)S(1)} collective-permute-done((bf16[320,128]{1,0:T(8,128)(2,1)S(1)}, bf16[320,128]{1,0:T(8,128)(2,1)S(1)}, u32[]{:S(2)}, u32[]{:S(2)}) %collective-permute-start.21) | collective-permute-done | bytes 81952 | tf_op jit(solution)/shard_map/ppermute | solution.py:73
  98.3 1.5 collective-permute-start.27
  99.8 1.8 %collective-permute-done.23.refs_4_ = bf16[320,128]{1,0:T(8,128)(2,1)S(1)} collective-permute-done((bf16[320,128]{1,0:T(8,128)(2,1)S(1)}, bf16[320,128]{1,0:T(8,128)(2,1)S(1)}, u32[]{:S(2)}, u32[]{:S(2)}) %collective-permute-start.23) | collective-permute-done | bytes 81952 | tf_op jit(solution)/shard_map/ppermute | solution.py:73
  101.6 3.9 %collective-permute-done.26.refs_7_ = bf16[320,128]{1,0:T(8,128)(2,1)S(1)} collective-permute-done((bf16[320,128]{1,0:T(8,128)(2,1)S(1)}, bf16[320,128]{1,0:T(8,128)(2,1)S(1)}, u32[]{:S(2)}, u32[]{:S(2)}) %collective-permute-start.26) | collective-permute-done | bytes 81952 | tf_op jit(solution)/shard_map/ppermute | solution.py:73
  105.6 0.6 copy-done.35
  106.2 3.4 %shard_map.138 = (f32[80,512]{1,0:T(8,128)}, bf16[80,512]{1,0:T(8,128)(2,1)}, bf16[80,512]{1,0:T(8,128)(2,1)}, bf16[80,512]{1,0:T(8,128)(2,1)}) custom-call(s32[2]{0:T(128)} %copy-done.21, bf16[320,128]{1,0:T(8,128)(2,1)} %copy-done.20, bf16[320,128]{1,0:T(8,128)(2,1)} %copy-done.30, bf16[320,128]{1,0:T(8,128)(2,1)} %copy-done.31, ...), custom_call_target="tpu_custom_call" | custom-call | flops 335544320 | bytes 3162120 | tf_op jit(solution)/shard_map/pallas_call | solution.py:97
  109.6 1.3 collective-permute-start.28
  110.8 1.6 collective-permute-start.29
  112.4 1.6 %collective-permute-start.30 = (bf16[80,512]{1,0:T(8,128)(2,1)}, bf16[80,512]{1,0:T(8,128)(2,1)S(1)}, u32[]{:S(2)}, u32[]{:S(2)}) collective-permute-start(bf16[80,512]{1,0:T(8,128)(2,1)} %get-tuple-element.90), channel_id=1, source_target_pairs={{0,24},{8,16},{16,8},{24,0},{1,25},{9,17},{17,9},{25,1},{2,26},{10... | collective-permute-start | bytes 245768 | tf_op jit(solution)/shard_map/ppermute | solution.py:73
  114.3 6.2 %collective-permute-done.29 = bf16[80,512]{1,0:T(8,128)(2,1)S(1)} collective-permute-done((bf16[80,512]{1,0:T(8,128)(2,1)}, bf16[80,512]{1,0:T(8,128)(2,1)S(1)}, u32[]{:S(2)}, u32[]{:S(2)}) %collective-permute-start.29) | collective-permute-done | bytes 81952 | tf_op jit(solution)/shard_map/ppermute | solution.py:73
  120.5 1.0 add_convert_fusion
  121.4 2.4 %collective-permute-start.33 = (bf16[80,512]{1,0:T(8,128)(2,1)S(1)}, bf16[80,512]{1,0:T(8,128)(2,1)S(1)}, u32[]{:S(2)}, u32[]{:S(2)}) collective-permute-start(bf16[80,512]{1,0:T(8,128)(2,1)S(1)} %add_convert_fusion), channel_id=1, source_target_pairs={{0,24},{8,16},{16,8},{24,0},{1,25},{9,17},{17,9},{25,1},{2,26},{10... | collective-permute-start | bytes 245768 | tf_op jit(solution)/shard_map/ppermute | solution.py:73
  123.8 0.6 collective-permute-start.32
  124.5 1.4 collective-permute-start.31
  125.9 2.8 %collective-permute-done.33 = bf16[80,512]{1,0:T(8,128)(2,1)S(1)} collective-permute-done((bf16[80,512]{1,0:T(8,128)(2,1)S(1)}, bf16[80,512]{1,0:T(8,128)(2,1)S(1)}, u32[]{:S(2)}, u32[]{:S(2)}) %collective-permute-start.33) | collective-permute-done | bytes 81952 | tf_op jit(solution)/shard_map/ppermute | solution.py:73
  128.7 2.7 %collective-permute-done.32 = bf16[80,512]{1,0:T(8,128)(2,1)S(1)} collective-permute-done((bf16[80,512]{1,0:T(8,128)(2,1)S(1)}, bf16[80,512]{1,0:T(8,128)(2,1)S(1)}, u32[]{:S(2)}, u32[]{:S(2)}) %collective-permute-start.32) | collective-permute-done | bytes 81952 | tf_op jit(solution)/shard_map/ppermute | solution.py:73
  131.5 1.5 collective-permute-start.35
  133.0 2.0 %collective-permute-start.34 = (bf16[320,512]{1,0:T(8,128)(2,1)S(1)}, bf16[320,512]{1,0:T(8,128)(2,1)S(1)}, u32[]{:S(2)}, u32[]{:S(2)}) collective-permute-start(bf16[320,512]{1,0:T(8,128)(2,1)S(1)} %pad_maximum_fusion.refs_1_), channel_id=1, source_target_pairs={{0,2},{1,3},{2,0},{3,1},{4,6},{5,7},{6,4},{7,5},{8,10},{9,11},{10,... | collective-permute-start | bytes 983048 | tf_op jit(solution)/shard_map/ppermute | solution.py:73
  135.0 1.2 shard_map.137
  136.2 3.1 %all-to-all-start.3 = ((bf16[32,4,512]{2,1,0:T(4,128)(2,1)}), bf16[32,4,512]{2,1,0:T(4,128)(2,1)S(1)}, u32[]{:S(2)}, u32[]{:S(2)}) async-start(bf16[32,4,512]{2,1,0:T(4,128)(2,1)} %shard_map.137), calls=%async_computation.3 | async-start | bytes 262144 | tf_op jit(solution)/shard_map/all_to_all | solution.py:657
  139.4 3.9 %shard_map.136 = (f32[512,512]{1,0:T(8,128)}, f32[2048,128]{1,0:T(8,128)}) custom-call(s32[2]{0:T(128)} %copy-done.21, s32[32,1,128]{2,1,0:T(1,128)} %all_to_all.20.asked_ref, bf16[1792,128]{1,0:T(8,128)(2,1)} %bitcast.8), custom_call_target="tpu_custom_call" | custom-call | flops 335544320 | bytes 2572296 | tf_op jit(solution)/shard_map/pallas_call | solution.py:97
  143.4 5.4 %collective-permute-done.35.refs_3_ = bf16[320,512]{1,0:T(8,128)(2,1)S(1)} collective-permute-done((bf16[320,512]{1,0:T(8,128)(2,1)S(1)}, bf16[320,512]{1,0:T(8,128)(2,1)S(1)}, u32[]{:S(2)}, u32[]{:S(2)}) %collective-permute-start.35) | collective-permute-done | bytes 327712 | tf_op jit(solution)/shard_map/ppermute | solution.py:73
  148.8 0.5 collective-permute-start.39
  149.3 2.0 %shard_map.132 = bf16[128,512]{1,0:T(8,128)(2,1)} custom-call(s32[2]{0:T(128)} %copy-done.21, bf16[128,512]{1,0:T(8,128)(2,1)} %copy-done.19, bf16[512,512]{1,0:T(8,128)(2,1)} %mix_ref.1, f32[128,512]{1,0:T(8,128)} %copy-done.12), custom_call_target="tpu_custom_call" | custom-call | bytes 1048584 | tf_op jit(solution)/shard_map/pallas_call | solution.py:97
  151.4 0.8 mul.11
  152.2 3.7 %shard_map.139 = (f32[512,2048]{1,0:T(8,128)}, f32[512,512]{1,0:T(8,128)}) custom-call(s32[2]{0:T(128)S(1)} %copy-done.25, bf16[320,512]{1,0:T(8,128)(2,1)S(1)} %pad_maximum_fusion.refs_1_, bf16[320,512]{1,0:T(8,128)(2,1)S(1)} %collective-permute-done.34.refs_2_, bf16[320,512]{1,0:T(8,128)(2,1)S(1)} %collective-permute-done.35.refs_3_, ...), custom_call_target="tpu_custom_call" | custom-call | bytes 7864328 | tf_op jit(solution)/shard_map/pallas_call | solution.py:97
  (117 shorter events, 2.5 us)
Async XLA Ops:
  0.6 23.2 %copy-start.4 = (bf16[128,512]{1,0:T(8,128)(2,1)S(1)}, bf16[128,512]{1,0:T(8,128)(2,1)}, u32[]{:S(2)}) copy-start(bf16[128,512]{1,0:T(8,128)(2,1)} %refs_9_.4) | copy-start | bytes 393220
  0.6 36.3 %copy-start.13 = (bf16[128,512]{1,0:T(8,128)(2,1)S(1)}, bf16[128,512]{1,0:T(8,128)(2,1)}, u32[]{:S(2)}) copy-start(bf16[128,512]{1,0:T(8,128)(2,1)} %refs_10_.1) | copy-start | bytes 393220
  0.7 49.2 %copy-start = (bf16[512,2048]{1,0:T(8,128)(2,1)S(1)}, bf16[512,2048]{1,0:T(8,128)(2,1)}, u32[]{:S(2)}) copy-start(bf16[512,2048]{1,0:T(8,128)(2,1)} %refs_3_.1) | copy-start | bytes 6291460
  0.7 16.9 %copy-start.21 = (s32[2]{0:T(128)}, s32[2]{0:T(128)S(1)}, u32[]{:S(2)}) copy-start(s32[2]{0:T(128)S(1)} %pad_add_fusion.here_ref.refs_0_) | copy-start | bytes 28
  3.2 39.6 %copy-start.16 = (s32[128,1]{1,0:T(8,128)}, s32[128,1]{1,0:T(8,128)S(1)}, u32[]{:S(2)}) copy-start(s32[128,1]{1,0:T(8,128)S(1)} %get-tuple-element.53.refs_3_.refs_9_) | copy-start | bytes 1540
  3.2 39.6 %copy-start.17 = (s32[128,1]{1,0:T(8,128)}, s32[128,1]{1,0:T(8,128)S(1)}, u32[]{:S(2)}) copy-start(s32[128,1]{1,0:T(8,128)S(1)} %get-tuple-element.51.refs_1_.refs_7_) | copy-start | bytes 1540
  3.2 48.3 %copy-start.15 = (s32[128,1]{1,0:T(8,128)}, s32[128,1]{1,0:T(8,128)S(1)}, u32[]{:S(2)}) copy-start(s32[128,1]{1,0:T(8,128)S(1)} %get-tuple-element.52.refs_2_.refs_8_) | copy-start | bytes 1540
  21.1 30.6 %copy-start.2 = (bf16[512,512]{1,0:T(8,128)(2,1)S(1)}, bf16[512,512]{1,0:T(8,128)(2,1)}, u32[]{:S(2)}) copy-start(bf16[512,512]{1,0:T(8,128)(2,1)} %mix_ref.1) | copy-start | bytes 1572868
  21.1 15.9 %all-to-all-start.1 = ((bf16[32,40,128]{2,1,0:T(8,128)(2,1)}), bf16[32,40,128]{2,1,0:T(8,128)(2,1)S(1)}, u32[]{:S(2)}, u32[]{:S(2)}) async-start(bf16[32,40,128]{2,1,0:T(8,128)(2,1)} %bitcast.13), calls=%async_computation.1 | async-start | bytes 655360 | tf_op jit(solution)/shard_map/all_to_all | solution.py:554
  23.8 10.0 %collective-permute-start.2 = (bf16[128,512]{1,0:T(8,128)(2,1)S(1)}, bf16[128,512]{1,0:T(8,128)(2,1)S(1)}, u32[]{:S(2)}, u32[]{:S(2)}) collective-permute-start(bf16[128,512]{1,0:T(8,128)(2,1)S(1)} %copy-done.4), channel_id=1, source_target_pairs={{0,6},{1,7},{2,4},{3,5},{4,2},{5,3},{6,0},{7,1},{8,14},{9,15},{10,... | collective-permute-start | bytes 393224 | tf_op jit(solution)/shard_map/ppermute | solution.py:73
  26.4 10.0 %collective-permute-start.1 = (bf16[128,512]{1,0:T(8,128)(2,1)S(1)}, bf16[128,512]{1,0:T(8,128)(2,1)}, u32[]{:S(2)}, u32[]{:S(2)}) collective-permute-start(bf16[128,512]{1,0:T(8,128)(2,1)S(1)} %copy-done.4), channel_id=1, source_target_pairs={{0,4},{1,5},{2,6},{3,7},{4,0},{5,1},{6,2},{7,3},{8,12},{9,13},{10,... | collective-permute-start | bytes 393224 | tf_op jit(solution)/shard_map/ppermute | solution.py:73
  27.0 9.5 %collective-permute-start = (bf16[128,512]{1,0:T(8,128)(2,1)S(1)}, bf16[128,512]{1,0:T(8,128)(2,1)}, u32[]{:S(2)}, u32[]{:S(2)}) collective-permute-start(bf16[128,512]{1,0:T(8,128)(2,1)S(1)} %copy-done.4), channel_id=1, source_target_pairs={{0,2},{1,3},{2,0},{3,1},{4,6},{5,7},{6,4},{7,5},{8,10},{9,11},{10,... | collective-permute-start | bytes 393224 | tf_op jit(solution)/shard_map/ppermute | solution.py:73
  27.4 12.9 %collective-permute-start.3 = (bf16[128,512]{1,0:T(8,128)(2,1)S(1)}, bf16[128,512]{1,0:T(8,128)(2,1)}, u32[]{:S(2)}, u32[]{:S(2)}) collective-permute-start(bf16[128,512]{1,0:T(8,128)(2,1)S(1)} %copy-done.4), channel_id=1, source_target_pairs={{0,1},{1,0},{2,3},{3,2},{4,5},{5,4},{6,7},{7,6},{8,9},{9,8},{10,11... | collective-permute-start | bytes 393224 | tf_op jit(solution)/shard_map/ppermute | solution.py:73
  33.8 23.8 %copy-start.29 = (bf16[128,512]{1,0:T(8,128)(2,1)}, bf16[128,512]{1,0:T(8,128)(2,1)S(1)}, u32[]{:S(2)}) copy-start(bf16[128,512]{1,0:T(8,128)(2,1)S(1)} %collective-permute-done.2.refs_12_) | copy-start | bytes 393220
  33.8 6.5 %collective-permute-start.6 = (bf16[128,512]{1,0:T(8,128)(2,1)S(1)}, bf16[128,512]{1,0:T(8,128)(2,1)}, u32[]{:S(2)}, u32[]{:S(2)}) collective-permute-start(bf16[128,512]{1,0:T(8,128)(2,1)S(1)} %collective-permute-done.2.refs_12_), channel_id=1, source_target_pairs={{0,1},{1,0},{2,3},{3,2},{4,5},{5,4},{6,7},{7,6},{8,9},{9,8},{10,11... | collective-permute-start | bytes 393224 | tf_op jit(solution)/shard_map/ppermute | solution.py:73
  36.4 3.8 %collective-permute-start.5 = (bf16[128,512]{1,0:T(8,128)(2,1)}, bf16[128,512]{1,0:T(8,128)(2,1)}, u32[]{:S(2)}, u32[]{:S(2)}) collective-permute-start(bf16[128,512]{1,0:T(8,128)(2,1)} %collective-permute-done.1.refs_11_), channel_id=1, source_target_pairs={{0,1},{1,0},{2,3},{3,2},{4,5},{5,4},{6,7},{7,6},{8,9},{9,8},{10,11... | collective-permute-start | bytes 393224 | tf_op jit(solution)/shard_map/ppermute | solution.py:73
  36.5 3.8 %collective-permute-start.4 = (bf16[128,512]{1,0:T(8,128)(2,1)}, bf16[128,512]{1,0:T(8,128)(2,1)}, u32[]{:S(2)}, u32[]{:S(2)}) collective-permute-start(bf16[128,512]{1,0:T(8,128)(2,1)} %collective-permute-done.refs_10_), channel_id=1, source_target_pairs={{0,1},{1,0},{2,3},{3,2},{4,5},{5,4},{6,7},{7,6},{8,9},{9,8},{10,11... | collective-permute-start | bytes 393224 | tf_op jit(solution)/shard_map/ppermute | solution.py:73
  40.2 27.7 %copy-start.1 = (bf16[128,512]{1,0:T(8,128)(2,1)}, bf16[128,512]{1,0:T(8,128)(2,1)S(1)}, u32[]{:S(2)}) copy-start(bf16[128,512]{1,0:T(8,128)(2,1)S(1)} %get-tuple-element.56.normed_ref.refs_1_.refs_17_) | copy-start | bytes 393220
  40.3 7.4 %collective-permute-start.9 = (bf16[128,512]{1,0:T(8,128)(2,1)S(1)}, bf16[128,512]{1,0:T(8,128)(2,1)S(1)}, u32[]{:S(2)}, u32[]{:S(2)}) collective-permute-start(bf16[128,512]{1,0:T(8,128)(2,1)S(1)} %get-tuple-element.56.normed_ref.refs_1_.refs_17_), channel_id=1, source_target_pairs={{0,6},{1,7},{2,4},{3,5},{4,2},{5,3},{6,0},{7,1},{8,14},{9,15},{10,... | collective-permute-start | bytes 393224 | tf_op jit(solution)/shard_map/ppermute | solution.py:73
  41.3 8.1 %collective-permute-start.8 = (bf16[128,512]{1,0:T(8,128)(2,1)S(1)}, bf16[128,512]{1,0:T(8,128)(2,1)S(1)}, u32[]{:S(2)}, u32[]{:S(2)}) collective-permute-start(bf16[128,512]{1,0:T(8,128)(2,1)S(1)} %get-tuple-element.56.normed_ref.refs_1_.refs_17_), channel_id=1, source_target_pairs={{0,4},{1,5},{2,6},{3,7},{4,0},{5,1},{6,2},{7,3},{8,12},{9,13},{10,... | collective-permute-start | bytes 393224 | tf_op jit(solution)/shard_map/ppermute | solution.py:73
  42.8 6.6 %collective-permute-start.7 = (bf16[128,512]{1,0:T(8,128)(2,1)S(1)}, bf16[128,512]{1,0:T(8,128)(2,1)S(1)}, u32[]{:S(2)}, u32[]{:S(2)}) collective-permute-start(bf16[128,512]{1,0:T(8,128)(2,1)S(1)} %get-tuple-element.56.normed_ref.refs_1_.refs_17_), channel_id=1, source_target_pairs={{0,2},{1,3},{2,0},{3,1},{4,6},{5,7},{6,4},{7,5},{8,10},{9,11},{10,... | collective-permute-start | bytes 393224 | tf_op jit(solution)/shard_map/ppermute | solution.py:73
  43.8 7.7 %collective-permute-start.10 = (bf16[128,512]{1,0:T(8,128)(2,1)S(1)}, bf16[128,512]{1,0:T(8,128)(2,1)S(1)}, u32[]{:S(2)}, u32[]{:S(2)}) collective-permute-start(bf16[128,512]{1,0:T(8,128)(2,1)S(1)} %get-tuple-element.56.normed_ref.refs_1_.refs_17_), channel_id=1, source_target_pairs={{0,1},{1,0},{2,3},{3,2},{4,5},{5,4},{6,7},{7,6},{8,9},{9,8},{10,11... | collective-permute-start | bytes 393224 | tf_op jit(solution)/shard_map/ppermute | solution.py:73
  47.7 20.3 %copy-start.5 = (bf16[128,512]{1,0:T(8,128)(2,1)}, bf16[128,512]{1,0:T(8,128)(2,1)S(1)}, u32[]{:S(2)}) copy-start(bf16[128,512]{1,0:T(8,128)(2,1)S(1)} %collective-permute-done.9.refs_4_.refs_20_) | copy-start | bytes 393220
  47.7 3.9 %collective-permute-start.13 = (bf16[128,512]{1,0:T(8,128)(2,1)S(1)}, bf16[128,512]{1,0:T(8,128)(2,1)S(1)}, u32[]{:S(2)}, u32[]{:S(2)}) collective-permute-start(bf16[128,512]{1,0:T(8,128)(2,1)S(1)} %collective-permute-done.9.refs_4_.refs_20_), channel_id=1, source_target_pairs={{0,1},{1,0},{2,3},{3,2},{4,5},{5,4},{6,7},{7,6},{8,9},{9,8},{10,11... | collective-permute-start | bytes 393224 | tf_op jit(solution)/shard_map/ppermute | solution.py:73
  49.4 18.6 %copy-start.6 = (bf16[128,512]{1,0:T(8,128)(2,1)}, bf16[128,512]{1,0:T(8,128)(2,1)S(1)}, u32[]{:S(2)}) copy-start(bf16[128,512]{1,0:T(8,128)(2,1)S(1)} %collective-permute-done.8.refs_3_.refs_19_) | copy-start | bytes 393220
  49.4 2.2 %collective-permute-start.12 = (bf16[128,512]{1,0:T(8,128)(2,1)S(1)}, bf16[128,512]{1,0:T(8,128)(2,1)S(1)}, u32[]{:S(2)}, u32[]{:S(2)}) collective-permute-start(bf16[128,512]{1,0:T(8,128)(2,1)S(1)} %collective-permute-done.8.refs_3_.refs_19_), channel_id=1, source_target_pairs={{0,1},{1,0},{2,3},{3,2},{4,5},{5,4},{6,7},{7,6},{8,9},{9,8},{10,11... | collective-permute-start | bytes 393224 | tf_op jit(solution)/shard_map/ppermute | solution.py:73
  49.4 18.6 %copy-start.7 = (bf16[128,512]{1,0:T(8,128)(2,1)}, bf16[128,512]{1,0:T(8,128)(2,1)S(1)}, u32[]{:S(2)}) copy-start(bf16[128,512]{1,0:T(8,128)(2,1)S(1)} %collective-permute-done.7.refs_2_.refs_18_) | copy-start | bytes 393220
  49.4 2.2 %collective-permute-start.11 = (bf16[128,512]{1,0:T(8,128)(2,1)S(1)}, bf16[128,512]{1,0:T(8,128)(2,1)S(1)}, u32[]{:S(2)}, u32[]{:S(2)}) collective-permute-start(bf16[128,512]{1,0:T(8,128)(2,1)S(1)} %collective-permute-done.7.refs_2_.refs_18_), channel_id=1, source_target_pairs={{0,1},{1,0},{2,3},{3,2},{4,5},{5,4},{6,7},{7,6},{8,9},{9,8},{10,11... | collective-permute-start | bytes 393224 | tf_op jit(solution)/shard_map/ppermute | solution.py:73
  51.6 16.4 %copy-start.8 = (bf16[128,512]{1,0:T(8,128)(2,1)}, bf16[128,512]{1,0:T(8,128)(2,1)S(1)}, u32[]{:S(2)}) copy-start(bf16[128,512]{1,0:T(8,128)(2,1)S(1)} %collective-permute-done.10.refs_5_.refs_21_) | copy-start | bytes 393220
  51.6 16.4 %copy-start.9 = (bf16[128,512]{1,0:T(8,128)(2,1)}, bf16[128,512]{1,0:T(8,128)(2,1)S(1)}, u32[]{:S(2)}) copy-start(bf16[128,512]{1,0:T(8,128)(2,1)S(1)} %collective-permute-done.13.refs_8_.refs_24_) | copy-start | bytes 393220
  51.6 16.4 %copy-start.10 = (bf16[128,512]{1,0:T(8,128)(2,1)}, bf16[128,512]{1,0:T(8,128)(2,1)S(1)}, u32[]{:S(2)}) copy-start(bf16[128,512]{1,0:T(8,128)(2,1)S(1)} %collective-permute-done.12.refs_7_.refs_23_) | copy-start | bytes 393220
  51.6 16.4 %copy-start.11 = (bf16[128,512]{1,0:T(8,128)(2,1)}, bf16[128,512]{1,0:T(8,128)(2,1)S(1)}, u32[]{:S(2)}) copy-start(bf16[128,512]{1,0:T(8,128)(2,1)S(1)} %collective-permute-done.11.refs_6_.refs_22_) | copy-start | bytes 393220
  58.2 15.8 %copy-start.18 = (bf16[128,512]{1,0:T(8,128)(2,1)}, bf16[128,512]{1,0:T(8,128)(2,1)S(1)}, u32[]{:S(2)}) copy-start(bf16[128,512]{1,0:T(8,128)(2,1)S(1)} %get-tuple-element.61.refs_1_) | copy-start | bytes 393220
  58.2 7.3 %collective-permute-start.16 = (bf16[128,512]{1,0:T(8,128)(2,1)S(1)}, bf16[128,512]{1,0:T(8,128)(2,1)S(1)}, u32[]{:S(2)}, u32[]{:S(2)}) collective-permute-start(bf16[128,512]{1,0:T(8,128)(2,1)S(1)} %get-tuple-element.62.refs_12_.refs_1_), channel_id=1, source_target_pairs={{0,6},{1,7},{2,4},{3,5},{4,2},{5,3},{6,0},{7,1},{8,14},{9,15},{10,... | collective-permute-start | bytes 393224 | tf_op jit(solution)/shard_map/ppermute | solution.py:73
  59.4 8.0 %collective-permute-start.15 = (bf16[128,512]{1,0:T(8,128)(2,1)S(1)}, bf16[128,512]{1,0:T(8,128)(2,1)S(1)}, u32[]{:S(2)}, u32[]{:S(2)}) collective-permute-start(bf16[128,512]{1,0:T(8,128)(2,1)S(1)} %get-tuple-element.62.refs_12_.refs_1_), channel_id=1, source_target_pairs={{0,4},{1,5},{2,6},{3,7},{4,0},{5,1},{6,2},{7,3},{8,12},{9,13},{10,... | collective-permute-start | bytes 393224 | tf_op jit(solution)/shard_map/ppermute | solution.py:73
  60.8 6.7 %collective-permute-start.14 = (bf16[128,512]{1,0:T(8,128)(2,1)S(1)}, bf16[128,512]{1,0:T(8,128)(2,1)S(1)}, u32[]{:S(2)}, u32[]{:S(2)}) collective-permute-start(bf16[128,512]{1,0:T(8,128)(2,1)S(1)} %get-tuple-element.62.refs_12_.refs_1_), channel_id=1, source_target_pairs={{0,2},{1,3},{2,0},{3,1},{4,6},{5,7},{6,4},{7,5},{8,10},{9,11},{10,... | collective-permute-start | bytes 393224 | tf_op jit(solution)/shard_map/ppermute | solution.py:73
  61.7 12.3 %collective-permute-start.17 = (bf16[128,512]{1,0:T(8,128)(2,1)S(1)}, bf16[128,512]{1,0:T(8,128)(2,1)S(1)}, u32[]{:S(2)}, u32[]{:S(2)}) collective-permute-start(bf16[128,512]{1,0:T(8,128)(2,1)S(1)} %get-tuple-element.62.refs_12_.refs_1_), channel_id=1, source_target_pairs={{0,1},{1,0},{2,3},{3,2},{4,5},{5,4},{6,7},{7,6},{8,9},{9,8},{10,11... | collective-permute-start | bytes 393224 | tf_op jit(solution)/shard_map/ppermute | solution.py:73
  65.5 8.5 %collective-permute-start.20 = (bf16[128,512]{1,0:T(8,128)(2,1)S(1)}, bf16[128,512]{1,0:T(8,128)(2,1)S(1)}, u32[]{:S(2)}, u32[]{:S(2)}) collective-permute-start(bf16[128,512]{1,0:T(8,128)(2,1)S(1)} %collective-permute-done.16.refs_4_), channel_id=1, source_target_pairs={{0,1},{1,0},{2,3},{3,2},{4,5},{5,4},{6,7},{7,6},{8,9},{9,8},{10,11... | collective-permute-start | bytes 393224 | tf_op jit(solution)/shard_map/ppermute | solution.py:73
  67.4 6.6 %collective-permute-start.19 = (bf16[128,512]{1,0:T(8,128)(2,1)S(1)}, bf16[128,512]{1,0:T(8,128)(2,1)S(1)}, u32[]{:S(2)}, u32[]{:S(2)}) collective-permute-start(bf16[128,512]{1,0:T(8,128)(2,1)S(1)} %collective-permute-done.15.refs_3_), channel_id=1, source_target_pairs={{0,1},{1,0},{2,3},{3,2},{4,5},{5,4},{6,7},{7,6},{8,9},{9,8},{10,11... | collective-permute-start | bytes 393224 | tf_op jit(solution)/shard_map/ppermute | solution.py:73
  67.4 6.6 %collective-permute-start.18 = (bf16[128,512]{1,0:T(8,128)(2,1)S(1)}, bf16[128,512]{1,0:T(8,128)(2,1)S(1)}, u32[]{:S(2)}, u32[]{:S(2)}) collective-permute-start(bf16[128,512]{1,0:T(8,128)(2,1)S(1)} %collective-permute-done.14.refs_2_), channel_id=1, source_target_pairs={{0,1},{1,0},{2,3},{3,2},{4,5},{5,4},{6,7},{7,6},{8,9},{9,8},{10,11... | collective-permute-start | bytes 393224 | tf_op jit(solution)/shard_map/ppermute | solution.py:73
  85.2 49.7 %all-to-all-start.2 = ((bf16[32,56,128]{2,1,0:T(8,128)(2,1)}), bf16[32,56,128]{2,1,0:T(8,128)(2,1)S(1)}, u32[]{:S(2)}, u32[]{:S(2)}) async-start(bf16[32,56,128]{2,1,0:T(8,128)(2,1)} %bitcast.12), calls=%async_computation.2 | async-start | bytes 917504 | tf_op jit(solution)/shard_map/all_to_all | solution.py:627
  89.4 45.6 %copy-start.24 = (s32[2]{0:T(128)S(1)}, s32[2]{0:T(128)}, u32[]{:S(2)}) copy-start(s32[2]{0:T(128)} %copy-done.21) | copy-start | bytes 28
  89.4 8.8 %collective-permute-start.21 = (bf16[320,128]{1,0:T(8,128)(2,1)S(1)}, bf16[320,128]{1,0:T(8,128)(2,1)S(1)}, u32[]{:S(2)}, u32[]{:S(2)}) collective-permute-start(bf16[320,128]{1,0:T(8,128)(2,1)S(1)} %get-tuple-element.72), channel_id=1, source_target_pairs={{0,2},{1,3},{2,0},{3,1},{4,6},{5,7},{6,4},{7,5},{8,10},{9,11},{10,... | collective-permute-start | bytes 245768 | tf_op jit(solution)/shard_map/ppermute | solution.py:73
  91.3 7.0 %collective-permute-start.22 = (bf16[320,128]{1,0:T(8,128)(2,1)S(1)}, bf16[320,128]{1,0:T(8,128)(2,1)S(1)}, u32[]{:S(2)}, u32[]{:S(2)}) collective-permute-start(bf16[320,128]{1,0:T(8,128)(2,1)S(1)} %get-tuple-element.73), channel_id=1, source_target_pairs={{0,4},{1,5},{2,6},{3,7},{4,0},{5,1},{6,2},{7,3},{8,12},{9,13},{10,... | collective-permute-start | bytes 245768 | tf_op jit(solution)/shard_map/ppermute | solution.py:73
  92.7 8.8 %collective-permute-start.23 = (bf16[320,128]{1,0:T(8,128)(2,1)S(1)}, bf16[320,128]{1,0:T(8,128)(2,1)S(1)}, u32[]{:S(2)}, u32[]{:S(2)}) collective-permute-start(bf16[320,128]{1,0:T(8,128)(2,1)S(1)} %get-tuple-element.74), channel_id=1, source_target_pairs={{0,6},{1,7},{2,4},{3,5},{4,2},{5,3},{6,0},{7,1},{8,14},{9,15},{10,... | collective-permute-start | bytes 245768 | tf_op jit(solution)/shard_map/ppermute | solution.py:73
  93.0 8.6 %collective-permute-start.24 = (bf16[320,128]{1,0:T(8,128)(2,1)S(1)}, bf16[320,128]{1,0:T(8,128)(2,1)S(1)}, u32[]{:S(2)}, u32[]{:S(2)}) collective-permute-start(bf16[320,128]{1,0:T(8,128)(2,1)S(1)} %get-tuple-element.75), channel_id=1, source_target_pairs={{0,1},{1,0},{2,3},{3,2},{4,5},{5,4},{6,7},{7,6},{8,9},{9,8},{10,11... | collective-permute-start | bytes 245768 | tf_op jit(solution)/shard_map/ppermute | solution.py:73
  93.0 8.6 %collective-permute-start.25 = (bf16[320,128]{1,0:T(8,128)(2,1)S(1)}, bf16[320,128]{1,0:T(8,128)(2,1)S(1)}, u32[]{:S(2)}, u32[]{:S(2)}) collective-permute-start(bf16[320,128]{1,0:T(8,128)(2,1)S(1)} %get-tuple-element.76), channel_id=1, source_target_pairs={{0,3},{1,2},{2,1},{3,0},{4,7},{5,6},{6,5},{7,4},{8,11},{9,10},{10,... | collective-permute-start | bytes 245768 | tf_op jit(solution)/shard_map/ppermute | solution.py:73
  98.3 7.2 %collective-permute-start.26 = (bf16[320,128]{1,0:T(8,128)(2,1)S(1)}, bf16[320,128]{1,0:T(8,128)(2,1)S(1)}, u32[]{:S(2)}, u32[]{:S(2)}) collective-permute-start(bf16[320,128]{1,0:T(8,128)(2,1)S(1)} %get-tuple-element.77), channel_id=1, source_target_pairs={{0,5},{1,4},{2,7},{3,6},{4,1},{5,0},{6,3},{7,2},{8,13},{9,12},{10,... | collective-permute-start | bytes 245768 | tf_op jit(solution)/shard_map/ppermute | solution.py:73
  98.3 7.2 %collective-permute-start.27 = (bf16[320,128]{1,0:T(8,128)(2,1)S(1)}, bf16[320,128]{1,0:T(8,128)(2,1)S(1)}, u32[]{:S(2)}, u32[]{:S(2)}) collective-permute-start(bf16[320,128]{1,0:T(8,128)(2,1)S(1)} %get-tuple-element.78), channel_id=1, source_target_pairs={{0,7},{1,6},{2,5},{3,4},{4,3},{5,2},{6,1},{7,0},{8,15},{9,14},{10,... | collective-permute-start | bytes 245768 | tf_op jit(solution)/shard_map/ppermute | solution.py:73
  109.6 4.7 %collective-permute-start.28 = (bf16[80,512]{1,0:T(8,128)(2,1)}, bf16[80,512]{1,0:T(8,128)(2,1)S(1)}, u32[]{:S(2)}, u32[]{:S(2)}) collective-permute-start(bf16[80,512]{1,0:T(8,128)(2,1)} %get-tuple-element.88), channel_id=1, source_target_pairs={{0,8},{8,0},{16,24},{24,16},{1,9},{9,1},{17,25},{25,17},{2,10},{10... | collective-permute-start | bytes 245768 | tf_op jit(solution)/shard_map/ppermute | solution.py:73
  110.8 9.7 %collective-permute-start.29 = (bf16[80,512]{1,0:T(8,128)(2,1)}, bf16[80,512]{1,0:T(8,128)(2,1)S(1)}, u32[]{:S(2)}, u32[]{:S(2)}) collective-permute-start(bf16[80,512]{1,0:T(8,128)(2,1)} %get-tuple-element.89), channel_id=1, source_target_pairs={{0,16},{8,24},{16,0},{24,8},{1,17},{9,25},{17,1},{25,9},{2,18},{10... | collective-permute-start | bytes 245768 | tf_op jit(solution)/shard_map/ppermute | solution.py:73
  112.4 8.1 %collective-permute-start.30 = (bf16[80,512]{1,0:T(8,128)(2,1)}, bf16[80,512]{1,0:T(8,128)(2,1)S(1)}, u32[]{:S(2)}, u32[]{:S(2)}) collective-permute-start(bf16[80,512]{1,0:T(8,128)(2,1)} %get-tuple-element.90), channel_id=1, source_target_pairs={{0,24},{8,16},{16,8},{24,0},{1,25},{9,17},{17,9},{25,1},{2,26},{10... | collective-permute-start | bytes 245768 | tf_op jit(solution)/shard_map/ppermute | solution.py:73
  121.4 7.2 %collective-permute-start.33 = (bf16[80,512]{1,0:T(8,128)(2,1)S(1)}, bf16[80,512]{1,0:T(8,128)(2,1)S(1)}, u32[]{:S(2)}, u32[]{:S(2)}) collective-permute-start(bf16[80,512]{1,0:T(8,128)(2,1)S(1)} %add_convert_fusion), channel_id=1, source_target_pairs={{0,24},{8,16},{16,8},{24,0},{1,25},{9,17},{17,9},{25,1},{2,26},{10... | collective-permute-start | bytes 245768 | tf_op jit(solution)/shard_map/ppermute | solution.py:73
  123.8 7.5 %collective-permute-start.32 = (bf16[80,512]{1,0:T(8,128)(2,1)S(1)}, bf16[80,512]{1,0:T(8,128)(2,1)S(1)}, u32[]{:S(2)}, u32[]{:S(2)}) collective-permute-start(bf16[80,512]{1,0:T(8,128)(2,1)S(1)} %add_convert_fusion), channel_id=1, source_target_pairs={{0,16},{8,24},{16,0},{24,8},{1,17},{9,25},{17,1},{25,9},{2,18},{10... | collective-permute-start | bytes 245768 | tf_op jit(solution)/shard_map/ppermute | solution.py:73
  124.5 6.9 %collective-permute-start.31 = (bf16[80,512]{1,0:T(8,128)(2,1)S(1)}, bf16[80,512]{1,0:T(8,128)(2,1)S(1)}, u32[]{:S(2)}, u32[]{:S(2)}) collective-permute-start(bf16[80,512]{1,0:T(8,128)(2,1)S(1)} %add_convert_fusion), channel_id=1, source_target_pairs={{0,8},{8,0},{16,24},{24,16},{1,9},{9,1},{17,25},{25,17},{2,10},{10... | collective-permute-start | bytes 245768 | tf_op jit(solution)/shard_map/ppermute | solution.py:73
  131.4 20.8 %copy-start.25 = (s32[2]{0:T(128)S(1)}, s32[2]{0:T(128)}, u32[]{:S(2)}) copy-start(s32[2]{0:T(128)} %copy-done.21) | copy-start | bytes 28
  131.4 11.9 %collective-permute-start.36 = (bf16[320,512]{1,0:T(8,128)(2,1)S(1)}, bf16[320,512]{1,0:T(8,128)(2,1)S(1)}, u32[]{:S(2)}, u32[]{:S(2)}) collective-permute-start(bf16[320,512]{1,0:T(8,128)(2,1)S(1)} %pad_maximum_fusion.refs_1_), channel_id=1, source_target_pairs={{0,6},{1,7},{2,4},{3,5},{4,2},{5,3},{6,0},{7,1},{8,14},{9,15},{10,... | collective-permute-start | bytes 983048 | tf_op jit(solution)/shard_map/ppermute | solution.py:73
  131.5 17.3 %collective-permute-start.35 = (bf16[320,512]{1,0:T(8,128)(2,1)S(1)}, bf16[320,512]{1,0:T(8,128)(2,1)S(1)}, u32[]{:S(2)}, u32[]{:S(2)}) collective-permute-start(bf16[320,512]{1,0:T(8,128)(2,1)S(1)} %pad_maximum_fusion.refs_1_), channel_id=1, source_target_pairs={{0,4},{1,5},{2,6},{3,7},{4,0},{5,1},{6,2},{7,3},{8,12},{9,13},{10,... | collective-permute-start | bytes 983048 | tf_op jit(solution)/shard_map/ppermute | solution.py:73
  133.0 15.8 %collective-permute-start.34 = (bf16[320,512]{1,0:T(8,128)(2,1)S(1)}, bf16[320,512]{1,0:T(8,128)(2,1)S(1)}, u32[]{:S(2)}, u32[]{:S(2)}) collective-permute-start(bf16[320,512]{1,0:T(8,128)(2,1)S(1)} %pad_maximum_fusion.refs_1_), channel_id=1, source_target_pairs={{0,2},{1,3},{2,0},{3,1},{4,6},{5,7},{6,4},{7,5},{8,10},{9,11},{10,... | collective-permute-start | bytes 983048 | tf_op jit(solution)/shard_map/ppermute | solution.py:73
  136.2 15.1 %all-to-all-start.3 = ((bf16[32,4,512]{2,1,0:T(4,128)(2,1)}), bf16[32,4,512]{2,1,0:T(4,128)(2,1)S(1)}, u32[]{:S(2)}, u32[]{:S(2)}) async-start(bf16[32,4,512]{2,1,0:T(4,128)(2,1)} %shard_map.137), calls=%async_computation.3 | async-start | bytes 262144 | tf_op jit(solution)/shard_map/all_to_all | solution.py:657
  139.3 12.9 %collective-permute-start.37 = (bf16[320,512]{1,0:T(8,128)(2,1)S(1)}, bf16[320,512]{1,0:T(8,128)(2,1)S(1)}, u32[]{:S(2)}, u32[]{:S(2)}) collective-permute-start(bf16[320,512]{1,0:T(8,128)(2,1)S(1)} %pad_maximum_fusion.refs_1_), channel_id=1, source_target_pairs={{0,1},{1,0},{2,3},{3,2},{4,5},{5,4},{6,7},{7,6},{8,9},{9,8},{10,11... | collective-permute-start | bytes 983048 | tf_op jit(solution)/shard_map/ppermute | solution.py:73
  148.8 3.4 %collective-permute-start.38 = (bf16[320,512]{1,0:T(8,128)(2,1)S(1)}, bf16[320,512]{1,0:T(8,128)(2,1)S(1)}, u32[]{:S(2)}, u32[]{:S(2)}) collective-permute-start(bf16[320,512]{1,0:T(8,128)(2,1)S(1)} %collective-permute-done.34.refs_2_), channel_id=1, source_target_pairs={{0,1},{1,0},{2,3},{3,2},{4,5},{5,4},{6,7},{7,6},{8,9},{9,8},{10,11... | collective-permute-start | bytes 983048 | tf_op jit(solution)/shard_map/ppermute | solution.py:73
  148.8 3.4 %collective-permute-start.39 = (bf16[320,512]{1,0:T(8,128)(2,1)S(1)}, bf16[320,512]{1,0:T(8,128)(2,1)S(1)}, u32[]{:S(2)}, u32[]{:S(2)}) collective-permute-start(bf16[320,512]{1,0:T(8,128)(2,1)S(1)} %collective-permute-done.35.refs_3_), channel_id=1, source_target_pairs={{0,1},{1,0},{2,3},{3,2},{4,5},{5,4},{6,7},{7,6},{8,9},{9,8},{10,11... | collective-permute-start | bytes 983048 | tf_op jit(solution)/shard_map/ppermute | solution.py:73
  149.3 2.9 %collective-permute-start.40 = (bf16[320,512]{1,0:T(8,128)(2,1)S(1)}, bf16[320,512]{1,0:T(8,128)(2,1)S(1)}, u32[]{:S(2)}, u32[]{:S(2)}) collective-permute-start(bf16[320,512]{1,0:T(8,128)(2,1)S(1)} %collective-permute-done.36.refs_4_), channel_id=1, source_target_pairs={{0,1},{1,0},{2,3},{3,2},{4,5},{5,4},{6,7},{7,6},{8,9},{9,8},{10,11... | collective-permute-start | bytes 983048 | tf_op jit(solution)/shard_map/ppermute | solution.py:73
  (17 other events, 38.2 us)
